TPU v7x, 32 devices: a whole 2x2x4 slice. The times are simulated.
32 devices in a mesh: sea: 8 (over y, x, core), fault: 4 (over z).
Axes of the slice: x: 2, y: 2, z: 4, core: 2. Of those that a mesh axis runs over, the one named last changes fastest.
Arguments:
- slip_rate: bfloat16 [16384, 128], P(('fault', 'sea')), may hold values from -6 to 6
- near_blocks: bfloat16 [8, 4, 8, 256, 256], P('sea', 'fault'), may hold values from -0.375 to 0.375
- near_rows: int32 [8, 4, 8], P('sea', 'fault'), may hold values from 0 to 3
- near_cols: int32 [8, 4, 8], P('sea', 'fault'), may hold values from 0 to 15
- near_scale: float32 [8, 4, 8], P('sea', 'fault'), may hold values from 0.1 to 0.5
- far_left: bfloat16 [8, 4, 24, 48, 256], P('sea', 'fault'), may hold values from -0.875 to 0.875
- far_right: bfloat16 [8, 4, 24, 48, 256], P('sea', 'fault'), may hold values from -0.375 to 0.375
- far_rows: int32 [8, 4, 24], P('sea', 'fault'), may hold values from 0 to 3
- far_cols: int32 [8, 4, 24], P('sea', 'fault'), may hold values from 0 to 15
- far_rank: int32 [8, 4, 24], P('sea', 'fault'), may hold values from 16 to 48, as said below
- far_scale: float32 [8, 4, 24], P('sea', 'fault'), may hold values from 0.1 to 0.5
- sea_depth: float32 [128, 64], P('sea', 'fault'), may hold values from 0.3 to 1
- wet_mask: int32 [128, 64], P('sea', 'fault'), may hold values 0 or 1
Outputs:
- uplift: float32 [128, 64, 128], P('sea', 'fault')
- sea_level: float32 [128, 64, 128], P('sea', 'fault')
Inputs may be any that keep to these rules, and one draw needn't show every extreme that they name: `far_rank`: block 0 of every device has rank 48; every rank is at least 16.
All inputs are finite; a program needn't handle non-finite values. No bound on the sum of `wet_mask` on one device may be relied on, other than what follows from the above.
Results may differ from a plain program's by a relative error of at most 0.0024.
Values may be sent and summed in bfloat16 or wider, within the bound.
No kernel may reach another device: no remote copies, remote signals or barrier semaphores. Data moves between devices by JAX's collectives and lax.ppermute only.
A program may use at most 64 MiB of HBM per device.

v0:
```python
import jax
import jax.numpy as jnp
from jax import lax
from jax.sharding import PartitionSpec as P

STEPS = 6


gravity_step = 0.7
height_step = 0.7


def extended(cells, sides, width):
    for axis, dim in sides:
        count = lax.axis_size(axis)
        ends = count - 1
        head = lax.slice_in_dim(cells, 0, width, axis=dim)
        tail = lax.slice_in_dim(cells, cells.shape[dim] - width, cells.shape[dim], axis=dim)
        cells = jnp.concatenate(
            [
                lax.ppermute(tail, axis, [(i, (i + 1) % count) for i in range(ends)]),
                cells,
                lax.ppermute(head, axis, [((i + 1) % count, i) for i in range(ends)]),
            ],
            axis=dim,
        )
    return cells


def advance(height, east_flow, north_flow, depth_pad):
    new_east = east_flow[1:-1, :-1] - gravity_step * (height[1:-1, 1:] - height[1:-1, :-1])
    east_depth = jnp.minimum(depth_pad[1:-1, :-1], depth_pad[1:-1, 1:])
    flux_east = east_depth[:, :, None] * new_east
    new_north = north_flow[:-1, 1:-1] - gravity_step * (height[1:, 1:-1] - height[:-1, 1:-1])
    north_depth = jnp.minimum(depth_pad[:-1, 1:-1], depth_pad[1:, 1:-1])
    flux_north = north_depth[:, :, None] * new_north
    change = flux_east[:, 1:] - flux_east[:, :-1] + flux_north[1:] - flux_north[:-1]
    new_height = height[1:-1, 1:-1] - height_step * change
    return (new_height, new_east[:, 1:], new_north[1:])


def on_device(
    slip_rate,
    near_blocks,
    near_rows,
    near_cols,
    near_scale,
    far_left,
    far_right,
    far_rows,
    far_cols,
    far_rank,
    far_scale,
    sea_depth,
    wet_mask,
):
    brick_y, brick_x = sea_depth.shape
    fault_count = lax.axis_size("fault")
    leaf_size = near_blocks.shape[-1]
    rank_pad = far_left.shape[-2]
    members = slip_rate.shape[1]
    leaf_count = brick_y * brick_x * fault_count // leaf_size
    targets = jnp.arange(leaf_count)
    gathered = lax.all_gather(slip_rate, "sea", axis=0, tiled=True)
    leaves = gathered.reshape(-1, leaf_size, members)
    near_slip = leaves[near_cols[0, 0]]
    near_term = jnp.einsum(
        "bij,bjs->bis", near_blocks[0, 0], near_slip, preferred_element_type=jnp.float32
    )
    near_weight = (near_rows[0, 0][:, None] == targets).astype(jnp.float32) * near_scale[0, 0][
        :, None
    ]
    total = jnp.einsum("br,bis->ris", near_weight, near_term, precision=lax.Precision.HIGHEST)
    far_slip = leaves[far_cols[0, 0]]
    coeffs = jnp.einsum(
        "bkc,bcs->bks", far_right[0, 0], far_slip, preferred_element_type=jnp.float32
    )
    kept = jnp.arange(rank_pad)[None, :, None] < far_rank[0, 0][:, None, None]
    coeffs = jnp.where(kept, coeffs, jnp.float32(0.0)).astype(jnp.bfloat16)
    far_term = jnp.einsum(
        "bki,bks->bis", far_left[0, 0], coeffs, preferred_element_type=jnp.float32
    )
    far_weight = (far_rows[0, 0][:, None] == targets).astype(jnp.float32) * far_scale[0, 0][:, None]
    total = total + jnp.einsum("br,bis->ris", far_weight, far_term, precision=lax.Precision.HIGHEST)
    partial_value = total.reshape(brick_y, fault_count, brick_x, members)
    ordered = jnp.transpose(partial_value, (1, 0, 2, 3))
    summed = lax.psum_scatter(ordered, "fault", scatter_dimension=0, tiled=True)
    uplift = summed[0]
    wet = wet_mask.astype(jnp.float32)
    depth_cell = sea_depth * wet
    height = uplift * wet[:, :, None]
    east_flow = jnp.zeros_like(height)
    north_flow = jnp.zeros_like(height)
    depth_band = extended(depth_cell, (("sea", 0), ("fault", 1)), 3)
    for round_index in range(STEPS // 3):
        height, east_flow, north_flow = (
            extended(height, (("sea", 0), ("fault", 1)), 3),
            extended(east_flow, (("sea", 0), ("fault", 1)), 3),
            extended(north_flow, (("sea", 0), ("fault", 1)), 3),
        )
        depth_now = depth_band
        for inner_index in range(3):
            height, east_flow, north_flow = advance(height, east_flow, north_flow, depth_now)
            depth_now = depth_now[1:-1, 1:-1]
    return (uplift, height)


def solution(mesh):
    placed = (
        P(("fault", "sea"), None),
        P("sea", "fault", None, None, None),
        P("sea", "fault", None),
        P("sea", "fault", None),
        P("sea", "fault", None),
        P("sea", "fault", None, None, None),
        P("sea", "fault", None, None, None),
        P("sea", "fault", None),
        P("sea", "fault", None),
        P("sea", "fault", None),
        P("sea", "fault", None),
        P("sea", "fault"),
        P("sea", "fault"),
    )
    return jax.shard_map(
        on_device,
        mesh=mesh,
        in_specs=placed,
        out_specs=(P("sea", "fault", None), P("sea", "fault", None)),
        check_vma=False,
    )
```

profile of v0, /device:TPU:20, one launch (start us, length us, event | category | flops | bytes accessed | tf_op | source)
XLA Modules:
  0.0 162.4 jit_solution(1148505944774989426)
XLA Ops:
  7.2 2.9 %collective-permute-start.9 = (f32[3,16,128]{2,1,0:T(8,128)S(1)}, f32[3,16,128]{2,1,0:T(8,128)S(1)}, u32[]{:S(2)}, u32[]{:S(2)}) collective-permute-start(f32[3,16,128]{2,1,0:T(8,128)S(1)} %broadcast.112), channel_id=1, source_target_pairs={{4,0},{8,4},{12,8},{16,12},{20,16},{24,20},{28,24},{5,1},{9,5},{13... | collective-permute-start | bytes 73736 | tf_op jit(solution)/shard_map/ppermute | solution.py:23
  10.2 1.9 %collective-permute-start.8 = (f32[3,16,128]{2,1,0:T(8,128)S(1)}, f32[3,16,128]{2,1,0:T(8,128)S(1)}, u32[]{:S(2)}, u32[]{:S(2)}) collective-permute-start(f32[3,16,128]{2,1,0:T(8,128)S(1)} %broadcast.112), channel_id=1, source_target_pairs={{0,4},{4,8},{8,12},{12,16},{16,20},{20,24},{24,28},{1,5},{5,9},{9,... | collective-permute-start | bytes 73736 | tf_op jit(solution)/shard_map/ppermute | solution.py:21
  12.2 0.7 convert_multiply_fusion
  12.9 4.5 %collective-permute-start.5 = (f32[3,16]{1,0:T(4,128)S(1)}, f32[3,16]{1,0:T(4,128)S(1)}, u32[]{:S(2)}, u32[]{:S(2)}) collective-permute-start(f32[3,16]{1,0:T(4,128)S(1)} %get-tuple-element.45), channel_id=1, source_target_pairs={{4,0},{8,4},{12,8},{16,12},{20,16},{24,20},{28,24},{5,1},{9,5},{13... | collective-permute-start | bytes 584 | tf_op jit(solution)/shard_map/ppermute | solution.py:23
  17.4 1.9 %collective-permute-start.4 = (f32[3,16]{1,0:T(4,128)S(1)}, f32[3,16]{1,0:T(4,128)S(1)}, u32[]{:S(2)}, u32[]{:S(2)}) collective-permute-start(f32[3,16]{1,0:T(4,128)S(1)} %get-tuple-element.44), channel_id=1, source_target_pairs={{0,4},{4,8},{8,12},{12,16},{16,20},{20,24},{24,28},{1,5},{5,9},{9,... | collective-permute-start | bytes 584 | tf_op jit(solution)/shard_map/ppermute | solution.py:21
  19.4 0.7 convert_element_type.10
  20.1 0.7 fusion.58
  20.7 0.7 fusion.59
  21.4 0.7 iota_compare_fusion
  22.1 1.2 dynamic-slice
  23.5 2.3 %collective-permute-start.7 = (f32[22,3]{1,0:T(8,128)S(1)}, f32[22,3]{1,0:T(8,128)S(1)}, u32[]{:S(2)}, u32[]{:S(2)}) collective-permute-start(f32[22,3]{1,0:T(8,128)S(1)} %get-tuple-element.43), channel_id=1, source_target_pairs={{1,0},{2,1},{3,2},{5,4},{6,5},{7,6},{9,8},{10,9},{11,10},{13,12},{... | collective-permute-start | bytes 800 | tf_op jit(solution)/shard_map/ppermute | solution.py:23
  25.8 3.5 %collective-permute-start.6 = (f32[22,3]{1,0:T(8,128)S(1)}, f32[22,3]{1,0:T(8,128)S(1)}, u32[]{:S(2)}, u32[]{:S(2)}) collective-permute-start(f32[22,3]{1,0:T(8,128)S(1)} %get-tuple-element.42), channel_id=1, source_target_pairs={{0,1},{1,2},{2,3},{4,5},{5,6},{6,7},{8,9},{9,10},{10,11},{12,13},{... | collective-permute-start | bytes 800 | tf_op jit(solution)/shard_map/ppermute | solution.py:21
  29.3 2.1 %collective-permute-done.6 = f32[22,3]{1,0:T(8,128)S(1)} collective-permute-done((f32[22,3]{1,0:T(8,128)S(1)}, f32[22,3]{1,0:T(8,128)S(1)}, u32[]{:S(2)}, u32[]{:S(2)}) %collective-permute-start.6) | collective-permute-done | bytes 296 | tf_op jit(solution)/shard_map/ppermute | solution.py:21
  31.6 5.3 %all-gather.2.cloned.1.call-done = bf16[4096,128]{1,0:T(8,128)(2,1)} async-done(((bf16[512,128]{1,0:T(8,128)(2,1)}), bf16[4096,128]{1,0:T(8,128)(2,1)}) %all-gather.2.cloned.1.call-update) | async-done | bytes 1048592 | tf_op jit(solution)/shard_map/all_gather | solution.py:64
  36.9 1.9 %gather_fusion = bf16[8,256,128]{2,1,0:T(8,128)(2,1)S(1)} fusion(bf16[16,256,128]{2,1,0:T(8,128)(2,1)} %bitcast.47, s32[1024]{0:T(1024)S(1)} %pad_clamp_fusion.1), kind=kCustom, calls=%fused_computation | custom fusion | bytes 1048608 | tf_op jit(solution)/shard_map/gather | solution.py:66
  38.8 0.5 convolution_bitcast_fusion.1
  39.3 1.3 copy.20
  40.6 2.1 %gather_fusion.1 = bf16[24,256,128]{2,1,0:T(8,128)(2,1)S(1)} fusion(bf16[16,256,128]{2,1,0:T(8,128)(2,1)} %bitcast.48, s32[1024]{0:T(1024)S(1)} %pad_clamp_fusion), kind=kCustom, calls=%fused_computation.1 | custom fusion | bytes 3145824 | tf_op jit(solution)/shard_map/gather | solution.py:74
  42.8 3.9 %convolution_bitcast_fusion = f32[24,256,128]{1,2,0:T(8,128)} fusion(bf16[24,256,128]{2,1,0:T(8,128)(2,1)S(1)} %gather_fusion.1, bf16[1,1,24,48,256]{4,3,2,1,0:T(8,128)(2,1)S(1)} %copy-done.2, bf16[1,1,24,48,256]{4,3,2,1,0:T(8,128)(2,1)} %param.19, pred[24,48]{1,0:T(8,128)(4,1)S(1)} %iota_compare_fusion), kind=kOutput, calls=%fused_computation.2 | convolution fusion | flops 151289856 | bytes 5899392 | tf_op jit(solution)/shard_map/bki,bks->bis/dot_general | solution.py:80
  46.7 3.6 %copy.21 = f32[24,256,128]{2,0,1:T(8,128)} copy(f32[24,256,128]{1,2,0:T(8,128)} %convolution_bitcast_fusion) | data formatting | bytes 6291456 | tf_op jit(solution)/shard_map/bki,bks->bis/dot_general | solution.py:80
  50.3 1.0 fusion.48
  51.3 3.7 %convolution_add_fusion = f32[4,256,128]{2,0,1:T(4,128)S(1)} fusion(f32[4,256,128]{2,0,1:T(4,128)S(1)} %fusion.48, f32[24,256,128]{2,0,1:T(8,128)} %copy.21, f32[24]{0:T(128)S(1)} %bitcast.52, s32[24]{0:T(128)S(1)} %bitcast.53), kind=kOutput, calls=%fused_computation.5 | convolution fusion | flops 37880000 | bytes 4194496 | tf_op jit(solution)/shard_map/br,bis->ris/dot_general | solution.py:84
  55.0 0.8 copy.22
  56.0 38.2 %all-reduce.3.cloned.1.call-done = f32[4,16,16,128]{3,2,0,1:T(8,128)} async-done(((f32[4,16,16,128]{3,2,0,1:T(8,128)}), f32[4,16,16,128]{3,2,0,1:T(8,128)}) %all-reduce.3.cloned.1.call-update) | async-done | bytes 524304
  94.3 2.2 %broadcast_multiply_fusion.10 = (f32[16,16,128]{2,1,0:T(8,128)S(1)}, f32[16,16,128]{2,1,0:T(8,128)}) fusion(f32[16,16]{1,0:T(8,128)S(1)} %convert_element_type.10, f32[4,16,16,128]{3,2,0,1:T(8,128)} %all-reduce.3.cloned.1.call-done, u32[]{:T(128)} %bitcast.23), kind=kLoop, calls=%fused_computation.102 | loop fusion | flops 32768 | bytes 394244 | tf_op jit(solution)/shard_map/mul | solution.py:91
  96.5 1.9 %collective-permute-start.1 = (f32[3,16,128]{2,1,0:T(8,128)S(1)}, f32[3,16,128]{2,1,0:T(8,128)S(1)}, u32[]{:S(2)}, u32[]{:S(2)}) collective-permute-start(f32[3,16,128]{2,1,0:T(8,128)S(1)} %get-tuple-element.41), channel_id=1, source_target_pairs={{4,0},{8,4},{12,8},{16,12},{20,16},{24,20},{28,24},{5,1},{9,5},{13... | collective-permute-start | bytes 73736 | tf_op jit(solution)/shard_map/ppermute | solution.py:23
  98.4 2.4 %collective-permute-start = (f32[3,16,128]{2,1,0:T(8,128)S(1)}, f32[3,16,128]{2,1,0:T(8,128)S(1)}, u32[]{:S(2)}, u32[]{:S(2)}) collective-permute-start(f32[3,16,128]{2,1,0:T(8,128)S(1)} %get-tuple-element.40), channel_id=1, source_target_pairs={{0,4},{4,8},{8,12},{12,16},{16,20},{20,24},{24,28},{1,5},{5,9},{9,... | collective-permute-start | bytes 73736 | tf_op jit(solution)/shard_map/ppermute | solution.py:21
  100.9 3.0 %collective-permute-start.11 = (f32[22,3,128]{2,1,0:T(4,128)S(1)}, f32[22,3,128]{2,1,0:T(4,128)S(1)}, u32[]{:S(2)}, u32[]{:S(2)}) collective-permute-start(f32[22,3,128]{2,1,0:T(4,128)S(1)} %get-tuple-element.33), channel_id=1, source_target_pairs={{1,0},{2,1},{3,2},{5,4},{6,5},{7,6},{9,8},{10,9},{11,10},{13,12},{... | collective-permute-start | bytes 101384 | tf_op jit(solution)/shard_map/ppermute | solution.py:23
  103.9 2.9 %collective-permute-start.10 = (f32[22,3,128]{2,1,0:T(4,128)S(1)}, f32[22,3,128]{2,1,0:T(4,128)S(1)}, u32[]{:S(2)}, u32[]{:S(2)}) collective-permute-start(f32[22,3,128]{2,1,0:T(4,128)S(1)} %get-tuple-element.32), channel_id=1, source_target_pairs={{0,1},{1,2},{2,3},{4,5},{5,6},{6,7},{8,9},{9,10},{10,11},{12,13},{... | collective-permute-start | bytes 101384 | tf_op jit(solution)/shard_map/ppermute | solution.py:21
  106.8 3.0 %collective-permute-start.3 = (f32[22,3,128]{2,1,0:T(4,128)S(1)}, f32[22,3,128]{2,1,0:T(4,128)S(1)}, u32[]{:S(2)}, u32[]{:S(2)}) collective-permute-start(f32[22,3,128]{2,1,0:T(4,128)S(1)} %get-tuple-element.35), channel_id=1, source_target_pairs={{1,0},{2,1},{3,2},{5,4},{6,5},{7,6},{9,8},{10,9},{11,10},{13,12},{... | collective-permute-start | bytes 101384 | tf_op jit(solution)/shard_map/ppermute | solution.py:23
  109.8 2.9 %collective-permute-start.2 = (f32[22,3,128]{2,1,0:T(4,128)S(1)}, f32[22,3,128]{2,1,0:T(4,128)S(1)}, u32[]{:S(2)}, u32[]{:S(2)}) collective-permute-start(f32[22,3,128]{2,1,0:T(4,128)S(1)} %get-tuple-element.34), channel_id=1, source_target_pairs={{0,1},{1,2},{2,3},{4,5},{5,6},{6,7},{8,9},{9,10},{10,11},{12,13},{... | collective-permute-start | bytes 101384 | tf_op jit(solution)/shard_map/ppermute | solution.py:21
  112.8 2.9 %collective-permute-done.2 = f32[22,3,128]{2,1,0:T(4,128)S(1)} collective-permute-done((f32[22,3,128]{2,1,0:T(4,128)S(1)}, f32[22,3,128]{2,1,0:T(4,128)S(1)}, u32[]{:S(2)}, u32[]{:S(2)}) %collective-permute-start.2) | collective-permute-done | bytes 33824 | tf_op jit(solution)/shard_map/ppermute | solution.py:21
  115.8 0.1 broadcast_multiply_fusion.1
  116.1 0.1 broadcast_multiply_fusion.5
  116.8 2.1 %collective-permute-start.13 = (f32[3,16,128]{2,1,0:T(8,128)S(1)}, f32[3,16,128]{2,1,0:T(8,128)S(1)}, u32[]{:S(2)}, u32[]{:S(2)}) collective-permute-start(f32[3,16,128]{2,1,0:T(8,128)S(1)} %get-tuple-element.39), channel_id=1, source_target_pairs={{4,0},{8,4},{12,8},{16,12},{20,16},{24,20},{28,24},{5,1},{9,5},{13... | collective-permute-start | bytes 73736 | tf_op jit(solution)/shard_map/ppermute | solution.py:23
  118.9 2.3 %collective-permute-start.12 = (f32[3,16,128]{2,1,0:T(8,128)S(1)}, f32[3,16,128]{2,1,0:T(8,128)S(1)}, u32[]{:S(2)}, u32[]{:S(2)}) collective-permute-start(f32[3,16,128]{2,1,0:T(8,128)S(1)} %get-tuple-element.38), channel_id=1, source_target_pairs={{0,4},{4,8},{8,12},{12,16},{16,20},{20,24},{24,28},{1,5},{5,9},{9,... | collective-permute-start | bytes 73736 | tf_op jit(solution)/shard_map/ppermute | solution.py:21
  121.2 4.2 %collective-permute-start.21 = (f32[3,16,128]{2,1,0:T(8,128)S(1)}, f32[3,16,128]{2,1,0:T(8,128)S(1)}, u32[]{:S(2)}, u32[]{:S(2)}) collective-permute-start(f32[3,16,128]{2,1,0:T(8,128)S(1)} %get-tuple-element.37), channel_id=1, source_target_pairs={{4,0},{8,4},{12,8},{16,12},{20,16},{24,20},{28,24},{5,1},{9,5},{13... | collective-permute-start | bytes 73736 | tf_op jit(solution)/shard_map/ppermute | solution.py:23
  125.4 1.9 %collective-permute-start.20 = (f32[3,16,128]{2,1,0:T(8,128)S(1)}, f32[3,16,128]{2,1,0:T(8,128)S(1)}, u32[]{:S(2)}, u32[]{:S(2)}) collective-permute-start(f32[3,16,128]{2,1,0:T(8,128)S(1)} %get-tuple-element.36), channel_id=1, source_target_pairs={{0,4},{4,8},{8,12},{12,16},{16,20},{20,24},{24,28},{1,5},{5,9},{9,... | collective-permute-start | bytes 73736 | tf_op jit(solution)/shard_map/ppermute | solution.py:21
  127.4 4.5 %collective-permute-start.17 = (f32[3,16,128]{2,1,0:T(8,128)S(1)}, f32[3,16,128]{2,1,0:T(8,128)S(1)}, u32[]{:S(2)}, u32[]{:S(2)}) collective-permute-start(f32[3,16,128]{2,1,0:T(8,128)S(1)} %get-tuple-element.25), channel_id=1, source_target_pairs={{4,0},{8,4},{12,8},{16,12},{20,16},{24,20},{28,24},{5,1},{9,5},{13... | collective-permute-start | bytes 73736 | tf_op jit(solution)/shard_map/ppermute | solution.py:23
  131.9 1.9 %collective-permute-start.16 = (f32[3,16,128]{2,1,0:T(8,128)S(1)}, f32[3,16,128]{2,1,0:T(8,128)S(1)}, u32[]{:S(2)}, u32[]{:S(2)}) collective-permute-start(f32[3,16,128]{2,1,0:T(8,128)S(1)} %get-tuple-element.24), channel_id=1, source_target_pairs={{0,4},{4,8},{8,12},{12,16},{16,20},{20,24},{24,28},{1,5},{5,9},{9,... | collective-permute-start | bytes 73736 | tf_op jit(solution)/shard_map/ppermute | solution.py:21
  133.9 2.4 %collective-permute-start.15 = (f32[22,3,128]{2,1,0:T(4,128)S(1)}, f32[22,3,128]{2,1,0:T(4,128)S(1)}, u32[]{:S(2)}, u32[]{:S(2)}) collective-permute-start(f32[22,3,128]{2,1,0:T(4,128)S(1)} %get-tuple-element.31), channel_id=1, source_target_pairs={{1,0},{2,1},{3,2},{5,4},{6,5},{7,6},{9,8},{10,9},{11,10},{13,12},{... | collective-permute-start | bytes 101384 | tf_op jit(solution)/shard_map/ppermute | solution.py:23
  136.3 3.5 %collective-permute-start.14 = (f32[22,3,128]{2,1,0:T(4,128)S(1)}, f32[22,3,128]{2,1,0:T(4,128)S(1)}, u32[]{:S(2)}, u32[]{:S(2)}) collective-permute-start(f32[22,3,128]{2,1,0:T(4,128)S(1)} %get-tuple-element.30), channel_id=1, source_target_pairs={{0,1},{1,2},{2,3},{4,5},{5,6},{6,7},{8,9},{9,10},{10,11},{12,13},{... | collective-permute-start | bytes 101384 | tf_op jit(solution)/shard_map/ppermute | solution.py:21
  139.8 2.4 %collective-permute-start.23 = (f32[22,3,128]{2,1,0:T(4,128)S(1)}, f32[22,3,128]{2,1,0:T(4,128)S(1)}, u32[]{:S(2)}, u32[]{:S(2)}) collective-permute-start(f32[22,3,128]{2,1,0:T(4,128)S(1)} %get-tuple-element.29), channel_id=1, source_target_pairs={{1,0},{2,1},{3,2},{5,4},{6,5},{7,6},{9,8},{10,9},{11,10},{13,12},{... | collective-permute-start | bytes 101384 | tf_op jit(solution)/shard_map/ppermute | solution.py:23
  142.2 3.5 %collective-permute-start.22 = (f32[22,3,128]{2,1,0:T(4,128)S(1)}, f32[22,3,128]{2,1,0:T(4,128)S(1)}, u32[]{:S(2)}, u32[]{:S(2)}) collective-permute-start(f32[22,3,128]{2,1,0:T(4,128)S(1)} %get-tuple-element.28), channel_id=1, source_target_pairs={{0,1},{1,2},{2,3},{4,5},{5,6},{6,7},{8,9},{9,10},{10,11},{12,13},{... | collective-permute-start | bytes 101384 | tf_op jit(solution)/shard_map/ppermute | solution.py:21
  145.7 2.4 %collective-permute-start.19 = (f32[22,3,128]{2,1,0:T(4,128)S(1)}, f32[22,3,128]{2,1,0:T(4,128)S(1)}, u32[]{:S(2)}, u32[]{:S(2)}) collective-permute-start(f32[22,3,128]{2,1,0:T(4,128)S(1)} %get-tuple-element.27), channel_id=1, source_target_pairs={{1,0},{2,1},{3,2},{5,4},{6,5},{7,6},{9,8},{10,9},{11,10},{13,12},{... | collective-permute-start | bytes 101384 | tf_op jit(solution)/shard_map/ppermute | solution.py:23
  148.1 3.5 %collective-permute-start.18 = (f32[22,3,128]{2,1,0:T(4,128)S(1)}, f32[22,3,128]{2,1,0:T(4,128)S(1)}, u32[]{:S(2)}, u32[]{:S(2)}) collective-permute-start(f32[22,3,128]{2,1,0:T(4,128)S(1)} %get-tuple-element.26), channel_id=1, source_target_pairs={{0,1},{1,2},{2,3},{4,5},{5,6},{6,7},{8,9},{9,10},{10,11},{12,13},{... | collective-permute-start | bytes 101384 | tf_op jit(solution)/shard_map/ppermute | solution.py:21
  151.8 2.2 %collective-permute-done.18 = f32[22,3,128]{2,1,0:T(4,128)S(1)} collective-permute-done((f32[22,3,128]{2,1,0:T(4,128)S(1)}, f32[22,3,128]{2,1,0:T(4,128)S(1)}, u32[]{:S(2)}, u32[]{:S(2)}) %collective-permute-start.18) | collective-permute-done | bytes 33824 | tf_op jit(solution)/shard_map/ppermute | solution.py:21
  154.9 0.7 fusion.42
  (82 shorter events, 2.8 us)
Async XLA Ops:
  7.2 31.6 %copy-start = (bf16[1,1,8,256,256]{4,3,2,1,0:T(8,128)(2,1)S(1)}, bf16[1,1,8,256,256]{4,3,2,1,0:T(8,128)(2,1)}, u32[]{:S(2)}) copy-start(bf16[1,1,8,256,256]{4,3,2,1,0:T(8,128)(2,1)} %param.14) | copy-start | bytes 3145732
  7.2 29.7 %all-gather.2.cloned.1.call-start = ((), (), s32[]{:S(2)}) async-start(), calls=%async_computation | async-start | bytes 1179648 | tf_op jit(solution)/shard_map/all_gather | solution.py:64
  7.2 93.6 %collective-permute-start.9 = (f32[3,16,128]{2,1,0:T(8,128)S(1)}, f32[3,16,128]{2,1,0:T(8,128)S(1)}, u32[]{:S(2)}, u32[]{:S(2)}) collective-permute-start(f32[3,16,128]{2,1,0:T(8,128)S(1)} %broadcast.112), channel_id=1, source_target_pairs={{4,0},{8,4},{12,8},{16,12},{20,16},{24,20},{28,24},{5,1},{9,5},{13... | collective-permute-start | bytes 73736 | tf_op jit(solution)/shard_map/ppermute | solution.py:23
  10.2 90.7 %collective-permute-start.8 = (f32[3,16,128]{2,1,0:T(8,128)S(1)}, f32[3,16,128]{2,1,0:T(8,128)S(1)}, u32[]{:S(2)}, u32[]{:S(2)}) collective-permute-start(f32[3,16,128]{2,1,0:T(8,128)S(1)} %broadcast.112), channel_id=1, source_target_pairs={{0,4},{4,8},{8,12},{12,16},{16,20},{20,24},{24,28},{1,5},{5,9},{9,... | collective-permute-start | bytes 73736 | tf_op jit(solution)/shard_map/ppermute | solution.py:21
  12.1 82.2 %all-reduce.3.cloned.1.call-start = ((), (), s32[]{:S(2)}) async-start(), calls=%async_computation.1 | async-start | bytes 1048576
  12.9 10.5 %collective-permute-start.5 = (f32[3,16]{1,0:T(4,128)S(1)}, f32[3,16]{1,0:T(4,128)S(1)}, u32[]{:S(2)}, u32[]{:S(2)}) collective-permute-start(f32[3,16]{1,0:T(4,128)S(1)} %get-tuple-element.45), channel_id=1, source_target_pairs={{4,0},{8,4},{12,8},{16,12},{20,16},{24,20},{28,24},{5,1},{9,5},{13... | collective-permute-start | bytes 584 | tf_op jit(solution)/shard_map/ppermute | solution.py:23
  17.4 5.9 %collective-permute-start.4 = (f32[3,16]{1,0:T(4,128)S(1)}, f32[3,16]{1,0:T(4,128)S(1)}, u32[]{:S(2)}, u32[]{:S(2)}) collective-permute-start(f32[3,16]{1,0:T(4,128)S(1)} %get-tuple-element.44), channel_id=1, source_target_pairs={{0,4},{4,8},{8,12},{12,16},{16,20},{20,24},{24,28},{1,5},{5,9},{9,... | collective-permute-start | bytes 584 | tf_op jit(solution)/shard_map/ppermute | solution.py:21
  23.5 5.9 %collective-permute-start.7 = (f32[22,3]{1,0:T(8,128)S(1)}, f32[22,3]{1,0:T(8,128)S(1)}, u32[]{:S(2)}, u32[]{:S(2)}) collective-permute-start(f32[22,3]{1,0:T(8,128)S(1)} %get-tuple-element.43), channel_id=1, source_target_pairs={{1,0},{2,1},{3,2},{5,4},{6,5},{7,6},{9,8},{10,9},{11,10},{13,12},{... | collective-permute-start | bytes 800 | tf_op jit(solution)/shard_map/ppermute | solution.py:23
  25.8 5.6 %collective-permute-start.6 = (f32[22,3]{1,0:T(8,128)S(1)}, f32[22,3]{1,0:T(8,128)S(1)}, u32[]{:S(2)}, u32[]{:S(2)}) collective-permute-start(f32[22,3]{1,0:T(8,128)S(1)} %get-tuple-element.42), channel_id=1, source_target_pairs={{0,1},{1,2},{2,3},{4,5},{5,6},{6,7},{8,9},{9,10},{10,11},{12,13},{... | collective-permute-start | bytes 800 | tf_op jit(solution)/shard_map/ppermute | solution.py:21
  40.6 2.1 %copy-start.2 = (bf16[1,1,24,48,256]{4,3,2,1,0:T(8,128)(2,1)S(1)}, bf16[1,1,24,48,256]{4,3,2,1,0:T(8,128)(2,1)}, u32[]{:S(2)}) copy-start(bf16[1,1,24,48,256]{4,3,2,1,0:T(8,128)(2,1)} %param.18) | copy-start | bytes 1769476
  46.6 3.6 %copy-start.1 = (f32[8,256,128]{2,0,1:T(8,128)S(1)}, f32[8,256,128]{2,0,1:T(8,128)}, u32[]{:S(2)}) copy-start(f32[8,256,128]{2,0,1:T(8,128)} %copy.20) | copy-start | bytes 3145732
  46.6 3.6 %copy-start.3 = (f32[1,1,8]{2,1,0:T(1,128)S(1)}, f32[1,1,8]{2,1,0:T(1,128)}, u32[]{:S(2)}) copy-start(f32[1,1,8]{2,1,0:T(1,128)} %param.17) | copy-start | bytes 100
  46.6 3.6 %copy-start.4 = (s32[1,1,8]{2,1,0:T(1,128)S(1)}, s32[1,1,8]{2,1,0:T(1,128)}, u32[]{:S(2)}) copy-start(s32[1,1,8]{2,1,0:T(1,128)} %param.15) | copy-start | bytes 100
  50.3 1.0 copy-start.5
  50.3 1.0 copy-start.6
  96.5 10.3 %collective-permute-start.1 = (f32[3,16,128]{2,1,0:T(8,128)S(1)}, f32[3,16,128]{2,1,0:T(8,128)S(1)}, u32[]{:S(2)}, u32[]{:S(2)}) collective-permute-start(f32[3,16,128]{2,1,0:T(8,128)S(1)} %get-tuple-element.41), channel_id=1, source_target_pairs={{4,0},{8,4},{12,8},{16,12},{20,16},{24,20},{28,24},{5,1},{9,5},{13... | collective-permute-start | bytes 73736 | tf_op jit(solution)/shard_map/ppermute | solution.py:23
  98.4 8.3 %collective-permute-start = (f32[3,16,128]{2,1,0:T(8,128)S(1)}, f32[3,16,128]{2,1,0:T(8,128)S(1)}, u32[]{:S(2)}, u32[]{:S(2)}) collective-permute-start(f32[3,16,128]{2,1,0:T(8,128)S(1)} %get-tuple-element.40), channel_id=1, source_target_pairs={{0,4},{4,8},{8,12},{12,16},{16,20},{20,24},{24,28},{1,5},{5,9},{9,... | collective-permute-start | bytes 73736 | tf_op jit(solution)/shard_map/ppermute | solution.py:21
  100.9 11.8 %collective-permute-start.11 = (f32[22,3,128]{2,1,0:T(4,128)S(1)}, f32[22,3,128]{2,1,0:T(4,128)S(1)}, u32[]{:S(2)}, u32[]{:S(2)}) collective-permute-start(f32[22,3,128]{2,1,0:T(4,128)S(1)} %get-tuple-element.33), channel_id=1, source_target_pairs={{1,0},{2,1},{3,2},{5,4},{6,5},{7,6},{9,8},{10,9},{11,10},{13,12},{... | collective-permute-start | bytes 101384 | tf_op jit(solution)/shard_map/ppermute | solution.py:23
  103.9 8.8 %collective-permute-start.10 = (f32[22,3,128]{2,1,0:T(4,128)S(1)}, f32[22,3,128]{2,1,0:T(4,128)S(1)}, u32[]{:S(2)}, u32[]{:S(2)}) collective-permute-start(f32[22,3,128]{2,1,0:T(4,128)S(1)} %get-tuple-element.32), channel_id=1, source_target_pairs={{0,1},{1,2},{2,3},{4,5},{5,6},{6,7},{8,9},{9,10},{10,11},{12,13},{... | collective-permute-start | bytes 101384 | tf_op jit(solution)/shard_map/ppermute | solution.py:21
  106.8 6.0 %collective-permute-start.3 = (f32[22,3,128]{2,1,0:T(4,128)S(1)}, f32[22,3,128]{2,1,0:T(4,128)S(1)}, u32[]{:S(2)}, u32[]{:S(2)}) collective-permute-start(f32[22,3,128]{2,1,0:T(4,128)S(1)} %get-tuple-element.35), channel_id=1, source_target_pairs={{1,0},{2,1},{3,2},{5,4},{6,5},{7,6},{9,8},{10,9},{11,10},{13,12},{... | collective-permute-start | bytes 101384 | tf_op jit(solution)/shard_map/ppermute | solution.py:23
  109.8 5.9 %collective-permute-start.2 = (f32[22,3,128]{2,1,0:T(4,128)S(1)}, f32[22,3,128]{2,1,0:T(4,128)S(1)}, u32[]{:S(2)}, u32[]{:S(2)}) collective-permute-start(f32[22,3,128]{2,1,0:T(4,128)S(1)} %get-tuple-element.34), channel_id=1, source_target_pairs={{0,1},{1,2},{2,3},{4,5},{5,6},{6,7},{8,9},{9,10},{10,11},{12,13},{... | collective-permute-start | bytes 101384 | tf_op jit(solution)/shard_map/ppermute | solution.py:21
  116.8 15.1 %collective-permute-start.13 = (f32[3,16,128]{2,1,0:T(8,128)S(1)}, f32[3,16,128]{2,1,0:T(8,128)S(1)}, u32[]{:S(2)}, u32[]{:S(2)}) collective-permute-start(f32[3,16,128]{2,1,0:T(8,128)S(1)} %get-tuple-element.39), channel_id=1, source_target_pairs={{4,0},{8,4},{12,8},{16,12},{20,16},{24,20},{28,24},{5,1},{9,5},{13... | collective-permute-start | bytes 73736 | tf_op jit(solution)/shard_map/ppermute | solution.py:23
  118.9 15.0 %collective-permute-start.12 = (f32[3,16,128]{2,1,0:T(8,128)S(1)}, f32[3,16,128]{2,1,0:T(8,128)S(1)}, u32[]{:S(2)}, u32[]{:S(2)}) collective-permute-start(f32[3,16,128]{2,1,0:T(8,128)S(1)} %get-tuple-element.38), channel_id=1, source_target_pairs={{0,4},{4,8},{8,12},{12,16},{16,20},{20,24},{24,28},{1,5},{5,9},{9,... | collective-permute-start | bytes 73736 | tf_op jit(solution)/shard_map/ppermute | solution.py:21
  121.2 15.0 %collective-permute-start.21 = (f32[3,16,128]{2,1,0:T(8,128)S(1)}, f32[3,16,128]{2,1,0:T(8,128)S(1)}, u32[]{:S(2)}, u32[]{:S(2)}) collective-permute-start(f32[3,16,128]{2,1,0:T(8,128)S(1)} %get-tuple-element.37), channel_id=1, source_target_pairs={{4,0},{8,4},{12,8},{16,12},{20,16},{24,20},{28,24},{5,1},{9,5},{13... | collective-permute-start | bytes 73736 | tf_op jit(solution)/shard_map/ppermute | solution.py:23
  125.4 14.3 %collective-permute-start.20 = (f32[3,16,128]{2,1,0:T(8,128)S(1)}, f32[3,16,128]{2,1,0:T(8,128)S(1)}, u32[]{:S(2)}, u32[]{:S(2)}) collective-permute-start(f32[3,16,128]{2,1,0:T(8,128)S(1)} %get-tuple-element.36), channel_id=1, source_target_pairs={{0,4},{4,8},{8,12},{12,16},{16,20},{20,24},{24,28},{1,5},{5,9},{9,... | collective-permute-start | bytes 73736 | tf_op jit(solution)/shard_map/ppermute | solution.py:21
  127.4 14.8 %collective-permute-start.17 = (f32[3,16,128]{2,1,0:T(8,128)S(1)}, f32[3,16,128]{2,1,0:T(8,128)S(1)}, u32[]{:S(2)}, u32[]{:S(2)}) collective-permute-start(f32[3,16,128]{2,1,0:T(8,128)S(1)} %get-tuple-element.25), channel_id=1, source_target_pairs={{4,0},{8,4},{12,8},{16,12},{20,16},{24,20},{28,24},{5,1},{9,5},{13... | collective-permute-start | bytes 73736 | tf_op jit(solution)/shard_map/ppermute | solution.py:23
  131.9 13.7 %collective-permute-start.16 = (f32[3,16,128]{2,1,0:T(8,128)S(1)}, f32[3,16,128]{2,1,0:T(8,128)S(1)}, u32[]{:S(2)}, u32[]{:S(2)}) collective-permute-start(f32[3,16,128]{2,1,0:T(8,128)S(1)} %get-tuple-element.24), channel_id=1, source_target_pairs={{0,4},{4,8},{8,12},{12,16},{16,20},{20,24},{24,28},{1,5},{5,9},{9,... | collective-permute-start | bytes 73736 | tf_op jit(solution)/shard_map/ppermute | solution.py:21
  133.9 14.2 %collective-permute-start.15 = (f32[22,3,128]{2,1,0:T(4,128)S(1)}, f32[22,3,128]{2,1,0:T(4,128)S(1)}, u32[]{:S(2)}, u32[]{:S(2)}) collective-permute-start(f32[22,3,128]{2,1,0:T(4,128)S(1)} %get-tuple-element.31), channel_id=1, source_target_pairs={{1,0},{2,1},{3,2},{5,4},{6,5},{7,6},{9,8},{10,9},{11,10},{13,12},{... | collective-permute-start | bytes 101384 | tf_op jit(solution)/shard_map/ppermute | solution.py:23
  136.3 15.3 %collective-permute-start.14 = (f32[22,3,128]{2,1,0:T(4,128)S(1)}, f32[22,3,128]{2,1,0:T(4,128)S(1)}, u32[]{:S(2)}, u32[]{:S(2)}) collective-permute-start(f32[22,3,128]{2,1,0:T(4,128)S(1)} %get-tuple-element.30), channel_id=1, source_target_pairs={{0,1},{1,2},{2,3},{4,5},{5,6},{6,7},{8,9},{9,10},{10,11},{12,13},{... | collective-permute-start | bytes 101384 | tf_op jit(solution)/shard_map/ppermute | solution.py:21
  139.8 11.8 %collective-permute-start.23 = (f32[22,3,128]{2,1,0:T(4,128)S(1)}, f32[22,3,128]{2,1,0:T(4,128)S(1)}, u32[]{:S(2)}, u32[]{:S(2)}) collective-permute-start(f32[22,3,128]{2,1,0:T(4,128)S(1)} %get-tuple-element.29), channel_id=1, source_target_pairs={{1,0},{2,1},{3,2},{5,4},{6,5},{7,6},{9,8},{10,9},{11,10},{13,12},{... | collective-permute-start | bytes 101384 | tf_op jit(solution)/shard_map/ppermute | solution.py:23
  142.2 9.5 %collective-permute-start.22 = (f32[22,3,128]{2,1,0:T(4,128)S(1)}, f32[22,3,128]{2,1,0:T(4,128)S(1)}, u32[]{:S(2)}, u32[]{:S(2)}) collective-permute-start(f32[22,3,128]{2,1,0:T(4,128)S(1)} %get-tuple-element.28), channel_id=1, source_target_pairs={{0,1},{1,2},{2,3},{4,5},{5,6},{6,7},{8,9},{9,10},{10,11},{12,13},{... | collective-permute-start | bytes 101384 | tf_op jit(solution)/shard_map/ppermute | solution.py:21
  145.7 6.1 %collective-permute-start.19 = (f32[22,3,128]{2,1,0:T(4,128)S(1)}, f32[22,3,128]{2,1,0:T(4,128)S(1)}, u32[]{:S(2)}, u32[]{:S(2)}) collective-permute-start(f32[22,3,128]{2,1,0:T(4,128)S(1)} %get-tuple-element.27), channel_id=1, source_target_pairs={{1,0},{2,1},{3,2},{5,4},{6,5},{7,6},{9,8},{10,9},{11,10},{13,12},{... | collective-permute-start | bytes 101384 | tf_op jit(solution)/shard_map/ppermute | solution.py:23
  148.1 5.9 %collective-permute-start.18 = (f32[22,3,128]{2,1,0:T(4,128)S(1)}, f32[22,3,128]{2,1,0:T(4,128)S(1)}, u32[]{:S(2)}, u32[]{:S(2)}) collective-permute-start(f32[22,3,128]{2,1,0:T(4,128)S(1)} %get-tuple-element.26), channel_id=1, source_target_pairs={{0,1},{1,2},{2,3},{4,5},{5,6},{6,7},{8,9},{9,10},{10,11},{12,13},{... | collective-permute-start | bytes 101384 | tf_op jit(solution)/shard_map/ppermute | solution.py:21
Sparse Core Ops, SparseCore 0:
  12.2 24.6 all-gather.1
  55.9 38.2 all-reduce.2
where the time goes:
time: 163 us; the launch traced here: 162 us
  starting transfers between devices  67.6 us (41%)
  waiting for transfers between devices  50.9 us (31%)
  between operations  14.6 us (9%)
  local copies, waits for them, and re-layouts  11.2 us (7%)
  other arithmetic  9.09 us (6%)
  matrix products  9.01 us (6%)
    unnamed x3, waiting for transfers between devices  38.3 us
    ppermute x12, starting transfers between devices, extended(): lax.ppermute(head, axis, [((i + 1) % count, i) for i in range(ends)])  35.5 us
    ppermute x12, starting transfers between devices, extended(): lax.ppermute(tail, axis, [(i, (i + 1) % count) for i in range(ends)])  32 us
    ppermute x12, waiting for transfers between devices, extended(): lax.ppermute(tail, axis, [(i, (i + 1) % count) for i in range(ends)])  7.24 us
    all_gather x1, waiting for transfers between devices, on_device(): gathered = lax.all_gather(slip_rate, 'sea', axis=0, tiled=True)  5.29 us
    dot_general x1, matrix products, on_device(): jnp.einsum('bki,bks->bis', far_left[0, 0], coeffs, preferred_element_type...  3.88 us
    dot_general x1, matrix products, on_device(): jnp.einsum('br,bis->ris', far_weight, far_term, precision=lax.Precision.H...  3.66 us
    dot_general x1, local copies, waits for them, and re-layouts, on_device(): jnp.einsum('bki,bks->bis', far_left[0, 0], coeffs, preferred_element_type...  3.6 us
  transfers between devices with their start and end apart: 26, of which 6 were waited for; matrix products, arithmetic and copies ran while one was open for 16% of the time, Pallas kernels for 0%

commit v1 on v0

v1 whole, which is shorter than its diff:
```python
import functools

import jax
import jax.numpy as jnp
from jax import lax
from jax.experimental import pallas as pl
from jax.experimental.pallas import tpu as pltpu
from jax.sharding import PartitionSpec as P

STEPS = 6
SUB = 8
TILE = 16
LANES = 128

gravity_step = 0.7
height_step = 0.7


def swap(x, axis, k):
    count = lax.axis_size(axis)
    return lax.ppermute(x, axis, [(i, i ^ k) for i in range(count)])


def pieces(d, gap):
    hi = d.astype(jnp.bfloat16).astype(jnp.float32)
    rest = d - hi
    mid = rest.astype(jnp.bfloat16).astype(jnp.float32)
    low = rest - mid
    packed = hi + pltpu.roll(mid, gap, 1) + pltpu.roll(low, 2 * gap, 1)
    return packed.astype(jnp.bfloat16)


def joined(tile, gap):
    t = tile.astype(jnp.float32)
    lanes = t.shape[1]
    d = (t + pltpu.roll(t, lanes - gap, 1)) + pltpu.roll(t, lanes - 2 * gap, 1)
    lane = lax.broadcasted_iota(jnp.int32, t.shape, 1)
    return jnp.where(lane < gap, d, 0.0)


def blocks_kernel(dims, *refs):
    n_sea, n_fault, n_near, n_far, leaf, rank, rows, leaf_count, bx, wx = dims
    ints, scales, tile = refs[:3]
    slots = refs[3 : 3 + n_sea]
    near, left, right = refs[3 + n_sea : 6 + n_sea]
    own = refs[6 + n_sea]
    outs = refs[7 + n_sea : 6 + n_sea + n_fault]
    slip, near_v, left_v, right_v, coeffs, acc, wide, sems = refs[6 + n_sea + n_fault :]
    sea = ints[0]
    fault = ints[1]
    members = slip.shape[1]
    by = tile.shape[0]
    width = leaf_count * leaf // by
    halo = (wx - bx) // 2
    copies = []
    for k in range(n_sea):
        start = pl.multiple_of((sea ^ k) * rows, rows)
        copies.append(pltpu.make_async_copy(slots[k], slip.at[pl.ds(start, rows)], sems.at[k]))
    loads = [
        pltpu.make_async_copy(right, right_v, sems.at[n_sea]),
        pltpu.make_async_copy(near, near_v, sems.at[n_sea + 1]),
        pltpu.make_async_copy(left, left_v, sems.at[n_sea + 2]),
    ]
    for copy in copies + loads:
        copy.start()
    acc[...] = jnp.zeros_like(acc)
    edge = jnp.zeros((halo,) + wide.shape[1:], jnp.float32)
    wide[0:halo] = edge
    wide[halo + width :] = edge
    for copy in copies:
        copy.wait()
    at_near_rows, at_near_cols = 2, 2 + n_near
    at_far_rows = 2 + 2 * n_near
    at_far_cols, at_far_rank = at_far_rows + n_far, at_far_rows + 2 * n_far
    loads[0].wait()
    level = lax.broadcasted_iota(jnp.int32, (rank, members), 0)
    for b in range(n_far):
        start = pl.multiple_of(ints[at_far_cols + b] * leaf, leaf)
        c = jnp.dot(
            right_v[b], slip[pl.ds(start, leaf), :], preferred_element_type=jnp.float32
        )
        coeffs[b] = jnp.where(level < ints[at_far_rank + b], c, 0.0).astype(jnp.bfloat16)
    loads[1].wait()
    for b in range(n_near):
        start = pl.multiple_of(ints[at_near_cols + b] * leaf, leaf)
        target = pl.multiple_of(ints[at_near_rows + b] * leaf, leaf)
        term = jnp.dot(
            near_v[b], slip[pl.ds(start, leaf), :], preferred_element_type=jnp.float32
        )
        acc[pl.ds(target, leaf), :] += scales[b] * term
    loads[2].wait()
    for b in range(n_far):
        target = pl.multiple_of(ints[at_far_rows + b] * leaf, leaf)
        term = lax.dot_general(
            left_v[b], coeffs[b], (((0,), (0,)), ((), ())), preferred_element_type=jnp.float32
        )
        acc[pl.ds(target, leaf), :] += scales[n_near + b] * term
    for x in range(width):
        wide[halo + x] = acc[pl.ds(x, by, stride=width), :]
    own[...] = wide[pl.ds(fault * bx, wx)].reshape(wx * by, members)
    packed = pieces(tile[...], bx)
    for k in range(1, n_fault):
        part = wide[pl.ds((fault ^ k) * bx, wx)].reshape(wx * by, members)
        outs[k - 1][0 : wx * by] = part.astype(jnp.bfloat16)
        outs[k - 1][wx * by :] = packed


def sum_kernel(dims, *refs):
    n_fault, bx, wx, by = dims
    ints, tile, own = refs[:3]
    parts = refs[3 : 2 + n_fault]
    total, depth, uplift, near_edge, far_edge = refs[2 + n_fault :]
    sea = ints[0]
    fault = ints[1]
    halo = (wx - bx) // 2
    cells = wx * by
    s = own[...]
    for part in parts:
        s = s + part[0:cells].astype(jnp.float32)
    total[...] = s
    mid = tile[...]
    before = jnp.zeros_like(mid)
    after = jnp.zeros_like(mid)
    for k in range(1, n_fault):
        other = joined(parts[k - 1][cells:], bx)
        source = fault ^ k
        before = before + jnp.where(source == fault - 1, other, 0.0)
        after = after + jnp.where(source == fault + 1, other, 0.0)
    lanes = mid.shape[1]
    lane = lax.broadcasted_iota(jnp.int32, mid.shape, 1)
    d = jnp.where(lane < halo, pltpu.roll(before, lanes - (bx - halo), 1), 0.0)
    d = d + pltpu.roll(mid, halo, 1)
    d = d + pltpu.roll(jnp.where(lane < halo, after, 0.0), halo + bx, 1)
    depth[...] = d
    packed = pieces(d, lanes // 4)
    odd = sea & 1
    for y in range(by):
        uplift[y] = total[pl.ds(halo * by + y, bx, stride=by), :]
    stack = s.reshape(wx, by, s.shape[1])
    first = stack[:, 0:SUB, :].reshape(wx * SUB, -1).astype(jnp.bfloat16)
    last = stack[:, by - SUB :, :].reshape(wx * SUB, -1).astype(jnp.bfloat16)
    near_edge[0 : wx * SUB] = jnp.where(odd == 1, first, last)
    far_edge[0 : wx * SUB] = jnp.where(odd == 1, last, first)
    near_edge[wx * SUB :] = packed
    far_edge[wx * SUB :] = packed


def steps_kernel(dims, ints, total, depth, near_edge, far_edge, level, h, e, n, de, dn):
    bx, wx, by = dims
    halo = (wx - bx) // 2
    odd = ints[0] & 1
    span = by + 2 * SUB
    edge = wx * SUB
    lanes = depth.shape[1]
    near = near_edge[...].astype(jnp.float32)
    far = far_edge[...].astype(jnp.float32)
    prev = jnp.where(odd == 1, near, far)
    post = jnp.where(odd == 1, far, near)
    prev_d = joined(prev[edge:], lanes // 4)[by - SUB :]
    post_d = joined(post[edge:], lanes // 4)[0:SUB]
    d = jnp.concatenate([prev_d, depth[...], post_d], axis=0)
    east = jnp.minimum(d, pltpu.roll(d, lanes - 1, 1))
    north = jnp.minimum(d, pltpu.roll(d, span - 1, 0))
    wet = jnp.where(d > 0.0, 1.0, 0.0)
    zero = jnp.zeros((span, lanes), jnp.float32)
    for x in range(wx):
        column = jnp.concatenate(
            [prev[x * SUB : (x + 1) * SUB], total[x * by : (x + 1) * by], post[x * SUB : (x + 1) * SUB]],
            axis=0,
        )
        h[x] = column * jnp.broadcast_to(wet[:, x : x + 1], (span, lanes))
        de[x] = jnp.broadcast_to(east[:, x : x + 1], (span, lanes))
        dn[x] = jnp.broadcast_to(north[:, x : x + 1], (span, lanes))
        e[x] = zero
        n[x] = zero
    for step in range(STEPS):
        h_here = h[step]
        flux_before = None
        for x in range(step, wx - 1 - step):
            h_next = h[x + 1]
            new_east = e[x] - gravity_step * (h_next - h_here)
            e[x] = new_east
            flux = de[x] * new_east
            if flux_before is not None:
                new_north = n[x] - gravity_step * (pltpu.roll(h_here, span - 1, 0) - h_here)
                n[x] = new_north
                flux_north = dn[x] * new_north
                change = ((flux - flux_before) + flux_north) - pltpu.roll(flux_north, 1, 0)
                h[x] = h_here - height_step * change
            flux_before = flux
            h_here = h_next
    for y in range(by):
        level[y] = jnp.concatenate(
            [h[halo + x, SUB + y : SUB + y + 1, :] for x in range(bx)], axis=0
        )


def on_device(
    slip_rate,
    near_blocks,
    near_rows,
    near_cols,
    near_scale,
    far_left,
    far_right,
    far_rows,
    far_cols,
    far_rank,
    far_scale,
    sea_depth,
    wet_mask,
):
    by, bx = sea_depth.shape
    n_sea = lax.axis_size("sea")
    n_fault = lax.axis_size("fault")
    n_near = near_blocks.shape[2]
    n_far, rank, leaf = far_left.shape[2:]
    rows, members = slip_rate.shape
    leaf_count = by * bx * n_fault // leaf
    wx = bx + 2 * STEPS
    f32, bf16 = jnp.float32, jnp.bfloat16

    slots = [slip_rate]
    across = [swap(slip_rate, "sea", k) for k in range(2, n_sea, 2)]
    slots.append(swap(slip_rate, "sea", 1))
    for part in across:
        slots += [part, swap(part, "sea", 1)]

    place = jnp.stack([lax.axis_index("sea"), lax.axis_index("fault")]).astype(jnp.int32)
    ints = jnp.concatenate(
        [place]
        + [a.reshape(-1) for a in (near_rows, near_cols, far_rows, far_cols, far_rank)]
    )
    scales = jnp.concatenate([near_scale.reshape(-1), far_scale.reshape(-1)])
    tile = jnp.pad(sea_depth * wet_mask.astype(f32), ((0, 0), (0, LANES - bx)))

    anywhere = pl.BlockSpec(memory_space=pl.ANY)
    vector = pl.BlockSpec(memory_space=pltpu.VMEM)
    scalar = pl.BlockSpec(memory_space=pltpu.SMEM)
    cells = wx * by
    dims = (n_sea, n_fault, n_near, n_far, leaf, rank, rows, leaf_count, bx, wx)
    own, *chunks = pl.pallas_call(
        functools.partial(blocks_kernel, dims),
        out_shape=[jax.ShapeDtypeStruct((cells, members), f32)]
        + [jax.ShapeDtypeStruct((cells + by, members), bf16)] * (n_fault - 1),
        in_specs=[scalar, scalar, vector] + [anywhere] * (n_sea + 3),
        out_specs=[vector] * n_fault,
        scratch_shapes=[
            pltpu.VMEM((n_sea * rows, members), bf16),
            pltpu.VMEM(near_blocks.shape[2:], bf16),
            pltpu.VMEM(far_left.shape[2:], bf16),
            pltpu.VMEM(far_right.shape[2:], bf16),
            pltpu.VMEM((n_far, rank, members), bf16),
            pltpu.VMEM((leaf_count * leaf, members), f32),
            pltpu.VMEM((n_fault * bx + 2 * STEPS, by, members), f32),
            pltpu.SemaphoreType.DMA((n_sea + 3,)),
        ],
        name="blocks",
    )(ints, scales, tile, *slots, near_blocks[0, 0], far_left[0, 0], far_right[0, 0])

    got = [swap(chunks[k - 1], "fault", k) for k in range(1, n_fault)]

    edge = jax.ShapeDtypeStruct((wx * SUB + by, members), bf16)
    total, depth, uplift, near_edge, far_edge = pl.pallas_call(
        functools.partial(sum_kernel, (n_fault, bx, wx, by)),
        out_shape=[
            jax.ShapeDtypeStruct((cells, members), f32),
            jax.ShapeDtypeStruct((by, LANES), f32),
            jax.ShapeDtypeStruct((by, bx, members), f32),
            edge,
            edge,
        ],
        in_specs=[scalar] + [vector] * (1 + n_fault),
        out_specs=[vector] * 5,
        name="sums",
    )(ints, tile, own, *got)

    near_edge = swap(near_edge, "sea", 1)
    pairs = [(i, i + 1) for i in range(1, n_sea - 1, 2)]
    far_edge = lax.ppermute(far_edge, "sea", pairs + [(b, a) for a, b in pairs])

    span = by + 2 * SUB
    field = pltpu.VMEM((wx, span, members), f32)
    level = pl.pallas_call(
        functools.partial(steps_kernel, (bx, wx, by)),
        out_shape=jax.ShapeDtypeStruct((by, bx, members), f32),
        in_specs=[scalar] + [vector] * 4,
        out_specs=vector,
        scratch_shapes=[field] * 5,
        name="steps",
    )(ints, total, depth, near_edge, far_edge)
    return uplift, level


def solution(mesh):
    placed = (
        P(("fault", "sea"), None),
        P("sea", "fault", None, None, None),
        P("sea", "fault", None),
        P("sea", "fault", None),
        P("sea", "fault", None),
        P("sea", "fault", None, None, None),
        P("sea", "fault", None, None, None),
        P("sea", "fault", None),
        P("sea", "fault", None),
        P("sea", "fault", None),
        P("sea", "fault", None),
        P("sea", "fault"),
        P("sea", "fault"),
    )
    return jax.shard_map(
        on_device,
        mesh=mesh,
        in_specs=placed,
        out_specs=(P("sea", "fault", None), P("sea", "fault", None)),
        check_vma=False,
    )
```

time: 163 us -> 48.9 us (0.30)
  starting transfers between devices: 67.6 us -> 10.6 us
  waiting for transfers between devices: 50.9 us -> 20.7 us
  between operations: 14.6 us -> 0.77 us
  Pallas kernels: 0 us -> 10.3 us
  matrix products: 9.01 us -> 0 us
  other arithmetic: 9.09 us -> 1.42 us
  local copies, waits for them, and re-layouts: 11.2 us -> 4.55 us
    ppermute x24 -> x12, starting transfers between devices: 67.5 us -> 10.6 us  [the longest x11 7.12 us: swap(): return lax.ppermute(x, axis, [(i, i ^ k) for i in range(count)])]
    unnamed x3 -> x0, waiting for transfers between devices: 38.3 us -> none
    ppermute x24 -> x12, waiting for transfers between devices: 7.32 us -> 20.7 us  [the longest x11 17.1 us: swap(): return lax.ppermute(x, axis, [(i, i ^ k) for i in range(count)])]
    pallas_call x0 -> x3, Pallas kernels: none -> 10.3 us  [the longest x1 5 us: on_device(): pl.pallas_call(functools.partial(blocks_kernel, dims), out_shape=[jax.Sha...]
    dot_general x4 -> x0, matrix products: 9.01 us -> none  [the longest x1 3.88 us: on_device(): jnp.einsum('bki,bks->bis', far_left[0, 0], coeffs, preferred_element_type...]
    all_gather x1 -> x0, waiting for transfers between devices: 5.29 us -> none  [on_device(): gathered = lax.all_gather(slip_rate, 'sea', axis=0, tiled=True)]
    dot_general x2 -> x0, local copies, waits for them, and re-layouts: 4.92 us -> none  [the longest x1 3.6 us: on_device(): jnp.einsum('bki,bks->bis', far_left[0, 0], coeffs, preferred_element_type...]
    gather x2 -> x0, local copies, waits for them, and re-layouts: 4 us -> none  [the longest x1 2.13 us: on_device(): far_slip = leaves[far_cols[0, 0]]]
  transfers between devices with their start and end apart: 26 -> 12, of which waited for: 6 -> 7; matrix products, arithmetic and copies ran while one was open for 16% -> 5% of each run, Pallas kernels for 0% -> 0%
where the time goes in v1:
time: 48.9 us; the launch traced here: 48.2 us
  waiting for transfers between devices  20.7 us (42%)
  starting transfers between devices  10.6 us (22%)
  Pallas kernels  10.3 us (21%)
  local copies, waits for them, and re-layouts  4.55 us (9%)
  other arithmetic  1.42 us (3%)
  between operations  0.77 us (2%)
    ppermute x11, waiting for transfers between devices, swap(): return lax.ppermute(x, axis, [(i, i ^ k) for i in range(count)])  17.1 us
    ppermute x11, starting transfers between devices, swap(): return lax.ppermute(x, axis, [(i, i ^ k) for i in range(count)])  7.12 us
    pallas_call x1, Pallas kernels, on_device(): pl.pallas_call(functools.partial(blocks_kernel, dims), out_shape=[jax.Sha...  5 us
    ppermute x1, waiting for transfers between devices, on_device(): far_edge = lax.ppermute(far_edge, 'sea', pairs + [(b, a) for a, b in pairs])  3.57 us
    ppermute x1, starting transfers between devices, on_device(): far_edge = lax.ppermute(far_edge, 'sea', pairs + [(b, a) for a, b in pairs])  3.44 us
    unnamed x38, local copies, waits for them, and re-layouts  3.35 us
    pallas_call x1, Pallas kernels, on_device(): pl.pallas_call(functools.partial(steps_kernel, (bx, wx, by)), out_shape=j...  3.13 us
    pallas_call x1, Pallas kernels, on_device(): pl.pallas_call(functools.partial(sum_kernel, (n_fault, bx, wx, by)), out_...  2.13 us
  transfers between devices with their start and end apart: 12, of which 7 were waited for; matrix products, arithmetic and copies ran while one was open for 5% of the time, Pallas kernels for 0%

profile of v1, /device:TPU:20, one launch (start us, length us, event | category | flops | bytes accessed | tf_op | source)
XLA Modules:
  0.0 48.2 jit_solution(6356767448656109279)
XLA Ops:
  0.6 0.6 %collective-permute-start.3 = (bf16[512,128]{1,0:T(8,128)(2,1)}, bf16[512,128]{1,0:T(8,128)(2,1)S(1)}, u32[]{:S(2)}, u32[]{:S(2)}) collective-permute-start(bf16[512,128]{1,0:T(8,128)(2,1)} %refs_3_.1), channel_id=1, source_target_pairs={{0,16},{4,20},{8,24},{12,28},{16,0},{20,4},{24,8},{28,12},{1,17},{... | collective-permute-start | bytes 393224 | tf_op jit(solution)/shard_map/ppermute | solution.py:21
  1.2 1.5 %collective-permute-start.1 = (bf16[512,128]{1,0:T(8,128)(2,1)}, bf16[512,128]{1,0:T(8,128)(2,1)S(1)}, u32[]{:S(2)}, u32[]{:S(2)}) collective-permute-start(bf16[512,128]{1,0:T(8,128)(2,1)} %refs_3_.1), channel_id=1, source_target_pairs={{0,8},{4,12},{8,0},{12,4},{16,24},{20,28},{24,16},{28,20},{1,9},{5... | collective-permute-start | bytes 393224 | tf_op jit(solution)/shard_map/ppermute | solution.py:21
  2.7 1.5 %collective-permute-start.5 = (bf16[512,128]{1,0:T(8,128)(2,1)}, bf16[512,128]{1,0:T(8,128)(2,1)S(1)}, u32[]{:S(2)}, u32[]{:S(2)}) collective-permute-start(bf16[512,128]{1,0:T(8,128)(2,1)} %refs_3_.1), channel_id=1, source_target_pairs={{0,24},{4,28},{8,16},{12,20},{16,8},{20,12},{24,0},{28,4},{1,25},{... | collective-permute-start | bytes 393224 | tf_op jit(solution)/shard_map/ppermute | solution.py:21
  4.2 0.0 collective-permute-start
  4.2 2.2 %collective-permute-done.3.refs_7_ = bf16[512,128]{1,0:T(8,128)(2,1)S(1)} collective-permute-done((bf16[512,128]{1,0:T(8,128)(2,1)}, bf16[512,128]{1,0:T(8,128)(2,1)S(1)}, u32[]{:S(2)}, u32[]{:S(2)}) %collective-permute-start.3) | collective-permute-done | bytes 131104 | tf_op jit(solution)/shard_map/ppermute | solution.py:21
  6.4 0.0 collective-permute-start.4
  6.4 0.7 %collective-permute-done.1.refs_5_ = bf16[512,128]{1,0:T(8,128)(2,1)S(1)} collective-permute-done((bf16[512,128]{1,0:T(8,128)(2,1)}, bf16[512,128]{1,0:T(8,128)(2,1)S(1)}, u32[]{:S(2)}, u32[]{:S(2)}) %collective-permute-start.1) | collective-permute-done | bytes 131104 | tf_op jit(solution)/shard_map/ppermute | solution.py:21
  7.0 0.0 collective-permute-start.2
  7.0 3.1 %collective-permute-done.5.refs_9_ = bf16[512,128]{1,0:T(8,128)(2,1)S(1)} collective-permute-done((bf16[512,128]{1,0:T(8,128)(2,1)}, bf16[512,128]{1,0:T(8,128)(2,1)S(1)}, u32[]{:S(2)}, u32[]{:S(2)}) %collective-permute-start.5) | collective-permute-done | bytes 131104 | tf_op jit(solution)/shard_map/ppermute | solution.py:21
  10.1 0.0 collective-permute-start.6
  10.1 0.8 %convert_multiply_fusion = f32[16,16]{1,0:T(8,128)S(1)} fusion(f32[16,16]{1,0:T(8,128)} %param.24, s32[16,16]{1,0:T(8,128)} %param.25), kind=kLoop, calls=%fused_computation | loop fusion | flops 512 | bytes 3072 | tf_op jit(solution)/shard_map/mul | solution.py:235
  10.9 0.6 %pad.4.refs_2_.refs_1_ = f32[16,128]{1,0:T(8,128)} pad(f32[16,16]{1,0:T(8,128)S(1)} %convert_multiply_fusion, f32[]{:T(128)} %constant.11.clone.1), padding=0_0x0_112 | pad | bytes 9220 | tf_op jit(solution)/shard_map/jit(_pad)/pad | solution.py:235
  11.5 0.0 copy-start.14
  11.5 0.6 %copy-done.15 = s32[1,1,24]{2,1,0:T(1,128)S(1)} copy-done((s32[1,1,24]{2,1,0:T(1,128)S(1)}, s32[1,1,24]{2,1,0:T(1,128)}, u32[]{:S(2)}) %copy-start.15) | copy-done | bytes 120
  12.2 0.0 copy-done.16
  12.2 0.0 copy-done.12
  12.2 0.0 copy-done.13
  12.2 0.0 copy-done.14
  12.2 0.6 %concatenate.6.refs_0_.ints = s32[90]{0:T(128)} concatenate(s32[1]{0:T(128)} %bitcast, s32[1]{0:T(128)} %bitcast.1, s32[8]{0:T(128)S(1)} %bitcast.15, s32[8]{0:T(128)S(1)} %bitcast.16, s32[24]{0:T(128)S(1)} %bitcast.17, s32[24]{0:T(128)S(1)} %bitcast.18, s32[24]{0:T(128)S(1)} %bitcast.19), dimensions={0} | concatenate | bytes 720 | tf_op jit(solution)/shard_map/concatenate | solution.py:230
  12.8 0.7 %copy-done.17 = f32[1,1,24]{2,1,0:T(1,128)S(1)} copy-done((f32[1,1,24]{2,1,0:T(1,128)S(1)}, f32[1,1,24]{2,1,0:T(1,128)}, u32[]{:S(2)}) %copy-start.17) | copy-done | bytes 120
  13.5 0.0 copy-done.18
  13.5 0.7 %pad_maximum_fusion.refs_1_ = f32[32]{0:T(128)} fusion(f32[24]{0:T(128)S(1)} %bitcast.20, f32[8]{0:T(128)S(1)} %bitcast.21), kind=kLoop, calls=%fused_computation.1 | loop fusion | flops 32 | bytes 256 | tf_op jit(solution)/shard_map/concatenate | solution.py:234
  14.2 0.0 collective-permute-done.refs_4_
  14.2 0.0 collective-permute-done.4.refs_8_
  14.2 0.0 collective-permute-done.2.refs_6_
  14.2 0.0 collective-permute-done.6.refs_10_
  14.2 0.0 copy-start.6
  14.2 0.0 copy-done
  14.2 0.0 copy-done.1
  14.3 0.6 %copy-done.3 = bf16[512,128]{1,0:T(8,128)(2,1)} copy-done((bf16[512,128]{1,0:T(8,128)(2,1)}, bf16[512,128]{1,0:T(8,128)(2,1)S(1)}, u32[]{:S(2)}) %copy-start.3) | copy-done | bytes 131096
  14.8 0.0 copy-done.4
  14.9 0.0 copy-done.5
  14.9 0.0 copy-done.6
  14.9 5.0 %blocks.1 = (f32[448,128]{1,0:T(8,128)}, bf16[464,128]{1,0:T(8,128)(2,1)}, bf16[464,128]{1,0:T(8,128)(2,1)}, bf16[464,128]{1,0:T(8,128)(2,1)}) custom-call(s32[90]{0:T(128)} %concatenate.6.refs_0_.ints, f32[32]{0:T(128)} %pad_maximum_fusion.refs_1_, f32[16,128]{1,0:T(8,128)} %pad.4.refs_2_.refs_1_, bf16[512,128]{1,0:T(8,128)(2,1)} %refs_3_.1, ...), custom_call_target="tpu_custom_call" | custom-call | tf_op jit(solution)/shard_map/blocks/pallas_call | solution.py:242
  20.0 1.6 %collective-permute-start.7 = (bf16[464,128]{1,0:T(8,128)(2,1)}, bf16[464,128]{1,0:T(8,128)(2,1)S(1)}, u32[]{:S(2)}, u32[]{:S(2)}) collective-permute-start(bf16[464,128]{1,0:T(8,128)(2,1)} %get-tuple-element.12), channel_id=1, source_target_pairs={{0,1},{1,0},{2,3},{3,2},{4,5},{5,4},{6,7},{7,6},{8,9},{9,8},{10,11... | collective-permute-start | bytes 356360 | tf_op jit(solution)/shard_map/ppermute | solution.py:21
  21.6 0.3 collective-permute-start.8
  21.9 1.6 %collective-permute-start.9 = (bf16[464,128]{1,0:T(8,128)(2,1)}, bf16[464,128]{1,0:T(8,128)(2,1)S(1)}, u32[]{:S(2)}, u32[]{:S(2)}) collective-permute-start(bf16[464,128]{1,0:T(8,128)(2,1)} %get-tuple-element.14), channel_id=1, source_target_pairs={{0,3},{1,2},{2,1},{3,0},{4,7},{5,6},{6,5},{7,4},{8,11},{9,10},{10,... | collective-permute-start | bytes 356360 | tf_op jit(solution)/shard_map/ppermute | solution.py:21
  23.5 2.8 %collective-permute-done.7.refs_3_ = bf16[464,128]{1,0:T(8,128)(2,1)S(1)} collective-permute-done((bf16[464,128]{1,0:T(8,128)(2,1)}, bf16[464,128]{1,0:T(8,128)(2,1)S(1)}, u32[]{:S(2)}, u32[]{:S(2)}) %collective-permute-start.7) | collective-permute-done | bytes 118816 | tf_op jit(solution)/shard_map/ppermute | solution.py:21
  26.3 4.7 %collective-permute-done.8.refs_4_ = bf16[464,128]{1,0:T(8,128)(2,1)S(1)} collective-permute-done((bf16[464,128]{1,0:T(8,128)(2,1)}, bf16[464,128]{1,0:T(8,128)(2,1)S(1)}, u32[]{:S(2)}, u32[]{:S(2)}) %collective-permute-start.8) | collective-permute-done | bytes 118816 | tf_op jit(solution)/shard_map/ppermute | solution.py:21
  31.0 3.7 %collective-permute-done.9.refs_5_ = bf16[464,128]{1,0:T(8,128)(2,1)S(1)} collective-permute-done((bf16[464,128]{1,0:T(8,128)(2,1)}, bf16[464,128]{1,0:T(8,128)(2,1)S(1)}, u32[]{:S(2)}, u32[]{:S(2)}) %collective-permute-start.9) | collective-permute-done | bytes 118816 | tf_op jit(solution)/shard_map/ppermute | solution.py:21
  34.7 0.6 %copy-done.9 = bf16[464,128]{1,0:T(8,128)(2,1)} copy-done((bf16[464,128]{1,0:T(8,128)(2,1)}, bf16[464,128]{1,0:T(8,128)(2,1)S(1)}, u32[]{:S(2)}) %copy-start.9) | copy-done | bytes 118808
  35.3 2.1 %sums.1 = (f32[448,128]{1,0:T(8,128)}, f32[16,128]{1,0:T(8,128)}, f32[16,16,128]{2,1,0:T(8,128)}, bf16[240,128]{1,0:T(8,128)(2,1)}, bf16[240,128]{1,0:T(8,128)(2,1)}) custom-call(s32[90]{0:T(128)} %concatenate.6.refs_0_.ints, f32[16,128]{1,0:T(8,128)} %pad.4.refs_2_.refs_1_, f32[448,128]{1,0:T(8,128)} %get-tuple-element.11.refs_2_, ...), custom_call_target="tpu_custom_call" | custom-call | tf_op jit(solution)/shard_map/sums/pallas_call | solution.py:264
  37.5 0.0 collective-permute-start.10
  37.5 3.4 %collective-permute-start.11 = (bf16[240,128]{1,0:T(8,128)(2,1)}, bf16[240,128]{1,0:T(8,128)(2,1)S(1)}, u32[]{:S(2)}, u32[]{:S(2)}) collective-permute-start(bf16[240,128]{1,0:T(8,128)(2,1)} %get-tuple-element.19), channel_id=1, source_target_pairs={{4,8},{12,16},{20,24},{8,4},{16,12},{24,20},{5,9},{13,17},{21,25},... | collective-permute-start | bytes 184328 | tf_op jit(solution)/shard_map/ppermute | solution.py:280
  40.9 0.0 collective-permute-done.10.near_edge
  40.9 3.6 %collective-permute-done.11.far_edge = bf16[240,128]{1,0:T(8,128)(2,1)S(1)} collective-permute-done((bf16[240,128]{1,0:T(8,128)(2,1)}, bf16[240,128]{1,0:T(8,128)(2,1)S(1)}, u32[]{:S(2)}, u32[]{:S(2)}) %collective-permute-start.11) | collective-permute-done | bytes 61472 | tf_op jit(solution)/shard_map/ppermute | solution.py:280
  44.5 0.6 %copy-done.11 = bf16[240,128]{1,0:T(8,128)(2,1)} copy-done((bf16[240,128]{1,0:T(8,128)(2,1)}, bf16[240,128]{1,0:T(8,128)(2,1)S(1)}, u32[]{:S(2)}) %copy-start.11) | copy-done | bytes 61464
  45.1 3.1 %steps.1 = f32[16,16,128]{2,1,0:T(8,128)} custom-call(s32[90]{0:T(128)} %concatenate.6.refs_0_.ints, f32[448,128]{1,0:T(8,128)} %get-tuple-element.16.total, f32[16,128]{1,0:T(8,128)} %get-tuple-element.17.depth, bf16[240,128]{1,0:T(8,128)(2,1)} %copy-done.10, bf16[240,128]{1,0:T(8,128)(2,1)} %copy-done.11), custom_call_target="tpu_custom_call" | custom-call | tf_op jit(solution)/shard_map/steps/pallas_call | solution.py:284
  (21 shorter events, 0.0 us)
Async XLA Ops:
  0.6 5.7 %collective-permute-start.3 = (bf16[512,128]{1,0:T(8,128)(2,1)}, bf16[512,128]{1,0:T(8,128)(2,1)S(1)}, u32[]{:S(2)}, u32[]{:S(2)}) collective-permute-start(bf16[512,128]{1,0:T(8,128)(2,1)} %refs_3_.1), channel_id=1, source_target_pairs={{0,16},{4,20},{8,24},{12,28},{16,0},{20,4},{24,8},{28,12},{1,17},{... | collective-permute-start | bytes 393224 | tf_op jit(solution)/shard_map/ppermute | solution.py:21
  1.2 5.8 %collective-permute-start.1 = (bf16[512,128]{1,0:T(8,128)(2,1)}, bf16[512,128]{1,0:T(8,128)(2,1)S(1)}, u32[]{:S(2)}, u32[]{:S(2)}) collective-permute-start(bf16[512,128]{1,0:T(8,128)(2,1)} %refs_3_.1), channel_id=1, source_target_pairs={{0,8},{4,12},{8,0},{12,4},{16,24},{20,28},{24,16},{28,20},{1,9},{5... | collective-permute-start | bytes 393224 | tf_op jit(solution)/shard_map/ppermute | solution.py:21
  2.7 7.4 %collective-permute-start.5 = (bf16[512,128]{1,0:T(8,128)(2,1)}, bf16[512,128]{1,0:T(8,128)(2,1)S(1)}, u32[]{:S(2)}, u32[]{:S(2)}) collective-permute-start(bf16[512,128]{1,0:T(8,128)(2,1)} %refs_3_.1), channel_id=1, source_target_pairs={{0,24},{4,28},{8,16},{12,20},{16,8},{20,12},{24,0},{28,4},{1,25},{... | collective-permute-start | bytes 393224 | tf_op jit(solution)/shard_map/ppermute | solution.py:21
  4.2 10.0 %collective-permute-start = (bf16[512,128]{1,0:T(8,128)(2,1)}, bf16[512,128]{1,0:T(8,128)(2,1)S(1)}, u32[]{:S(2)}, u32[]{:S(2)}) collective-permute-start(bf16[512,128]{1,0:T(8,128)(2,1)} %refs_3_.1), channel_id=1, source_target_pairs={{0,4},{4,0},{8,12},{12,8},{16,20},{20,16},{24,28},{28,24},{1,5},{5... | collective-permute-start | bytes 393224 | tf_op jit(solution)/shard_map/ppermute | solution.py:21
  6.4 7.9 %copy-start = (bf16[512,128]{1,0:T(8,128)(2,1)}, bf16[512,128]{1,0:T(8,128)(2,1)S(1)}, u32[]{:S(2)}) copy-start(bf16[512,128]{1,0:T(8,128)(2,1)S(1)} %collective-permute-done.3.refs_7_) | copy-start | bytes 393220
  6.4 7.8 %collective-permute-start.4 = (bf16[512,128]{1,0:T(8,128)(2,1)S(1)}, bf16[512,128]{1,0:T(8,128)(2,1)S(1)}, u32[]{:S(2)}, u32[]{:S(2)}) collective-permute-start(bf16[512,128]{1,0:T(8,128)(2,1)S(1)} %collective-permute-done.3.refs_7_), channel_id=1, source_target_pairs={{0,4},{4,0},{8,12},{12,8},{16,20},{20,16},{24,28},{28,24},{1,5},{5... | collective-permute-start | bytes 393224 | tf_op jit(solution)/shard_map/ppermute | solution.py:21
  7.0 7.2 %copy-start.1 = (bf16[512,128]{1,0:T(8,128)(2,1)}, bf16[512,128]{1,0:T(8,128)(2,1)S(1)}, u32[]{:S(2)}) copy-start(bf16[512,128]{1,0:T(8,128)(2,1)S(1)} %collective-permute-done.1.refs_5_) | copy-start | bytes 393220
  7.0 7.2 %collective-permute-start.2 = (bf16[512,128]{1,0:T(8,128)(2,1)S(1)}, bf16[512,128]{1,0:T(8,128)(2,1)S(1)}, u32[]{:S(2)}, u32[]{:S(2)}) collective-permute-start(bf16[512,128]{1,0:T(8,128)(2,1)S(1)} %collective-permute-done.1.refs_5_), channel_id=1, source_target_pairs={{0,4},{4,0},{8,12},{12,8},{16,20},{20,16},{24,28},{28,24},{1,5},{5... | collective-permute-start | bytes 393224 | tf_op jit(solution)/shard_map/ppermute | solution.py:21
  10.1 4.1 %copy-start.2 = (bf16[512,128]{1,0:T(8,128)(2,1)}, bf16[512,128]{1,0:T(8,128)(2,1)S(1)}, u32[]{:S(2)}) copy-start(bf16[512,128]{1,0:T(8,128)(2,1)S(1)} %collective-permute-done.5.refs_9_) | copy-start | bytes 393220
  10.1 4.1 %collective-permute-start.6 = (bf16[512,128]{1,0:T(8,128)(2,1)S(1)}, bf16[512,128]{1,0:T(8,128)(2,1)S(1)}, u32[]{:S(2)}, u32[]{:S(2)}) collective-permute-start(bf16[512,128]{1,0:T(8,128)(2,1)S(1)} %collective-permute-done.5.refs_9_), channel_id=1, source_target_pairs={{0,4},{4,0},{8,12},{12,8},{16,20},{20,16},{24,28},{28,24},{1,5},{5... | collective-permute-start | bytes 393224 | tf_op jit(solution)/shard_map/ppermute | solution.py:21
  11.5 0.7 %copy-start.15 = (s32[1,1,24]{2,1,0:T(1,128)S(1)}, s32[1,1,24]{2,1,0:T(1,128)}, u32[]{:S(2)}) copy-start(s32[1,1,24]{2,1,0:T(1,128)} %param.21) | copy-start | bytes 292
  11.5 0.7 %copy-start.16 = (s32[1,1,24]{2,1,0:T(1,128)S(1)}, s32[1,1,24]{2,1,0:T(1,128)}, u32[]{:S(2)}) copy-start(s32[1,1,24]{2,1,0:T(1,128)} %param.22) | copy-start | bytes 292
  11.5 0.7 %copy-start.12 = (s32[1,1,8]{2,1,0:T(1,128)S(1)}, s32[1,1,8]{2,1,0:T(1,128)}, u32[]{:S(2)}) copy-start(s32[1,1,8]{2,1,0:T(1,128)} %param.15) | copy-start | bytes 100
  11.5 0.7 %copy-start.13 = (s32[1,1,8]{2,1,0:T(1,128)S(1)}, s32[1,1,8]{2,1,0:T(1,128)}, u32[]{:S(2)}) copy-start(s32[1,1,8]{2,1,0:T(1,128)} %param.16) | copy-start | bytes 100
  11.5 0.7 %copy-start.14 = (s32[1,1,24]{2,1,0:T(1,128)S(1)}, s32[1,1,24]{2,1,0:T(1,128)}, u32[]{:S(2)}) copy-start(s32[1,1,24]{2,1,0:T(1,128)} %param.20) | copy-start | bytes 292
  12.8 0.7 %copy-start.17 = (f32[1,1,24]{2,1,0:T(1,128)S(1)}, f32[1,1,24]{2,1,0:T(1,128)}, u32[]{:S(2)}) copy-start(f32[1,1,24]{2,1,0:T(1,128)} %param.23) | copy-start | bytes 292
  12.8 0.7 %copy-start.18 = (f32[1,1,8]{2,1,0:T(1,128)S(1)}, f32[1,1,8]{2,1,0:T(1,128)}, u32[]{:S(2)}) copy-start(f32[1,1,8]{2,1,0:T(1,128)} %param.17) | copy-start | bytes 100
  14.2 0.7 %copy-start.3 = (bf16[512,128]{1,0:T(8,128)(2,1)}, bf16[512,128]{1,0:T(8,128)(2,1)S(1)}, u32[]{:S(2)}) copy-start(bf16[512,128]{1,0:T(8,128)(2,1)S(1)} %collective-permute-done.refs_4_) | copy-start | bytes 393220
  14.2 0.7 %copy-start.4 = (bf16[512,128]{1,0:T(8,128)(2,1)}, bf16[512,128]{1,0:T(8,128)(2,1)S(1)}, u32[]{:S(2)}) copy-start(bf16[512,128]{1,0:T(8,128)(2,1)S(1)} %collective-permute-done.4.refs_8_) | copy-start | bytes 393220
  14.2 0.7 %copy-start.5 = (bf16[512,128]{1,0:T(8,128)(2,1)}, bf16[512,128]{1,0:T(8,128)(2,1)S(1)}, u32[]{:S(2)}) copy-start(bf16[512,128]{1,0:T(8,128)(2,1)S(1)} %collective-permute-done.2.refs_6_) | copy-start | bytes 393220
  14.2 0.7 %copy-start.6 = (bf16[512,128]{1,0:T(8,128)(2,1)}, bf16[512,128]{1,0:T(8,128)(2,1)S(1)}, u32[]{:S(2)}) copy-start(bf16[512,128]{1,0:T(8,128)(2,1)S(1)} %collective-permute-done.6.refs_10_) | copy-start | bytes 393220
  20.0 6.4 %collective-permute-start.7 = (bf16[464,128]{1,0:T(8,128)(2,1)}, bf16[464,128]{1,0:T(8,128)(2,1)S(1)}, u32[]{:S(2)}, u32[]{:S(2)}) collective-permute-start(bf16[464,128]{1,0:T(8,128)(2,1)} %get-tuple-element.12), channel_id=1, source_target_pairs={{0,1},{1,0},{2,3},{3,2},{4,5},{5,4},{6,7},{7,6},{8,9},{9,8},{10,11... | collective-permute-start | bytes 356360 | tf_op jit(solution)/shard_map/ppermute | solution.py:21
  21.6 9.4 %collective-permute-start.8 = (bf16[464,128]{1,0:T(8,128)(2,1)}, bf16[464,128]{1,0:T(8,128)(2,1)S(1)}, u32[]{:S(2)}, u32[]{:S(2)}) collective-permute-start(bf16[464,128]{1,0:T(8,128)(2,1)} %get-tuple-element.13), channel_id=1, source_target_pairs={{0,2},{1,3},{2,0},{3,1},{4,6},{5,7},{6,4},{7,5},{8,10},{9,11},{10,... | collective-permute-start | bytes 356360 | tf_op jit(solution)/shard_map/ppermute | solution.py:21
  21.9 12.8 %collective-permute-start.9 = (bf16[464,128]{1,0:T(8,128)(2,1)}, bf16[464,128]{1,0:T(8,128)(2,1)S(1)}, u32[]{:S(2)}, u32[]{:S(2)}) collective-permute-start(bf16[464,128]{1,0:T(8,128)(2,1)} %get-tuple-element.14), channel_id=1, source_target_pairs={{0,3},{1,2},{2,1},{3,0},{4,7},{5,6},{6,5},{7,4},{8,11},{9,10},{10,... | collective-permute-start | bytes 356360 | tf_op jit(solution)/shard_map/ppermute | solution.py:21
  26.3 8.4 %copy-start.7 = (bf16[464,128]{1,0:T(8,128)(2,1)}, bf16[464,128]{1,0:T(8,128)(2,1)S(1)}, u32[]{:S(2)}) copy-start(bf16[464,128]{1,0:T(8,128)(2,1)S(1)} %collective-permute-done.7.refs_3_) | copy-start | bytes 356356
  31.0 3.7 %copy-start.8 = (bf16[464,128]{1,0:T(8,128)(2,1)}, bf16[464,128]{1,0:T(8,128)(2,1)S(1)}, u32[]{:S(2)}) copy-start(bf16[464,128]{1,0:T(8,128)(2,1)S(1)} %collective-permute-done.8.refs_4_) | copy-start | bytes 356356
  34.7 0.6 %copy-start.9 = (bf16[464,128]{1,0:T(8,128)(2,1)}, bf16[464,128]{1,0:T(8,128)(2,1)S(1)}, u32[]{:S(2)}) copy-start(bf16[464,128]{1,0:T(8,128)(2,1)S(1)} %collective-permute-done.9.refs_5_) | copy-start | bytes 356356
  37.5 3.5 %collective-permute-start.10 = (bf16[240,128]{1,0:T(8,128)(2,1)}, bf16[240,128]{1,0:T(8,128)(2,1)S(1)}, u32[]{:S(2)}, u32[]{:S(2)}) collective-permute-start(bf16[240,128]{1,0:T(8,128)(2,1)} %get-tuple-element.18), channel_id=1, source_target_pairs={{0,4},{4,0},{8,12},{12,8},{16,20},{20,16},{24,28},{28,24},{1,5},{5... | collective-permute-start | bytes 184328 | tf_op jit(solution)/shard_map/ppermute | solution.py:21
  37.5 7.0 %collective-permute-start.11 = (bf16[240,128]{1,0:T(8,128)(2,1)}, bf16[240,128]{1,0:T(8,128)(2,1)S(1)}, u32[]{:S(2)}, u32[]{:S(2)}) collective-permute-start(bf16[240,128]{1,0:T(8,128)(2,1)} %get-tuple-element.19), channel_id=1, source_target_pairs={{4,8},{12,16},{20,24},{8,4},{16,12},{24,20},{5,9},{13,17},{21,25},... | collective-permute-start | bytes 184328 | tf_op jit(solution)/shard_map/ppermute | solution.py:280
  40.9 3.6 %copy-start.10 = (bf16[240,128]{1,0:T(8,128)(2,1)}, bf16[240,128]{1,0:T(8,128)(2,1)S(1)}, u32[]{:S(2)}) copy-start(bf16[240,128]{1,0:T(8,128)(2,1)S(1)} %collective-permute-done.10.near_edge) | copy-start | bytes 184324
  44.5 0.6 %copy-start.11 = (bf16[240,128]{1,0:T(8,128)(2,1)}, bf16[240,128]{1,0:T(8,128)(2,1)S(1)}, u32[]{:S(2)}) copy-start(bf16[240,128]{1,0:T(8,128)(2,1)S(1)} %collective-permute-done.11.far_edge) | copy-start | bytes 184324

commit v2 on v1

--- a/solution.py
+++ b/solution.py
@@ -7,9 +7,9 @@
 from jax.experimental.pallas import tpu as pltpu
 from jax.sharding import PartitionSpec as P
 
+
 STEPS = 6
 SUB = 8
-TILE = 16
 LANES = 128
 
 gravity_step = 0.7
@@ -38,63 +38,71 @@
     return jnp.where(lane < gap, d, 0.0)
 
 
+def fetch_kernel(*refs):
+    sources, refs = refs[:13], refs[13:]
+    tables, scales, tile = refs[:3]
+    targets, small, sems = refs[3:7], refs[7:16], refs[16]
+    copies = [
+        pltpu.make_async_copy(source, target, sems.at[k])
+        for k, (source, target) in enumerate(zip(sources, small + targets))
+    ]
+    for copy in copies:
+        copy.start()
+    for copy in copies[:9]:
+        copy.wait()
+    near_rows, near_cols, near_scale, far_rows, far_cols, far_rank, far_scale = small[:7]
+    for k, part in enumerate((near_rows, near_cols, far_rows, far_cols, far_rank)):
+        tables[k : k + 1, 0 : part.shape[1]] = part[...]
+    for k, part in enumerate((near_scale, far_scale)):
+        scales[k : k + 1, 0 : part.shape[1]] = part[...]
+    d = small[7][...] * small[8][...].astype(jnp.float32)
+    by, bx = d.shape
+    tile[...] = jnp.concatenate([d, jnp.zeros((by, LANES - bx), jnp.float32)], axis=1)
+    for copy in copies[9:]:
+        copy.wait()
+
+
 def blocks_kernel(dims, *refs):
     n_sea, n_fault, n_near, n_far, leaf, rank, rows, leaf_count, bx, wx = dims
-    ints, scales, tile = refs[:3]
-    slots = refs[3 : 3 + n_sea]
-    near, left, right = refs[3 + n_sea : 6 + n_sea]
-    own = refs[6 + n_sea]
-    outs = refs[7 + n_sea : 6 + n_sea + n_fault]
-    slip, near_v, left_v, right_v, coeffs, acc, wide, sems = refs[6 + n_sea + n_fault :]
-    sea = ints[0]
-    fault = ints[1]
+    tables, scales, tile = refs[:3]
+    refs = refs[3:]
+    slots = refs[:n_sea]
+    near, left, right, own = refs[n_sea : 4 + n_sea]
+    outs = refs[4 + n_sea : 3 + n_sea + n_fault]
+    slip, coeffs, acc, wide = refs[3 + n_sea + n_fault :]
+    sea = lax.axis_index("sea")
+    fault = lax.axis_index("fault")
     members = slip.shape[1]
     by = tile.shape[0]
     width = leaf_count * leaf // by
     halo = (wx - bx) // 2
-    copies = []
     for k in range(n_sea):
         start = pl.multiple_of((sea ^ k) * rows, rows)
-        copies.append(pltpu.make_async_copy(slots[k], slip.at[pl.ds(start, rows)], sems.at[k]))
-    loads = [
-        pltpu.make_async_copy(right, right_v, sems.at[n_sea]),
-        pltpu.make_async_copy(near, near_v, sems.at[n_sea + 1]),
-        pltpu.make_async_copy(left, left_v, sems.at[n_sea + 2]),
-    ]
-    for copy in copies + loads:
-        copy.start()
+        slip[pl.ds(start, rows)] = slots[k][...]
     acc[...] = jnp.zeros_like(acc)
     edge = jnp.zeros((halo,) + wide.shape[1:], jnp.float32)
     wide[0:halo] = edge
     wide[halo + width :] = edge
-    for copy in copies:
-        copy.wait()
-    at_near_rows, at_near_cols = 2, 2 + n_near
-    at_far_rows = 2 + 2 * n_near
-    at_far_cols, at_far_rank = at_far_rows + n_far, at_far_rows + 2 * n_far
-    loads[0].wait()
     level = lax.broadcasted_iota(jnp.int32, (rank, members), 0)
     for b in range(n_far):
-        start = pl.multiple_of(ints[at_far_cols + b] * leaf, leaf)
+        start = pl.multiple_of(tables[3, b] * leaf, leaf)
         c = jnp.dot(
-            right_v[b], slip[pl.ds(start, leaf), :], preferred_element_type=jnp.float32
-        )
-        coeffs[b] = jnp.where(level < ints[at_far_rank + b], c, 0.0).astype(jnp.bfloat16)
-    loads[1].wait()
+            right[b], slip[pl.ds(start, leaf), :], preferred_element_type=jnp.float32
+        )
+        coeffs[b] = jnp.where(level < tables[4, b], c, 0.0).astype(jnp.bfloat16)
     for b in range(n_near):
-        start = pl.multiple_of(ints[at_near_cols + b] * leaf, leaf)
-        target = pl.multiple_of(ints[at_near_rows + b] * leaf, leaf)
+        start = pl.multiple_of(tables[1, b] * leaf, leaf)
+        target = pl.multiple_of(tables[0, b] * leaf, leaf)
         term = jnp.dot(
-            near_v[b], slip[pl.ds(start, leaf), :], preferred_element_type=jnp.float32
-        )
-        acc[pl.ds(target, leaf), :] += scales[b] * term
-    loads[2].wait()
+            near[b], slip[pl.ds(start, leaf), :], preferred_element_type=jnp.float32
+        )
+        acc[pl.ds(target, leaf), :] += scales[0, b] * term
     for b in range(n_far):
-        target = pl.multiple_of(ints[at_far_rows + b] * leaf, leaf)
+        target = pl.multiple_of(tables[2, b] * leaf, leaf)
         term = lax.dot_general(
-            left_v[b], coeffs[b], (((0,), (0,)), ((), ())), preferred_element_type=jnp.float32
-        )
-        acc[pl.ds(target, leaf), :] += scales[n_near + b] * term
+            left[b], coeffs[b], (((0,), (0,)), ((), ())), preferred_element_type=jnp.float32
+        )
+        acc[pl.ds(target, leaf), :] += scales[1, b] * term
     for x in range(width):
         wide[halo + x] = acc[pl.ds(x, by, stride=width), :]
     own[...] = wide[pl.ds(fault * bx, wx)].reshape(wx * by, members)
@@ -107,11 +115,11 @@
 
 def sum_kernel(dims, *refs):
     n_fault, bx, wx, by = dims
-    ints, tile, own = refs[:3]
-    parts = refs[3 : 2 + n_fault]
-    total, depth, uplift, near_edge, far_edge = refs[2 + n_fault :]
-    sea = ints[0]
-    fault = ints[1]
+    tile, own = refs[:2]
+    parts = refs[2 : 1 + n_fault]
+    total, depth, uplift, near_edge, far_edge = refs[1 + n_fault :]
+    sea = lax.axis_index("sea")
+    fault = lax.axis_index("fault")
     halo = (wx - bx) // 2
     cells = wx * by
     s = own[...]
@@ -145,10 +153,10 @@
     far_edge[wx * SUB :] = packed
 
 
-def steps_kernel(dims, ints, total, depth, near_edge, far_edge, level, h, e, n, de, dn):
+def steps_kernel(dims, total, depth, near_edge, far_edge, level, h, e, n, de, dn):
     bx, wx, by = dims
     halo = (wx - bx) // 2
-    odd = ints[0] & 1
+    odd = lax.axis_index("sea") & 1
     span = by + 2 * SUB
     edge = wx * SUB
     lanes = depth.shape[1]
@@ -220,75 +228,98 @@
     wx = bx + 2 * STEPS
     f32, bf16 = jnp.float32, jnp.bfloat16
 
-    slots = [slip_rate]
-    across = [swap(slip_rate, "sea", k) for k in range(2, n_sea, 2)]
-    slots.append(swap(slip_rate, "sea", 1))
-    for part in across:
-        slots += [part, swap(part, "sea", 1)]
-
-    place = jnp.stack([lax.axis_index("sea"), lax.axis_index("fault")]).astype(jnp.int32)
-    ints = jnp.concatenate(
-        [place]
-        + [a.reshape(-1) for a in (near_rows, near_cols, far_rows, far_cols, far_rank)]
-    )
-    scales = jnp.concatenate([near_scale.reshape(-1), far_scale.reshape(-1)])
-    tile = jnp.pad(sea_depth * wet_mask.astype(f32), ((0, 0), (0, LANES - bx)))
-
-    anywhere = pl.BlockSpec(memory_space=pl.ANY)
+    across = {}
+    for k in range(2, n_sea, 2):
+        across[k] = swap(slip_rate, "sea", k)
+    across[1] = swap(slip_rate, "sea", 1)
+    for k in range(2, n_sea, 2):
+        across[k + 1] = swap(across[k], "sea", 1)
+
     vector = pl.BlockSpec(memory_space=pltpu.VMEM)
     scalar = pl.BlockSpec(memory_space=pltpu.SMEM)
+    outside = pl.BlockSpec(memory_space=pltpu.HBM)
+    short = [near_rows, near_cols, near_scale, far_rows, far_cols, far_rank, far_scale]
+    short = [a[0] for a in short] + [sea_depth, wet_mask]
+    heavy = [slip_rate, near_blocks[0, 0], far_left[0, 0], far_right[0, 0]]
+    moved = sum(a.size * 2 for a in heavy)
+    tables, scales, tile, mine, near, left, right = pl.pallas_call(
+        fetch_kernel,
+        out_shape=[
+            jax.ShapeDtypeStruct((SUB, LANES), jnp.int32),
+            jax.ShapeDtypeStruct((SUB, LANES), f32),
+            jax.ShapeDtypeStruct((by, LANES), f32),
+        ]
+        + [jax.ShapeDtypeStruct(a.shape, bf16) for a in heavy],
+        in_specs=[outside] * 13,
+        out_specs=[vector] * 7,
+        scratch_shapes=[pltpu.VMEM(a.shape, a.dtype) for a in short]
+        + [pltpu.SemaphoreType.DMA((13,))],
+        compiler_params=pltpu.CompilerParams(vmem_limit_bytes=4 << 20),
+        cost_estimate=pl.CostEstimate(flops=0, bytes_accessed=2 * moved, transcendentals=0),
+        name="fetch",
+    )(*[pltpu.with_memory_space_constraint(a, pltpu.HBM) for a in short + heavy])
+    slots = [mine] + [across[k] for k in range(1, n_sea)]
     cells = wx * by
     dims = (n_sea, n_fault, n_near, n_far, leaf, rank, rows, leaf_count, bx, wx)
     own, *chunks = pl.pallas_call(
         functools.partial(blocks_kernel, dims),
         out_shape=[jax.ShapeDtypeStruct((cells, members), f32)]
         + [jax.ShapeDtypeStruct((cells + by, members), bf16)] * (n_fault - 1),
-        in_specs=[scalar, scalar, vector] + [anywhere] * (n_sea + 3),
+        in_specs=[scalar] * 2 + [vector] * (n_sea + 4),
         out_specs=[vector] * n_fault,
         scratch_shapes=[
             pltpu.VMEM((n_sea * rows, members), bf16),
-            pltpu.VMEM(near_blocks.shape[2:], bf16),
-            pltpu.VMEM(far_left.shape[2:], bf16),
-            pltpu.VMEM(far_right.shape[2:], bf16),
             pltpu.VMEM((n_far, rank, members), bf16),
             pltpu.VMEM((leaf_count * leaf, members), f32),
             pltpu.VMEM((n_fault * bx + 2 * STEPS, by, members), f32),
-            pltpu.SemaphoreType.DMA((n_sea + 3,)),
         ],
+        compiler_params=pltpu.CompilerParams(vmem_limit_bytes=12 << 20),
         name="blocks",
-    )(ints, scales, tile, *slots, near_blocks[0, 0], far_left[0, 0], far_right[0, 0])
-
-    got = [swap(chunks[k - 1], "fault", k) for k in range(1, n_fault)]
+    )(
+        tables,
+        scales,
+        tile,
+        *slots,
+        near,
+        left,
+        right,
+    )
+
+    got = []
+    for k in range(1, n_fault):
+        got.append(swap(chunks[k - 1], "fault", k))
 
     edge = jax.ShapeDtypeStruct((wx * SUB + by, members), bf16)
     total, depth, uplift, near_edge, far_edge = pl.pallas_call(
         functools.partial(sum_kernel, (n_fault, bx, wx, by)),
         out_shape=[
             jax.ShapeDtypeStruct((cells, members), f32),
-            jax.ShapeDtypeStruct((by, LANES), f32),
+            jax.ShapeDtypeStruct((by, members), f32),
             jax.ShapeDtypeStruct((by, bx, members), f32),
             edge,
             edge,
         ],
-        in_specs=[scalar] + [vector] * (1 + n_fault),
+        in_specs=[vector] * (1 + n_fault),
         out_specs=[vector] * 5,
+        compiler_params=pltpu.CompilerParams(vmem_limit_bytes=8 << 20),
         name="sums",
-    )(ints, tile, own, *got)
-
-    near_edge = swap(near_edge, "sea", 1)
+    )(tile, own, *got)
+
     pairs = [(i, i + 1) for i in range(1, n_sea - 1, 2)]
     far_edge = lax.ppermute(far_edge, "sea", pairs + [(b, a) for a, b in pairs])
+    near_edge = swap(near_edge, "sea", 1)
 
     span = by + 2 * SUB
     field = pltpu.VMEM((wx, span, members), f32)
     level = pl.pallas_call(
         functools.partial(steps_kernel, (bx, wx, by)),
         out_shape=jax.ShapeDtypeStruct((by, bx, members), f32),
-        in_specs=[scalar] + [vector] * 4,
+        in_specs=[vector] * 4,
         out_specs=vector,
         scratch_shapes=[field] * 5,
+        compiler_params=pltpu.CompilerParams(vmem_limit_bytes=8 << 20),
         name="steps",
-    )(ints, total, depth, near_edge, far_edge)
+    )(total, depth, near_edge, far_edge)
     return uplift, level
 
 
@@ -308,6 +339,7 @@
         P("sea", "fault"),
         P("sea", "fault"),
     )
+
     return jax.shard_map(
         on_device,
         mesh=mesh,

time: 48.9 us -> 40.4 us (0.83)
  the two profiles are of different devices: /device:TPU:20 before, /device:TPU:11 now
where the time goes in v2:
time: 40.4 us; the launch traced here: 40.2 us
  waiting for transfers between devices  16.7 us (41%)
  starting transfers between devices  15.7 us (39%)
  Pallas kernels  7.1 us (18%)
  between operations  0.71 us (2%)
    ppermute x11, starting transfers between devices, swap(): return lax.ppermute(x, axis, [(i, i ^ k) for i in range(count)])  13.7 us
    ppermute x11, waiting for transfers between devices, swap(): return lax.ppermute(x, axis, [(i, i ^ k) for i in range(count)])  12.3 us
    ppermute x1, waiting for transfers between devices, on_device(): far_edge = lax.ppermute(far_edge, 'sea', pairs + [(b, a) for a, b in pairs])  4.43 us
    pallas_call x1, Pallas kernels, on_device(): pl.pallas_call(functools.partial(blocks_kernel, dims), out_shape=[jax.Sha...  2.24 us
    pallas_call x1, Pallas kernels, on_device(): pl.pallas_call(functools.partial(steps_kernel, (bx, wx, by)), out_shape=j...  2.15 us
    ppermute x1, starting transfers between devices, on_device(): far_edge = lax.ppermute(far_edge, 'sea', pairs + [(b, a) for a, b in pairs])  1.98 us
    pallas_call x1, Pallas kernels, on_device(): pl.pallas_call(fetch_kernel, out_shape=[jax.ShapeDtypeStruct((SUB, LANES)...  1.87 us
    pallas_call x1, Pallas kernels, on_device(): pl.pallas_call(functools.partial(sum_kernel, (n_fault, bx, wx, by)), out_...  0.85 us
  transfers between devices with their start and end apart: 12, of which 6 were waited for; matrix products, arithmetic and copies ran while one was open for 0% of the time, Pallas kernels for 5%

profile of v2, /device:TPU:11, one launch (start us, length us, event | category | flops | bytes accessed | tf_op | source)
XLA Modules:
  0.0 40.2 jit_solution(3761397882554462405)
XLA Ops:
  0.6 0.3 collective-permute-start.1
  1.0 2.2 %collective-permute-start.5 = (bf16[512,128]{1,0:T(8,128)(2,1)}, bf16[512,128]{1,0:T(8,128)(2,1)S(1)}, u32[]{:S(2)}, u32[]{:S(2)}) collective-permute-start(bf16[512,128]{1,0:T(8,128)(2,1)} %refs_9_.1), channel_id=1, source_target_pairs={{0,24},{4,28},{8,16},{12,20},{16,8},{20,12},{24,0},{28,4},{1,25},{... | collective-permute-start | bytes 393224 | tf_op jit(solution)/shard_map/ppermute | solution.py:21
  3.1 0.2 collective-permute-start.3
  3.3 1.5 %collective-permute-start = (bf16[512,128]{1,0:T(8,128)(2,1)}, bf16[512,128]{1,0:T(8,128)(2,1)S(1)}, u32[]{:S(2)}, u32[]{:S(2)}) collective-permute-start(bf16[512,128]{1,0:T(8,128)(2,1)} %refs_9_.1), channel_id=1, source_target_pairs={{0,4},{4,0},{8,12},{12,8},{16,20},{20,16},{24,28},{28,24},{1,5},{5... | collective-permute-start | bytes 393224 | tf_op jit(solution)/shard_map/ppermute | solution.py:21
  4.9 0.4 %collective-permute-done.1.refs_5_ = bf16[512,128]{1,0:T(8,128)(2,1)S(1)} collective-permute-done((bf16[512,128]{1,0:T(8,128)(2,1)}, bf16[512,128]{1,0:T(8,128)(2,1)S(1)}, u32[]{:S(2)}, u32[]{:S(2)}) %collective-permute-start.1) | collective-permute-done | bytes 131104 | tf_op jit(solution)/shard_map/ppermute | solution.py:21
  5.3 2.7 %collective-permute-start.2 = (bf16[512,128]{1,0:T(8,128)(2,1)S(1)}, bf16[512,128]{1,0:T(8,128)(2,1)S(1)}, u32[]{:S(2)}, u32[]{:S(2)}) collective-permute-start(bf16[512,128]{1,0:T(8,128)(2,1)S(1)} %collective-permute-done.1.refs_5_), channel_id=1, source_target_pairs={{0,4},{4,0},{8,12},{12,8},{16,20},{20,16},{24,28},{28,24},{1,5},{5... | collective-permute-start | bytes 393224 | tf_op jit(solution)/shard_map/ppermute | solution.py:21
  8.0 1.1 %collective-permute-done.5.refs_9_ = bf16[512,128]{1,0:T(8,128)(2,1)S(1)} collective-permute-done((bf16[512,128]{1,0:T(8,128)(2,1)}, bf16[512,128]{1,0:T(8,128)(2,1)S(1)}, u32[]{:S(2)}, u32[]{:S(2)}) %collective-permute-start.5) | collective-permute-done | bytes 131104 | tf_op jit(solution)/shard_map/ppermute | solution.py:21
  9.1 1.6 %collective-permute-start.6 = (bf16[512,128]{1,0:T(8,128)(2,1)S(1)}, bf16[512,128]{1,0:T(8,128)(2,1)S(1)}, u32[]{:S(2)}, u32[]{:S(2)}) collective-permute-start(bf16[512,128]{1,0:T(8,128)(2,1)S(1)} %collective-permute-done.5.refs_9_), channel_id=1, source_target_pairs={{0,4},{4,0},{8,12},{12,8},{16,20},{20,16},{24,28},{28,24},{1,5},{5... | collective-permute-start | bytes 393224 | tf_op jit(solution)/shard_map/ppermute | solution.py:21
  10.7 0.0 collective-permute-done.3.refs_7_
  10.7 1.3 %collective-permute-start.4 = (bf16[512,128]{1,0:T(8,128)(2,1)S(1)}, bf16[512,128]{1,0:T(8,128)(2,1)S(1)}, u32[]{:S(2)}, u32[]{:S(2)}) collective-permute-start(bf16[512,128]{1,0:T(8,128)(2,1)S(1)} %collective-permute-done.3.refs_7_), channel_id=1, source_target_pairs={{0,4},{4,0},{8,12},{12,8},{16,20},{20,16},{24,28},{28,24},{1,5},{5... | collective-permute-start | bytes 393224 | tf_op jit(solution)/shard_map/ppermute | solution.py:21
  12.1 1.9 %fetch.1 = (s32[8,128]{1,0:T(8,128)S(1)}, f32[8,128]{1,0:T(8,128)S(1)}, f32[16,128]{1,0:T(8,128)S(1)}, bf16[512,128]{1,0:T(8,128)(2,1)S(1)}, bf16[8,256,256]{2,1...) custom-call(s32[1,8]{1,0:T(1,128)} %bitcast.13, s32[1,8]{1,0:T(1,128)} %bitcast.14, ...), custom_call_target="tpu_custom_call" | custom-call | bytes 4718592 | tf_op jit(solution)/shard_map/fetch/pallas_call | solution.py:245
  13.9 0.0 collective-permute-done.refs_4_
  13.9 0.0 collective-permute-done.2.refs_6_
  13.9 0.0 collective-permute-done.6.refs_10_
  14.0 0.0 collective-permute-done.4.refs_8_
  14.0 2.2 %blocks.1 = (f32[448,128]{1,0:T(8,128)S(1)}, bf16[464,128]{1,0:T(8,128)(2,1)S(1)}, bf16[464,128]{1,0:T(8,128)(2,1)S(1)}, bf16[464,128]{1,0:T(8,128)(2,1)S(1)}) custom-call(s32[8,128]{1,0:T(8,128)S(1)} %get-tuple-element.19.refs_0_, f32[8,128]{1,0:T(8,128)S(1)} %get-tuple-element.20.refs_1_, f32[16,128]{1,0:T(8,128)S(1)} %get-tuple-element.18.refs_2_.refs_0_, ...), custom_call_target="tpu_custom_call" | custom-call | tf_op jit(solution)/shard_map/blocks/pallas_call | solution.py:264
  16.2 0.2 collective-permute-start.7
  16.5 2.3 %collective-permute-start.8 = (bf16[464,128]{1,0:T(8,128)(2,1)S(1)}, bf16[464,128]{1,0:T(8,128)(2,1)S(1)}, u32[]{:S(2)}, u32[]{:S(2)}) collective-permute-start(bf16[464,128]{1,0:T(8,128)(2,1)S(1)} %get-tuple-element.27), channel_id=1, source_target_pairs={{0,2},{1,3},{2,0},{3,1},{4,6},{5,7},{6,4},{7,5},{8,10},{9,11},{10,... | collective-permute-start | bytes 356360 | tf_op jit(solution)/shard_map/ppermute | solution.py:21
  18.8 0.2 collective-permute-start.9
  18.9 2.1 %collective-permute-done.7.refs_2_ = bf16[464,128]{1,0:T(8,128)(2,1)S(1)} collective-permute-done((bf16[464,128]{1,0:T(8,128)(2,1)S(1)}, bf16[464,128]{1,0:T(8,128)(2,1)S(1)}, u32[]{:S(2)}, u32[]{:S(2)}) %collective-permute-start.7) | collective-permute-done | bytes 118816 | tf_op jit(solution)/shard_map/ppermute | solution.py:21
  21.1 5.0 %collective-permute-done.8.refs_3_ = bf16[464,128]{1,0:T(8,128)(2,1)S(1)} collective-permute-done((bf16[464,128]{1,0:T(8,128)(2,1)S(1)}, bf16[464,128]{1,0:T(8,128)(2,1)S(1)}, u32[]{:S(2)}, u32[]{:S(2)}) %collective-permute-start.8) | collective-permute-done | bytes 118816 | tf_op jit(solution)/shard_map/ppermute | solution.py:21
  26.1 3.6 %collective-permute-done.9.refs_4_ = bf16[464,128]{1,0:T(8,128)(2,1)S(1)} collective-permute-done((bf16[464,128]{1,0:T(8,128)(2,1)S(1)}, bf16[464,128]{1,0:T(8,128)(2,1)S(1)}, u32[]{:S(2)}, u32[]{:S(2)}) %collective-permute-start.9) | collective-permute-done | bytes 118816 | tf_op jit(solution)/shard_map/ppermute | solution.py:21
  29.7 0.8 %sums.1 = (f32[448,128]{1,0:T(8,128)S(1)}, f32[16,128]{1,0:T(8,128)S(1)}, f32[16,16,128]{2,1,0:T(8,128)}, bf16[240,128]{1,0:T(8,128)(2,1)S(1)}, bf16[240,128]{1,0:T(8,128)(2,1)S(1)}) custom-call(f32[16,128]{1,0:T(8,128)S(1)} %get-tuple-element.18.refs_2_.refs_0_, f32[448,128]{1,0:T(8,128)S(1)} %get-tuple-element.25.refs_1_, ...), custom_call_target="tpu_custom_call" | custom-call | tf_op jit(solution)/shard_map/sums/pallas_call | solution.py:293
  30.5 1.1 %collective-permute-start.10 = (bf16[240,128]{1,0:T(8,128)(2,1)S(1)}, bf16[240,128]{1,0:T(8,128)(2,1)S(1)}, u32[]{:S(2)}, u32[]{:S(2)}) collective-permute-start(bf16[240,128]{1,0:T(8,128)(2,1)S(1)} %get-tuple-element.32), channel_id=1, source_target_pairs={{0,4},{4,0},{8,12},{12,8},{16,20},{20,16},{24,28},{28,24},{1,5},{5... | collective-permute-start | bytes 184328 | tf_op jit(solution)/shard_map/ppermute | solution.py:21
  31.6 2.0 %collective-permute-start.11 = (bf16[240,128]{1,0:T(8,128)(2,1)S(1)}, bf16[240,128]{1,0:T(8,128)(2,1)S(1)}, u32[]{:S(2)}, u32[]{:S(2)}) collective-permute-start(bf16[240,128]{1,0:T(8,128)(2,1)S(1)} %get-tuple-element.33), channel_id=1, source_target_pairs={{4,8},{12,16},{20,24},{8,4},{16,12},{24,20},{5,9},{13,17},{21,25},... | collective-permute-start | bytes 184328 | tf_op jit(solution)/shard_map/ppermute | solution.py:309
  33.6 0.0 collective-permute-done.10.near_edge
  33.7 4.4 %collective-permute-done.11.far_edge = bf16[240,128]{1,0:T(8,128)(2,1)S(1)} collective-permute-done((bf16[240,128]{1,0:T(8,128)(2,1)S(1)}, bf16[240,128]{1,0:T(8,128)(2,1)S(1)}, u32[]{:S(2)}, u32[]{:S(2)}) %collective-permute-start.11) | collective-permute-done | bytes 61472 | tf_op jit(solution)/shard_map/ppermute | solution.py:309
  38.1 2.1 %steps.1 = f32[16,16,128]{2,1,0:T(8,128)} custom-call(f32[448,128]{1,0:T(8,128)S(1)} %get-tuple-element.30.total, f32[16,128]{1,0:T(8,128)S(1)} %get-tuple-element.31.depth, bf16[240,128]{1,0:T(8,128)(2,1)S(1)} %collective-permute-done.10.near_edge, bf16[240,128]{1,0:T(8,128)(2,1)S(1)} %collective-permute-done.11.far_edge), custom_call_target="tpu_custom_call" | custom-call | tf_op jit(solution)/shard_map/steps/pallas_call | solution.py:314
Async XLA Ops:
  0.6 4.7 %collective-permute-start.1 = (bf16[512,128]{1,0:T(8,128)(2,1)}, bf16[512,128]{1,0:T(8,128)(2,1)S(1)}, u32[]{:S(2)}, u32[]{:S(2)}) collective-permute-start(bf16[512,128]{1,0:T(8,128)(2,1)} %refs_9_.1), channel_id=1, source_target_pairs={{0,8},{4,12},{8,0},{12,4},{16,24},{20,28},{24,16},{28,20},{1,9},{5... | collective-permute-start | bytes 393224 | tf_op jit(solution)/shard_map/ppermute | solution.py:21
  1.0 8.1 %collective-permute-start.5 = (bf16[512,128]{1,0:T(8,128)(2,1)}, bf16[512,128]{1,0:T(8,128)(2,1)S(1)}, u32[]{:S(2)}, u32[]{:S(2)}) collective-permute-start(bf16[512,128]{1,0:T(8,128)(2,1)} %refs_9_.1), channel_id=1, source_target_pairs={{0,24},{4,28},{8,16},{12,20},{16,8},{20,12},{24,0},{28,4},{1,25},{... | collective-permute-start | bytes 393224 | tf_op jit(solution)/shard_map/ppermute | solution.py:21
  3.1 7.6 %collective-permute-start.3 = (bf16[512,128]{1,0:T(8,128)(2,1)}, bf16[512,128]{1,0:T(8,128)(2,1)S(1)}, u32[]{:S(2)}, u32[]{:S(2)}) collective-permute-start(bf16[512,128]{1,0:T(8,128)(2,1)} %refs_9_.1), channel_id=1, source_target_pairs={{0,16},{4,20},{8,24},{12,28},{16,0},{20,4},{24,8},{28,12},{1,17},{... | collective-permute-start | bytes 393224 | tf_op jit(solution)/shard_map/ppermute | solution.py:21
  3.3 10.6 %collective-permute-start = (bf16[512,128]{1,0:T(8,128)(2,1)}, bf16[512,128]{1,0:T(8,128)(2,1)S(1)}, u32[]{:S(2)}, u32[]{:S(2)}) collective-permute-start(bf16[512,128]{1,0:T(8,128)(2,1)} %refs_9_.1), channel_id=1, source_target_pairs={{0,4},{4,0},{8,12},{12,8},{16,20},{20,16},{24,28},{28,24},{1,5},{5... | collective-permute-start | bytes 393224 | tf_op jit(solution)/shard_map/ppermute | solution.py:21
  5.3 8.6 %collective-permute-start.2 = (bf16[512,128]{1,0:T(8,128)(2,1)S(1)}, bf16[512,128]{1,0:T(8,128)(2,1)S(1)}, u32[]{:S(2)}, u32[]{:S(2)}) collective-permute-start(bf16[512,128]{1,0:T(8,128)(2,1)S(1)} %collective-permute-done.1.refs_5_), channel_id=1, source_target_pairs={{0,4},{4,0},{8,12},{12,8},{16,20},{20,16},{24,28},{28,24},{1,5},{5... | collective-permute-start | bytes 393224 | tf_op jit(solution)/shard_map/ppermute | solution.py:21
  9.1 4.9 %collective-permute-start.6 = (bf16[512,128]{1,0:T(8,128)(2,1)S(1)}, bf16[512,128]{1,0:T(8,128)(2,1)S(1)}, u32[]{:S(2)}, u32[]{:S(2)}) collective-permute-start(bf16[512,128]{1,0:T(8,128)(2,1)S(1)} %collective-permute-done.5.refs_9_), channel_id=1, source_target_pairs={{0,4},{4,0},{8,12},{12,8},{16,20},{20,16},{24,28},{28,24},{1,5},{5... | collective-permute-start | bytes 393224 | tf_op jit(solution)/shard_map/ppermute | solution.py:21
  10.7 3.3 %collective-permute-start.4 = (bf16[512,128]{1,0:T(8,128)(2,1)S(1)}, bf16[512,128]{1,0:T(8,128)(2,1)S(1)}, u32[]{:S(2)}, u32[]{:S(2)}) collective-permute-start(bf16[512,128]{1,0:T(8,128)(2,1)S(1)} %collective-permute-done.3.refs_7_), channel_id=1, source_target_pairs={{0,4},{4,0},{8,12},{12,8},{16,20},{20,16},{24,28},{28,24},{1,5},{5... | collective-permute-start | bytes 393224 | tf_op jit(solution)/shard_map/ppermute | solution.py:21
  16.2 4.9 %collective-permute-start.7 = (bf16[464,128]{1,0:T(8,128)(2,1)S(1)}, bf16[464,128]{1,0:T(8,128)(2,1)S(1)}, u32[]{:S(2)}, u32[]{:S(2)}) collective-permute-start(bf16[464,128]{1,0:T(8,128)(2,1)S(1)} %get-tuple-element.26), channel_id=1, source_target_pairs={{0,1},{1,0},{2,3},{3,2},{4,5},{5,4},{6,7},{7,6},{8,9},{9,8},{10,11... | collective-permute-start | bytes 356360 | tf_op jit(solution)/shard_map/ppermute | solution.py:21
  16.5 9.6 %collective-permute-start.8 = (bf16[464,128]{1,0:T(8,128)(2,1)S(1)}, bf16[464,128]{1,0:T(8,128)(2,1)S(1)}, u32[]{:S(2)}, u32[]{:S(2)}) collective-permute-start(bf16[464,128]{1,0:T(8,128)(2,1)S(1)} %get-tuple-element.27), channel_id=1, source_target_pairs={{0,2},{1,3},{2,0},{3,1},{4,6},{5,7},{6,4},{7,5},{8,10},{9,11},{10,... | collective-permute-start | bytes 356360 | tf_op jit(solution)/shard_map/ppermute | solution.py:21
  18.8 10.9 %collective-permute-start.9 = (bf16[464,128]{1,0:T(8,128)(2,1)S(1)}, bf16[464,128]{1,0:T(8,128)(2,1)S(1)}, u32[]{:S(2)}, u32[]{:S(2)}) collective-permute-start(bf16[464,128]{1,0:T(8,128)(2,1)S(1)} %get-tuple-element.28), channel_id=1, source_target_pairs={{0,3},{1,2},{2,1},{3,0},{4,7},{5,6},{6,5},{7,4},{8,11},{9,10},{10,... | collective-permute-start | bytes 356360 | tf_op jit(solution)/shard_map/ppermute | solution.py:21
  30.5 3.1 %collective-permute-start.10 = (bf16[240,128]{1,0:T(8,128)(2,1)S(1)}, bf16[240,128]{1,0:T(8,128)(2,1)S(1)}, u32[]{:S(2)}, u32[]{:S(2)}) collective-permute-start(bf16[240,128]{1,0:T(8,128)(2,1)S(1)} %get-tuple-element.32), channel_id=1, source_target_pairs={{0,4},{4,0},{8,12},{12,8},{16,20},{20,16},{24,28},{28,24},{1,5},{5... | collective-permute-start | bytes 184328 | tf_op jit(solution)/shard_map/ppermute | solution.py:21
  31.6 6.4 %collective-permute-start.11 = (bf16[240,128]{1,0:T(8,128)(2,1)S(1)}, bf16[240,128]{1,0:T(8,128)(2,1)S(1)}, u32[]{:S(2)}, u32[]{:S(2)}) collective-permute-start(bf16[240,128]{1,0:T(8,128)(2,1)S(1)} %get-tuple-element.33), channel_id=1, source_target_pairs={{4,8},{12,16},{20,24},{8,4},{16,12},{24,20},{5,9},{13,17},{21,25},... | collective-permute-start | bytes 184328 | tf_op jit(solution)/shard_map/ppermute | solution.py:309

commit v3 on v2

--- a/solution.py
+++ b/solution.py
@@ -103,8 +103,7 @@
             left[b], coeffs[b], (((0,), (0,)), ((), ())), preferred_element_type=jnp.float32
         )
         acc[pl.ds(target, leaf), :] += scales[1, b] * term
-    for x in range(width):
-        wide[halo + x] = acc[pl.ds(x, by, stride=width), :]
+    wide[halo : halo + width] = jnp.swapaxes(acc[...].reshape(by, width, members), 0, 1)
     own[...] = wide[pl.ds(fault * bx, wx)].reshape(wx * by, members)
     packed = pieces(tile[...], bx)
     for k in range(1, n_fault):
@@ -117,7 +116,7 @@
     n_fault, bx, wx, by = dims
     tile, own = refs[:2]
     parts = refs[2 : 1 + n_fault]
-    total, depth, uplift, near_edge, far_edge = refs[1 + n_fault :]
+    total, depth, near_edge, far_edge = refs[1 + n_fault :]
     sea = lax.axis_index("sea")
     fault = lax.axis_index("fault")
     halo = (wx - bx) // 2
@@ -142,8 +141,6 @@
     depth[...] = d
     packed = pieces(d, lanes // 4)
     odd = sea & 1
-    for y in range(by):
-        uplift[y] = total[pl.ds(halo * by + y, bx, stride=by), :]
     stack = s.reshape(wx, by, s.shape[1])
     first = stack[:, 0:SUB, :].reshape(wx * SUB, -1).astype(jnp.bfloat16)
     last = stack[:, by - SUB :, :].reshape(wx * SUB, -1).astype(jnp.bfloat16)
@@ -153,11 +150,22 @@
     far_edge[wx * SUB :] = packed
 
 
-def steps_kernel(dims, total, depth, near_edge, far_edge, level, h, e, n, de, dn):
+def uplift_kernel(dims, total, depth, uplift, wet):
+    bx, wx, by = dims
+    halo = (wx - bx) // 2
+    across = jnp.transpose(jnp.where(depth[...] > 0.0, 1.0, 0.0))[halo : halo + bx]
+    for y in range(by):
+        wet[y] = jnp.broadcast_to(across[:, y : y + 1], wet.shape[1:])
+    for y in range(by):
+        uplift[y] = total[pl.ds(halo * by + y, bx, stride=by), :]
+
+
+def steps_kernel(dims, total, depth, wet, near_edge, far_edge, level, column, rows):
     bx, wx, by = dims
     halo = (wx - bx) // 2
     odd = lax.axis_index("sea") & 1
     span = by + 2 * SUB
+    folds = span // SUB
     edge = wx * SUB
     lanes = depth.shape[1]
     near = near_edge[...].astype(jnp.float32)
@@ -167,40 +175,52 @@
     prev_d = joined(prev[edge:], lanes // 4)[by - SUB :]
     post_d = joined(post[edge:], lanes // 4)[0:SUB]
     d = jnp.concatenate([prev_d, depth[...], post_d], axis=0)
-    east = jnp.minimum(d, pltpu.roll(d, lanes - 1, 1))
-    north = jnp.minimum(d, pltpu.roll(d, span - 1, 0))
-    wet = jnp.where(d > 0.0, 1.0, 0.0)
-    zero = jnp.zeros((span, lanes), jnp.float32)
+    scale = gravity_step * height_step
+    rows[0] = scale * jnp.minimum(d, pltpu.roll(d, lanes - 1, 1))
+    rows[1] = scale * jnp.minimum(d, pltpu.roll(d, span - 1, 0))
+    folded = [[rows[k, pl.ds(v, SUB, stride=folds), :] for v in range(folds)] for k in range(2)]
+
+    def spread(part, x):
+        return [jnp.broadcast_to(f[:, x : x + 1], (SUB, lanes)) for f in part]
+
+    h = []
     for x in range(wx):
-        column = jnp.concatenate(
-            [prev[x * SUB : (x + 1) * SUB], total[x * by : (x + 1) * by], post[x * SUB : (x + 1) * SUB]],
-            axis=0,
-        )
-        h[x] = column * jnp.broadcast_to(wet[:, x : x + 1], (span, lanes))
-        de[x] = jnp.broadcast_to(east[:, x : x + 1], (span, lanes))
-        dn[x] = jnp.broadcast_to(north[:, x : x + 1], (span, lanes))
-        e[x] = zero
-        n[x] = zero
+        base = x * span
+        column[base : base + SUB] = prev[x * SUB : (x + 1) * SUB]
+        column[base + SUB : base + SUB + by] = total[x * by : (x + 1) * by]
+        column[base + SUB + by : base + span] = post[x * SUB : (x + 1) * SUB]
+        h.append([column[pl.ds(base + v, SUB, stride=folds), :] for v in range(folds)])
+    de = [spread(folded[0], x) for x in range(wx)]
+    dn = [spread(folded[1], x) for x in range(wx)]
+    e = [None] * wx
+    n = [None] * wx
     for step in range(STEPS):
-        h_here = h[step]
-        flux_before = None
+        before = None
         for x in range(step, wx - 1 - step):
-            h_next = h[x + 1]
-            new_east = e[x] - gravity_step * (h_next - h_here)
-            e[x] = new_east
-            flux = de[x] * new_east
-            if flux_before is not None:
-                new_north = n[x] - gravity_step * (pltpu.roll(h_here, span - 1, 0) - h_here)
-                n[x] = new_north
-                flux_north = dn[x] * new_north
-                change = ((flux - flux_before) + flux_north) - pltpu.roll(flux_north, 1, 0)
-                h[x] = h_here - height_step * change
-            flux_before = flux
-            h_here = h_next
+            here = h[x]
+            flow = [a - b for a, b in zip(here, h[x + 1])]
+            if step:
+                flow = [a + b for a, b in zip(e[x], flow)]
+            e[x] = flow
+            flux = [a * b for a, b in zip(de[x], flow)]
+            if before is not None:
+                up = here[1:] + [pltpu.roll(here[0], SUB - 1, 0)]
+                flow = [a - b for a, b in zip(here, up)]
+                if step:
+                    flow = [a + b for a, b in zip(n[x], flow)]
+                n[x] = flow
+                rise = [a * b for a, b in zip(dn[x], flow)]
+                down = [pltpu.roll(rise[-1], 1, 0)] + rise[:-1]
+                h[x] = [
+                    here[v] - (((flux[v] - before[v]) + rise[v]) - down[v])
+                    for v in range(folds)
+                ]
+            before = flux
+    for x in range(bx):
+        for v in range(folds):
+            column[pl.ds(x * span + v, SUB, stride=folds), :] = h[halo + x][v]
     for y in range(by):
-        level[y] = jnp.concatenate(
-            [h[halo + x, SUB + y : SUB + y + 1, :] for x in range(bx)], axis=0
-        )
+        level[y] = wet[y] * column[pl.ds(SUB + y, bx, stride=span), :]
 
 
 def on_device(
@@ -290,17 +310,16 @@
         got.append(swap(chunks[k - 1], "fault", k))
 
     edge = jax.ShapeDtypeStruct((wx * SUB + by, members), bf16)
-    total, depth, uplift, near_edge, far_edge = pl.pallas_call(
+    total, depth, near_edge, far_edge = pl.pallas_call(
         functools.partial(sum_kernel, (n_fault, bx, wx, by)),
         out_shape=[
             jax.ShapeDtypeStruct((cells, members), f32),
             jax.ShapeDtypeStruct((by, members), f32),
-            jax.ShapeDtypeStruct((by, bx, members), f32),
             edge,
             edge,
         ],
         in_specs=[vector] * (1 + n_fault),
-        out_specs=[vector] * 5,
+        out_specs=[vector] * 4,
         compiler_params=pltpu.CompilerParams(vmem_limit_bytes=8 << 20),
         name="sums",
     )(tile, own, *got)
@@ -309,17 +328,25 @@
     far_edge = lax.ppermute(far_edge, "sea", pairs + [(b, a) for a, b in pairs])
     near_edge = swap(near_edge, "sea", 1)
 
+    uplift, wet = pl.pallas_call(
+        functools.partial(uplift_kernel, (bx, wx, by)),
+        out_shape=[jax.ShapeDtypeStruct((by, bx, members), f32)] * 2,
+        in_specs=[vector] * 2,
+        out_specs=[vector] * 2,
+        compiler_params=pltpu.CompilerParams(vmem_limit_bytes=4 << 20),
+        cost_estimate=pl.CostEstimate(flops=0, bytes_accessed=16 * cells * members, transcendentals=0),
+        name="uplift",
+    )(total, depth)
     span = by + 2 * SUB
-    field = pltpu.VMEM((wx, span, members), f32)
     level = pl.pallas_call(
         functools.partial(steps_kernel, (bx, wx, by)),
         out_shape=jax.ShapeDtypeStruct((by, bx, members), f32),
-        in_specs=[vector] * 4,
+        in_specs=[vector] * 5,
         out_specs=vector,
-        scratch_shapes=[field] * 5,
+        scratch_shapes=[pltpu.VMEM((wx * span, members), f32), pltpu.VMEM((2, span, LANES), f32)],
         compiler_params=pltpu.CompilerParams(vmem_limit_bytes=8 << 20),
         name="steps",
-    )(total, depth, near_edge, far_edge)
+    )(total, depth, wet, near_edge, far_edge)
     return uplift, level
 
 

time: 40.4 us -> 39.3 us (0.973)
  waiting for transfers between devices: 16.7 us -> 15.9 us
    ppermute x1, waiting for transfers between devices: 4.43 us -> 3.59 us  [on_device(): far_edge = lax.ppermute(far_edge, 'sea', pairs + [(b, a) for a, b in pairs])]
    pallas_call x0 -> x1, Pallas kernels: none -> 0.82 us  [on_device(): pl.pallas_call(functools.partial(uplift_kernel, (bx, wx, by)), out_shape=...]
    pallas_call x1, Pallas kernels: 0.85 us -> 0.24 us  [on_device(): pl.pallas_call(functools.partial(sum_kernel, (n_fault, bx, wx, by)), out_...]
  transfers between devices with their start and end apart: 12 -> 12, of which waited for: 6 -> 6; matrix products, arithmetic and copies ran while one was open for 0% -> 0% of each run, Pallas kernels for 5% -> 7%
where the time goes in v3:
time: 39.3 us; the launch traced here: 39.1 us
  waiting for transfers between devices  15.9 us (40%)
  starting transfers between devices  15.7 us (40%)
  Pallas kernels  6.79 us (17%)
  between operations  0.7 us (2%)
    ppermute x11, starting transfers between devices, swap(): return lax.ppermute(x, axis, [(i, i ^ k) for i in range(count)])  13.7 us
    ppermute x11, waiting for transfers between devices, swap(): return lax.ppermute(x, axis, [(i, i ^ k) for i in range(count)])  12.3 us
    ppermute x1, waiting for transfers between devices, on_device(): far_edge = lax.ppermute(far_edge, 'sea', pairs + [(b, a) for a, b in pairs])  3.59 us
    pallas_call x1, Pallas kernels, on_device(): pl.pallas_call(functools.partial(blocks_kernel, dims), out_shape=[jax.Sha...  2.03 us
    ppermute x1, starting transfers between devices, on_device(): far_edge = lax.ppermute(far_edge, 'sea', pairs + [(b, a) for a, b in pairs])  2 us
    pallas_call x1, Pallas kernels, on_device(): pl.pallas_call(fetch_kernel, out_shape=[jax.ShapeDtypeStruct((SUB, LANES)...  1.87 us
    pallas_call x1, Pallas kernels, on_device(): pl.pallas_call(functools.partial(steps_kernel, (bx, wx, by)), out_shape=j...  1.83 us
    pallas_call x1, Pallas kernels, on_device(): pl.pallas_call(functools.partial(uplift_kernel, (bx, wx, by)), out_shape=...  0.82 us
  transfers between devices with their start and end apart: 12, of which 6 were waited for; matrix products, arithmetic and copies ran while one was open for 0% of the time, Pallas kernels for 7%

profile of v3, /device:TPU:11, one launch (start us, length us, event | category | flops | bytes accessed | tf_op | source)
XLA Modules:
  0.0 39.1 jit_solution(10588410431720032109)
XLA Ops:
  0.6 0.3 collective-permute-start.1
  1.0 2.2 %collective-permute-start.5 = (bf16[512,128]{1,0:T(8,128)(2,1)}, bf16[512,128]{1,0:T(8,128)(2,1)S(1)}, u32[]{:S(2)}, u32[]{:S(2)}) collective-permute-start(bf16[512,128]{1,0:T(8,128)(2,1)} %refs_9_.1), channel_id=1, source_target_pairs={{0,24},{4,28},{8,16},{12,20},{16,8},{20,12},{24,0},{28,4},{1,25},{... | collective-permute-start | bytes 393224 | tf_op jit(solution)/shard_map/ppermute | solution.py:21
  3.1 0.2 collective-permute-start.3
  3.3 1.5 %collective-permute-start = (bf16[512,128]{1,0:T(8,128)(2,1)}, bf16[512,128]{1,0:T(8,128)(2,1)S(1)}, u32[]{:S(2)}, u32[]{:S(2)}) collective-permute-start(bf16[512,128]{1,0:T(8,128)(2,1)} %refs_9_.1), channel_id=1, source_target_pairs={{0,4},{4,0},{8,12},{12,8},{16,20},{20,16},{24,28},{28,24},{1,5},{5... | collective-permute-start | bytes 393224 | tf_op jit(solution)/shard_map/ppermute | solution.py:21
  4.9 0.4 %collective-permute-done.1.refs_5_ = bf16[512,128]{1,0:T(8,128)(2,1)S(1)} collective-permute-done((bf16[512,128]{1,0:T(8,128)(2,1)}, bf16[512,128]{1,0:T(8,128)(2,1)S(1)}, u32[]{:S(2)}, u32[]{:S(2)}) %collective-permute-start.1) | collective-permute-done | bytes 131104 | tf_op jit(solution)/shard_map/ppermute | solution.py:21
  5.3 2.7 %collective-permute-start.2 = (bf16[512,128]{1,0:T(8,128)(2,1)S(1)}, bf16[512,128]{1,0:T(8,128)(2,1)S(1)}, u32[]{:S(2)}, u32[]{:S(2)}) collective-permute-start(bf16[512,128]{1,0:T(8,128)(2,1)S(1)} %collective-permute-done.1.refs_5_), channel_id=1, source_target_pairs={{0,4},{4,0},{8,12},{12,8},{16,20},{20,16},{24,28},{28,24},{1,5},{5... | collective-permute-start | bytes 393224 | tf_op jit(solution)/shard_map/ppermute | solution.py:21
  8.0 1.1 %collective-permute-done.5.refs_9_ = bf16[512,128]{1,0:T(8,128)(2,1)S(1)} collective-permute-done((bf16[512,128]{1,0:T(8,128)(2,1)}, bf16[512,128]{1,0:T(8,128)(2,1)S(1)}, u32[]{:S(2)}, u32[]{:S(2)}) %collective-permute-start.5) | collective-permute-done | bytes 131104 | tf_op jit(solution)/shard_map/ppermute | solution.py:21
  9.1 1.6 %collective-permute-start.6 = (bf16[512,128]{1,0:T(8,128)(2,1)S(1)}, bf16[512,128]{1,0:T(8,128)(2,1)S(1)}, u32[]{:S(2)}, u32[]{:S(2)}) collective-permute-start(bf16[512,128]{1,0:T(8,128)(2,1)S(1)} %collective-permute-done.5.refs_9_), channel_id=1, source_target_pairs={{0,4},{4,0},{8,12},{12,8},{16,20},{20,16},{24,28},{28,24},{1,5},{5... | collective-permute-start | bytes 393224 | tf_op jit(solution)/shard_map/ppermute | solution.py:21
  10.7 0.0 collective-permute-done.3.refs_7_
  10.7 1.3 %collective-permute-start.4 = (bf16[512,128]{1,0:T(8,128)(2,1)S(1)}, bf16[512,128]{1,0:T(8,128)(2,1)S(1)}, u32[]{:S(2)}, u32[]{:S(2)}) collective-permute-start(bf16[512,128]{1,0:T(8,128)(2,1)S(1)} %collective-permute-done.3.refs_7_), channel_id=1, source_target_pairs={{0,4},{4,0},{8,12},{12,8},{16,20},{20,16},{24,28},{28,24},{1,5},{5... | collective-permute-start | bytes 393224 | tf_op jit(solution)/shard_map/ppermute | solution.py:21
  12.1 1.9 %fetch.1 = (s32[8,128]{1,0:T(8,128)S(1)}, f32[8,128]{1,0:T(8,128)S(1)}, f32[16,128]{1,0:T(8,128)S(1)}, bf16[512,128]{1,0:T(8,128)(2,1)S(1)}, bf16[8,256,256]{2,1...) custom-call(s32[1,8]{1,0:T(1,128)} %bitcast.13, s32[1,8]{1,0:T(1,128)} %bitcast.14, ...), custom_call_target="tpu_custom_call" | custom-call | bytes 4718592 | tf_op jit(solution)/shard_map/fetch/pallas_call | solution.py:265
  13.9 0.0 collective-permute-done.refs_4_
  13.9 0.0 collective-permute-done.2.refs_6_
  13.9 0.0 collective-permute-done.6.refs_10_
  14.0 0.0 collective-permute-done.4.refs_8_
  14.0 2.0 %blocks.1 = (f32[448,128]{1,0:T(8,128)S(1)}, bf16[464,128]{1,0:T(8,128)(2,1)S(1)}, bf16[464,128]{1,0:T(8,128)(2,1)S(1)}, bf16[464,128]{1,0:T(8,128)(2,1)S(1)}) custom-call(s32[8,128]{1,0:T(8,128)S(1)} %get-tuple-element.20.refs_0_, f32[8,128]{1,0:T(8,128)S(1)} %get-tuple-element.21.refs_1_, f32[16,128]{1,0:T(8,128)S(1)} %get-tuple-element.19.refs_2_.refs_0_, ...), custom_call_target="tpu_custom_call" | custom-call | tf_op jit(solution)/shard_map/blocks/pallas_call | solution.py:284
  16.0 0.2 collective-permute-start.7
  16.2 2.3 %collective-permute-start.8 = (bf16[464,128]{1,0:T(8,128)(2,1)S(1)}, bf16[464,128]{1,0:T(8,128)(2,1)S(1)}, u32[]{:S(2)}, u32[]{:S(2)}) collective-permute-start(bf16[464,128]{1,0:T(8,128)(2,1)S(1)} %get-tuple-element.28), channel_id=1, source_target_pairs={{0,2},{1,3},{2,0},{3,1},{4,6},{5,7},{6,4},{7,5},{8,10},{9,11},{10,... | collective-permute-start | bytes 356360 | tf_op jit(solution)/shard_map/ppermute | solution.py:21
  18.6 0.2 collective-permute-start.9
  18.7 2.1 %collective-permute-done.7.refs_2_ = bf16[464,128]{1,0:T(8,128)(2,1)S(1)} collective-permute-done((bf16[464,128]{1,0:T(8,128)(2,1)S(1)}, bf16[464,128]{1,0:T(8,128)(2,1)S(1)}, u32[]{:S(2)}, u32[]{:S(2)}) %collective-permute-start.7) | collective-permute-done | bytes 118816 | tf_op jit(solution)/shard_map/ppermute | solution.py:21
  20.9 5.0 %collective-permute-done.8.refs_3_ = bf16[464,128]{1,0:T(8,128)(2,1)S(1)} collective-permute-done((bf16[464,128]{1,0:T(8,128)(2,1)S(1)}, bf16[464,128]{1,0:T(8,128)(2,1)S(1)}, u32[]{:S(2)}, u32[]{:S(2)}) %collective-permute-start.8) | collective-permute-done | bytes 118816 | tf_op jit(solution)/shard_map/ppermute | solution.py:21
  25.9 3.6 %collective-permute-done.9.refs_4_ = bf16[464,128]{1,0:T(8,128)(2,1)S(1)} collective-permute-done((bf16[464,128]{1,0:T(8,128)(2,1)S(1)}, bf16[464,128]{1,0:T(8,128)(2,1)S(1)}, u32[]{:S(2)}, u32[]{:S(2)}) %collective-permute-start.9) | collective-permute-done | bytes 118816 | tf_op jit(solution)/shard_map/ppermute | solution.py:21
  29.5 0.2 sums.1
  29.7 1.1 %collective-permute-start.10 = (bf16[240,128]{1,0:T(8,128)(2,1)S(1)}, bf16[240,128]{1,0:T(8,128)(2,1)S(1)}, u32[]{:S(2)}, u32[]{:S(2)}) collective-permute-start(bf16[240,128]{1,0:T(8,128)(2,1)S(1)} %get-tuple-element.34), channel_id=1, source_target_pairs={{0,4},{4,0},{8,12},{12,8},{16,20},{20,16},{24,28},{28,24},{1,5},{5... | collective-permute-start | bytes 184328 | tf_op jit(solution)/shard_map/ppermute | solution.py:21
  30.8 2.0 %collective-permute-start.11 = (bf16[240,128]{1,0:T(8,128)(2,1)S(1)}, bf16[240,128]{1,0:T(8,128)(2,1)S(1)}, u32[]{:S(2)}, u32[]{:S(2)}) collective-permute-start(bf16[240,128]{1,0:T(8,128)(2,1)S(1)} %get-tuple-element.35), channel_id=1, source_target_pairs={{4,8},{12,16},{20,24},{8,4},{16,12},{24,20},{5,9},{13,17},{21,25},... | collective-permute-start | bytes 184328 | tf_op jit(solution)/shard_map/ppermute | solution.py:328
  32.8 0.8 %uplift.1 = (f32[16,16,128]{2,1,0:T(8,128)}, f32[16,16,128]{2,1,0:T(8,128)S(1)}) custom-call(f32[448,128]{1,0:T(8,128)S(1)} %get-tuple-element.30.total, f32[16,128]{1,0:T(8,128)S(1)} %get-tuple-element.31.depth), custom_call_target="tpu_custom_call" | custom-call | bytes 917504 | tf_op jit(solution)/shard_map/uplift/pallas_call | solution.py:331
  33.7 0.0 collective-permute-done.10.near_edge
  33.7 3.6 %collective-permute-done.11.far_edge = bf16[240,128]{1,0:T(8,128)(2,1)S(1)} collective-permute-done((bf16[240,128]{1,0:T(8,128)(2,1)S(1)}, bf16[240,128]{1,0:T(8,128)(2,1)S(1)}, u32[]{:S(2)}, u32[]{:S(2)}) %collective-permute-start.11) | collective-permute-done | bytes 61472 | tf_op jit(solution)/shard_map/ppermute | solution.py:328
  37.3 1.8 %steps.1 = f32[16,16,128]{2,1,0:T(8,128)} custom-call(f32[448,128]{1,0:T(8,128)S(1)} %get-tuple-element.30.total, f32[16,128]{1,0:T(8,128)S(1)} %get-tuple-element.31.depth, f32[16,16,128]{2,1,0:T(8,128)S(1)} %get-tuple-element.33.wet, bf16[240,128]{1,0:T(8,128)(2,1)S(1)} %collective-permute-done.10.near_edge, ...), custom_call_target="tpu_custom_call" | custom-call | tf_op jit(solution)/shard_map/steps/pallas_call | solution.py:341
Async XLA Ops:
  0.6 4.7 %collective-permute-start.1 = (bf16[512,128]{1,0:T(8,128)(2,1)}, bf16[512,128]{1,0:T(8,128)(2,1)S(1)}, u32[]{:S(2)}, u32[]{:S(2)}) collective-permute-start(bf16[512,128]{1,0:T(8,128)(2,1)} %refs_9_.1), channel_id=1, source_target_pairs={{0,8},{4,12},{8,0},{12,4},{16,24},{20,28},{24,16},{28,20},{1,9},{5... | collective-permute-start | bytes 393224 | tf_op jit(solution)/shard_map/ppermute | solution.py:21
  1.0 8.1 %collective-permute-start.5 = (bf16[512,128]{1,0:T(8,128)(2,1)}, bf16[512,128]{1,0:T(8,128)(2,1)S(1)}, u32[]{:S(2)}, u32[]{:S(2)}) collective-permute-start(bf16[512,128]{1,0:T(8,128)(2,1)} %refs_9_.1), channel_id=1, source_target_pairs={{0,24},{4,28},{8,16},{12,20},{16,8},{20,12},{24,0},{28,4},{1,25},{... | collective-permute-start | bytes 393224 | tf_op jit(solution)/shard_map/ppermute | solution.py:21
  3.1 7.6 %collective-permute-start.3 = (bf16[512,128]{1,0:T(8,128)(2,1)}, bf16[512,128]{1,0:T(8,128)(2,1)S(1)}, u32[]{:S(2)}, u32[]{:S(2)}) collective-permute-start(bf16[512,128]{1,0:T(8,128)(2,1)} %refs_9_.1), channel_id=1, source_target_pairs={{0,16},{4,20},{8,24},{12,28},{16,0},{20,4},{24,8},{28,12},{1,17},{... | collective-permute-start | bytes 393224 | tf_op jit(solution)/shard_map/ppermute | solution.py:21
  3.3 10.6 %collective-permute-start = (bf16[512,128]{1,0:T(8,128)(2,1)}, bf16[512,128]{1,0:T(8,128)(2,1)S(1)}, u32[]{:S(2)}, u32[]{:S(2)}) collective-permute-start(bf16[512,128]{1,0:T(8,128)(2,1)} %refs_9_.1), channel_id=1, source_target_pairs={{0,4},{4,0},{8,12},{12,8},{16,20},{20,16},{24,28},{28,24},{1,5},{5... | collective-permute-start | bytes 393224 | tf_op jit(solution)/shard_map/ppermute | solution.py:21
  5.3 8.6 %collective-permute-start.2 = (bf16[512,128]{1,0:T(8,128)(2,1)S(1)}, bf16[512,128]{1,0:T(8,128)(2,1)S(1)}, u32[]{:S(2)}, u32[]{:S(2)}) collective-permute-start(bf16[512,128]{1,0:T(8,128)(2,1)S(1)} %collective-permute-done.1.refs_5_), channel_id=1, source_target_pairs={{0,4},{4,0},{8,12},{12,8},{16,20},{20,16},{24,28},{28,24},{1,5},{5... | collective-permute-start | bytes 393224 | tf_op jit(solution)/shard_map/ppermute | solution.py:21
  9.1 4.9 %collective-permute-start.6 = (bf16[512,128]{1,0:T(8,128)(2,1)S(1)}, bf16[512,128]{1,0:T(8,128)(2,1)S(1)}, u32[]{:S(2)}, u32[]{:S(2)}) collective-permute-start(bf16[512,128]{1,0:T(8,128)(2,1)S(1)} %collective-permute-done.5.refs_9_), channel_id=1, source_target_pairs={{0,4},{4,0},{8,12},{12,8},{16,20},{20,16},{24,28},{28,24},{1,5},{5... | collective-permute-start | bytes 393224 | tf_op jit(solution)/shard_map/ppermute | solution.py:21
  10.7 3.3 %collective-permute-start.4 = (bf16[512,128]{1,0:T(8,128)(2,1)S(1)}, bf16[512,128]{1,0:T(8,128)(2,1)S(1)}, u32[]{:S(2)}, u32[]{:S(2)}) collective-permute-start(bf16[512,128]{1,0:T(8,128)(2,1)S(1)} %collective-permute-done.3.refs_7_), channel_id=1, source_target_pairs={{0,4},{4,0},{8,12},{12,8},{16,20},{20,16},{24,28},{28,24},{1,5},{5... | collective-permute-start | bytes 393224 | tf_op jit(solution)/shard_map/ppermute | solution.py:21
  16.0 4.9 %collective-permute-start.7 = (bf16[464,128]{1,0:T(8,128)(2,1)S(1)}, bf16[464,128]{1,0:T(8,128)(2,1)S(1)}, u32[]{:S(2)}, u32[]{:S(2)}) collective-permute-start(bf16[464,128]{1,0:T(8,128)(2,1)S(1)} %get-tuple-element.27), channel_id=1, source_target_pairs={{0,1},{1,0},{2,3},{3,2},{4,5},{5,4},{6,7},{7,6},{8,9},{9,8},{10,11... | collective-permute-start | bytes 356360 | tf_op jit(solution)/shard_map/ppermute | solution.py:21
  16.2 9.6 %collective-permute-start.8 = (bf16[464,128]{1,0:T(8,128)(2,1)S(1)}, bf16[464,128]{1,0:T(8,128)(2,1)S(1)}, u32[]{:S(2)}, u32[]{:S(2)}) collective-permute-start(bf16[464,128]{1,0:T(8,128)(2,1)S(1)} %get-tuple-element.28), channel_id=1, source_target_pairs={{0,2},{1,3},{2,0},{3,1},{4,6},{5,7},{6,4},{7,5},{8,10},{9,11},{10,... | collective-permute-start | bytes 356360 | tf_op jit(solution)/shard_map/ppermute | solution.py:21
  18.6 10.9 %collective-permute-start.9 = (bf16[464,128]{1,0:T(8,128)(2,1)S(1)}, bf16[464,128]{1,0:T(8,128)(2,1)S(1)}, u32[]{:S(2)}, u32[]{:S(2)}) collective-permute-start(bf16[464,128]{1,0:T(8,128)(2,1)S(1)} %get-tuple-element.29), channel_id=1, source_target_pairs={{0,3},{1,2},{2,1},{3,0},{4,7},{5,6},{6,5},{7,4},{8,11},{9,10},{10,... | collective-permute-start | bytes 356360 | tf_op jit(solution)/shard_map/ppermute | solution.py:21
  29.7 4.0 %collective-permute-start.10 = (bf16[240,128]{1,0:T(8,128)(2,1)S(1)}, bf16[240,128]{1,0:T(8,128)(2,1)S(1)}, u32[]{:S(2)}, u32[]{:S(2)}) collective-permute-start(bf16[240,128]{1,0:T(8,128)(2,1)S(1)} %get-tuple-element.34), channel_id=1, source_target_pairs={{0,4},{4,0},{8,12},{12,8},{16,20},{20,16},{24,28},{28,24},{1,5},{5... | collective-permute-start | bytes 184328 | tf_op jit(solution)/shard_map/ppermute | solution.py:21
  30.8 6.4 %collective-permute-start.11 = (bf16[240,128]{1,0:T(8,128)(2,1)S(1)}, bf16[240,128]{1,0:T(8,128)(2,1)S(1)}, u32[]{:S(2)}, u32[]{:S(2)}) collective-permute-start(bf16[240,128]{1,0:T(8,128)(2,1)S(1)} %get-tuple-element.35), channel_id=1, source_target_pairs={{4,8},{12,16},{20,24},{8,4},{16,12},{24,20},{5,9},{13,17},{21,25},... | collective-permute-start | bytes 184328 | tf_op jit(solution)/shard_map/ppermute | solution.py:328

commit v4 on v3

--- a/solution.py
+++ b/solution.py
@@ -36,6 +36,22 @@
     d = (t + pltpu.roll(t, lanes - gap, 1)) + pltpu.roll(t, lanes - 2 * gap, 1)
     lane = lax.broadcasted_iota(jnp.int32, t.shape, 1)
     return jnp.where(lane < gap, d, 0.0)
+
+
+def tucked(tile):
+    groups = tile.shape[0] // SUB
+    t = tile.astype(jnp.float32)
+    out = t[0:SUB]
+    for g in range(1, groups):
+        out = out + pltpu.roll(t[g * SUB : (g + 1) * SUB], g * LANES // groups, 1)
+    return out.astype(jnp.bfloat16)
+
+
+def untucked(tile, by, gap):
+    groups = by // SUB
+    t = tile.astype(jnp.float32)
+    turned = [t] + [pltpu.roll(t, LANES - g * LANES // groups, 1) for g in range(1, groups)]
+    return jnp.concatenate([joined(part, gap) for part in turned], axis=0)
 
 
 def fetch_kernel(*refs):
@@ -105,7 +121,7 @@
         acc[pl.ds(target, leaf), :] += scales[1, b] * term
     wide[halo : halo + width] = jnp.swapaxes(acc[...].reshape(by, width, members), 0, 1)
     own[...] = wide[pl.ds(fault * bx, wx)].reshape(wx * by, members)
-    packed = pieces(tile[...], bx)
+    packed = tucked(pieces(tile[...], bx))
     for k in range(1, n_fault):
         part = wide[pl.ds((fault ^ k) * bx, wx)].reshape(wx * by, members)
         outs[k - 1][0 : wx * by] = part.astype(jnp.bfloat16)
@@ -129,7 +145,7 @@
     before = jnp.zeros_like(mid)
     after = jnp.zeros_like(mid)
     for k in range(1, n_fault):
-        other = joined(parts[k - 1][cells:], bx)
+        other = untucked(parts[k - 1][cells:], by, bx)
         source = fault ^ k
         before = before + jnp.where(source == fault - 1, other, 0.0)
         after = after + jnp.where(source == fault + 1, other, 0.0)
@@ -163,7 +179,8 @@
 def steps_kernel(dims, total, depth, wet, near_edge, far_edge, level, column, rows):
     bx, wx, by = dims
     halo = (wx - bx) // 2
-    odd = lax.axis_index("sea") & 1
+    sea = lax.axis_index("sea")
+    odd = sea & 1
     span = by + 2 * SUB
     folds = span // SUB
     edge = wx * SUB
@@ -174,6 +191,8 @@
     post = jnp.where(odd == 1, far, near)
     prev_d = joined(prev[edge:], lanes // 4)[by - SUB :]
     post_d = joined(post[edge:], lanes // 4)[0:SUB]
+    prev_d = jnp.where(sea == 0, 0.0, prev_d)
+    post_d = jnp.where(sea == lax.axis_size("sea") - 1, 0.0, post_d)
     d = jnp.concatenate([prev_d, depth[...], post_d], axis=0)
     scale = gravity_step * height_step
     rows[0] = scale * jnp.minimum(d, pltpu.roll(d, lanes - 1, 1))
@@ -284,7 +303,7 @@
     own, *chunks = pl.pallas_call(
         functools.partial(blocks_kernel, dims),
         out_shape=[jax.ShapeDtypeStruct((cells, members), f32)]
-        + [jax.ShapeDtypeStruct((cells + by, members), bf16)] * (n_fault - 1),
+        + [jax.ShapeDtypeStruct((cells + SUB, members), bf16)] * (n_fault - 1),
         in_specs=[scalar] * 2 + [vector] * (n_sea + 4),
         out_specs=[vector] * n_fault,
         scratch_shapes=[
@@ -324,8 +343,13 @@
         name="sums",
     )(tile, own, *got)
 
-    pairs = [(i, i + 1) for i in range(1, n_sea - 1, 2)]
-    far_edge = lax.ppermute(far_edge, "sea", pairs + [(b, a) for a, b in pairs])
+    ring = []
+    for i in range(n_sea):
+        j = i + 2 * (i & 1) - 1
+        for f in range(n_fault):
+            inside = 0 <= j < n_sea
+            ring.append((i * n_fault + f, j * n_fault + f if inside else i * n_fault + (f ^ 1)))
+    far_edge = lax.ppermute(far_edge, ("sea", "fault"), ring)
     near_edge = swap(near_edge, "sea", 1)
 
     uplift, wet = pl.pallas_call(

time: 39.3 us -> 37.4 us (0.952)
  the two profiles are of different devices: /device:TPU:11 before, /device:TPU:0 now
where the time goes in v4:
time: 37.4 us; the launch traced here: 37.2 us
  waiting for transfers between devices  18.2 us (49%)
  starting transfers between devices  11.4 us (30%)
  Pallas kernels  6.85 us (18%)
  between operations  0.7 us (2%)
    ppermute x11, waiting for transfers between devices, swap(): return lax.ppermute(x, axis, [(i, i ^ k) for i in range(count)])  16.9 us
    ppermute x11, starting transfers between devices, swap(): return lax.ppermute(x, axis, [(i, i ^ k) for i in range(count)])  9.05 us
    ppermute x1, starting transfers between devices, on_device(): far_edge = lax.ppermute(far_edge, ('sea', 'fault'), ring)  2.38 us
    pallas_call x1, Pallas kernels, on_device(): pl.pallas_call(functools.partial(blocks_kernel, dims), out_shape=[jax.Sha...  2.03 us
    pallas_call x1, Pallas kernels, on_device(): pl.pallas_call(fetch_kernel, out_shape=[jax.ShapeDtypeStruct((SUB, LANES)...  1.87 us
    pallas_call x1, Pallas kernels, on_device(): pl.pallas_call(functools.partial(steps_kernel, (bx, wx, by)), out_shape=j...  1.83 us
    ppermute x1, waiting for transfers between devices, on_device(): far_edge = lax.ppermute(far_edge, ('sea', 'fault'), ring)  1.38 us
    pallas_call x1, Pallas kernels, on_device(): pl.pallas_call(functools.partial(uplift_kernel, (bx, wx, by)), out_shape=...  0.82 us
  transfers between devices with their start and end apart: 12, of which 6 were waited for; matrix products, arithmetic and copies ran while one was open for 0% of the time, Pallas kernels for 7%

profile of v4, /device:TPU:0, one launch (start us, length us, event | category | flops | bytes accessed | tf_op | source)
XLA Modules:
  0.0 37.2 jit_solution(4889841867075194493)
XLA Ops:
  0.6 3.0 %collective-permute-start.1 = (bf16[512,128]{1,0:T(8,128)(2,1)}, bf16[512,128]{1,0:T(8,128)(2,1)S(1)}, u32[]{:S(2)}, u32[]{:S(2)}) collective-permute-start(bf16[512,128]{1,0:T(8,128)(2,1)} %refs_9_.1), channel_id=1, source_target_pairs={{0,8},{4,12},{8,0},{12,4},{16,24},{20,28},{24,16},{28,20},{1,9},{5... | collective-permute-start | bytes 393224 | tf_op jit(solution)/shard_map/ppermute | solution.py:21
  3.7 1.5 %collective-permute-start.5 = (bf16[512,128]{1,0:T(8,128)(2,1)}, bf16[512,128]{1,0:T(8,128)(2,1)S(1)}, u32[]{:S(2)}, u32[]{:S(2)}) collective-permute-start(bf16[512,128]{1,0:T(8,128)(2,1)} %refs_9_.1), channel_id=1, source_target_pairs={{0,24},{4,28},{8,16},{12,20},{16,8},{20,12},{24,0},{28,4},{1,25},{... | collective-permute-start | bytes 393224 | tf_op jit(solution)/shard_map/ppermute | solution.py:21
  5.2 0.0 collective-permute-start.3
  5.2 0.0 collective-permute-start
  5.2 2.7 %collective-permute-done.1.refs_5_ = bf16[512,128]{1,0:T(8,128)(2,1)S(1)} collective-permute-done((bf16[512,128]{1,0:T(8,128)(2,1)}, bf16[512,128]{1,0:T(8,128)(2,1)S(1)}, u32[]{:S(2)}, u32[]{:S(2)}) %collective-permute-start.1) | collective-permute-done | bytes 131104 | tf_op jit(solution)/shard_map/ppermute | solution.py:21
  7.9 0.0 collective-permute-start.2
  7.9 3.6 %collective-permute-done.5.refs_9_ = bf16[512,128]{1,0:T(8,128)(2,1)S(1)} collective-permute-done((bf16[512,128]{1,0:T(8,128)(2,1)}, bf16[512,128]{1,0:T(8,128)(2,1)S(1)}, u32[]{:S(2)}, u32[]{:S(2)}) %collective-permute-start.5) | collective-permute-done | bytes 131104 | tf_op jit(solution)/shard_map/ppermute | solution.py:21
  11.5 0.0 collective-permute-start.6
  11.5 1.4 %collective-permute-done.3.refs_7_ = bf16[512,128]{1,0:T(8,128)(2,1)S(1)} collective-permute-done((bf16[512,128]{1,0:T(8,128)(2,1)}, bf16[512,128]{1,0:T(8,128)(2,1)S(1)}, u32[]{:S(2)}, u32[]{:S(2)}) %collective-permute-start.3) | collective-permute-done | bytes 131104 | tf_op jit(solution)/shard_map/ppermute | solution.py:21
  12.9 0.0 collective-permute-start.4
  12.9 1.9 %fetch.1 = (s32[8,128]{1,0:T(8,128)S(1)}, f32[8,128]{1,0:T(8,128)S(1)}, f32[16,128]{1,0:T(8,128)S(1)}, bf16[512,128]{1,0:T(8,128)(2,1)S(1)}, bf16[8,256,256]{2,1...) custom-call(s32[1,8]{1,0:T(1,128)} %bitcast.13, s32[1,8]{1,0:T(1,128)} %bitcast.14, ...), custom_call_target="tpu_custom_call" | custom-call | bytes 4718592 | tf_op jit(solution)/shard_map/fetch/pallas_call | solution.py:284
  14.7 0.0 collective-permute-done.refs_4_
  14.7 0.0 collective-permute-done.2.refs_6_
  14.8 0.0 collective-permute-done.6.refs_10_
  14.8 0.0 collective-permute-done.4.refs_8_
  14.8 2.0 %blocks.1 = (f32[448,128]{1,0:T(8,128)S(1)}, bf16[456,128]{1,0:T(8,128)(2,1)S(1)}, bf16[456,128]{1,0:T(8,128)(2,1)S(1)}, bf16[456,128]{1,0:T(8,128)(2,1)S(1)}) custom-call(s32[8,128]{1,0:T(8,128)S(1)} %get-tuple-element.20.refs_0_, f32[8,128]{1,0:T(8,128)S(1)} %get-tuple-element.21.refs_1_, f32[16,128]{1,0:T(8,128)S(1)} %get-tuple-element.19.refs_2_.refs_0_, ...), custom_call_target="tpu_custom_call" | custom-call | tf_op jit(solution)/shard_map/blocks/pallas_call | solution.py:303
  16.8 1.6 %collective-permute-start.7 = (bf16[456,128]{1,0:T(8,128)(2,1)S(1)}, bf16[456,128]{1,0:T(8,128)(2,1)S(1)}, u32[]{:S(2)}, u32[]{:S(2)}) collective-permute-start(bf16[456,128]{1,0:T(8,128)(2,1)S(1)} %get-tuple-element.27), channel_id=1, source_target_pairs={{0,1},{1,0},{2,3},{3,2},{4,5},{5,4},{6,7},{7,6},{8,9},{9,8},{10,11... | collective-permute-start | bytes 350216 | tf_op jit(solution)/shard_map/ppermute | solution.py:21
  18.5 2.6 %collective-permute-start.8 = (bf16[456,128]{1,0:T(8,128)(2,1)S(1)}, bf16[456,128]{1,0:T(8,128)(2,1)S(1)}, u32[]{:S(2)}, u32[]{:S(2)}) collective-permute-start(bf16[456,128]{1,0:T(8,128)(2,1)S(1)} %get-tuple-element.28), channel_id=1, source_target_pairs={{0,2},{1,3},{2,0},{3,1},{4,6},{5,7},{6,4},{7,5},{8,10},{9,11},{10,... | collective-permute-start | bytes 350216 | tf_op jit(solution)/shard_map/ppermute | solution.py:21
  21.1 0.2 collective-permute-start.9
  21.3 3.1 %collective-permute-done.7.refs_2_ = bf16[456,128]{1,0:T(8,128)(2,1)S(1)} collective-permute-done((bf16[456,128]{1,0:T(8,128)(2,1)S(1)}, bf16[456,128]{1,0:T(8,128)(2,1)S(1)}, u32[]{:S(2)}, u32[]{:S(2)}) %collective-permute-start.7) | collective-permute-done | bytes 116768 | tf_op jit(solution)/shard_map/ppermute | solution.py:21
  24.3 6.1 %collective-permute-done.8.refs_3_ = bf16[456,128]{1,0:T(8,128)(2,1)S(1)} collective-permute-done((bf16[456,128]{1,0:T(8,128)(2,1)S(1)}, bf16[456,128]{1,0:T(8,128)(2,1)S(1)}, u32[]{:S(2)}, u32[]{:S(2)}) %collective-permute-start.8) | collective-permute-done | bytes 116768 | tf_op jit(solution)/shard_map/ppermute | solution.py:21
  30.5 0.0 collective-permute-done.9.refs_4_
  30.5 0.3 sums.1
  30.8 0.0 collective-permute-start.10
  30.8 2.4 %collective-permute-start.11 = (bf16[240,128]{1,0:T(8,128)(2,1)S(1)}, bf16[240,128]{1,0:T(8,128)(2,1)S(1)}, u32[]{:S(2)}, u32[]{:S(2)}) collective-permute-start(bf16[240,128]{1,0:T(8,128)(2,1)S(1)} %get-tuple-element.35), channel_id=1, source_target_pairs={{0,1},{1,0},{2,3},{3,2},{4,8},{5,9},{6,10},{7,11},{8,4},{9,5},{10,... | collective-permute-start | bytes 184328 | tf_op jit(solution)/shard_map/ppermute | solution.py:352
  33.2 0.8 %uplift.1 = (f32[16,16,128]{2,1,0:T(8,128)}, f32[16,16,128]{2,1,0:T(8,128)S(1)}) custom-call(f32[448,128]{1,0:T(8,128)S(1)} %get-tuple-element.30.total, f32[16,128]{1,0:T(8,128)S(1)} %get-tuple-element.31.depth), custom_call_target="tpu_custom_call" | custom-call | bytes 917504 | tf_op jit(solution)/shard_map/uplift/pallas_call | solution.py:355
  34.0 0.0 collective-permute-done.10.near_edge
  34.0 1.4 %collective-permute-done.11.far_edge = bf16[240,128]{1,0:T(8,128)(2,1)S(1)} collective-permute-done((bf16[240,128]{1,0:T(8,128)(2,1)S(1)}, bf16[240,128]{1,0:T(8,128)(2,1)S(1)}, u32[]{:S(2)}, u32[]{:S(2)}) %collective-permute-start.11) | collective-permute-done | bytes 61472 | tf_op jit(solution)/shard_map/ppermute | solution.py:352
  35.4 1.8 %steps.1 = f32[16,16,128]{2,1,0:T(8,128)} custom-call(f32[448,128]{1,0:T(8,128)S(1)} %get-tuple-element.30.total, f32[16,128]{1,0:T(8,128)S(1)} %get-tuple-element.31.depth, f32[16,16,128]{2,1,0:T(8,128)S(1)} %get-tuple-element.33.wet, bf16[240,128]{1,0:T(8,128)(2,1)S(1)} %collective-permute-done.10.near_edge, ...), custom_call_target="tpu_custom_call" | custom-call | tf_op jit(solution)/shard_map/steps/pallas_call | solution.py:365
Async XLA Ops:
  0.6 7.2 %collective-permute-start.1 = (bf16[512,128]{1,0:T(8,128)(2,1)}, bf16[512,128]{1,0:T(8,128)(2,1)S(1)}, u32[]{:S(2)}, u32[]{:S(2)}) collective-permute-start(bf16[512,128]{1,0:T(8,128)(2,1)} %refs_9_.1), channel_id=1, source_target_pairs={{0,8},{4,12},{8,0},{12,4},{16,24},{20,28},{24,16},{28,20},{1,9},{5... | collective-permute-start | bytes 393224 | tf_op jit(solution)/shard_map/ppermute | solution.py:21
  3.7 7.8 %collective-permute-start.5 = (bf16[512,128]{1,0:T(8,128)(2,1)}, bf16[512,128]{1,0:T(8,128)(2,1)S(1)}, u32[]{:S(2)}, u32[]{:S(2)}) collective-permute-start(bf16[512,128]{1,0:T(8,128)(2,1)} %refs_9_.1), channel_id=1, source_target_pairs={{0,24},{4,28},{8,16},{12,20},{16,8},{20,12},{24,0},{28,4},{1,25},{... | collective-permute-start | bytes 393224 | tf_op jit(solution)/shard_map/ppermute | solution.py:21
  5.2 7.7 %collective-permute-start.3 = (bf16[512,128]{1,0:T(8,128)(2,1)}, bf16[512,128]{1,0:T(8,128)(2,1)S(1)}, u32[]{:S(2)}, u32[]{:S(2)}) collective-permute-start(bf16[512,128]{1,0:T(8,128)(2,1)} %refs_9_.1), channel_id=1, source_target_pairs={{0,16},{4,20},{8,24},{12,28},{16,0},{20,4},{24,8},{28,12},{1,17},{... | collective-permute-start | bytes 393224 | tf_op jit(solution)/shard_map/ppermute | solution.py:21
  5.2 9.5 %collective-permute-start = (bf16[512,128]{1,0:T(8,128)(2,1)}, bf16[512,128]{1,0:T(8,128)(2,1)S(1)}, u32[]{:S(2)}, u32[]{:S(2)}) collective-permute-start(bf16[512,128]{1,0:T(8,128)(2,1)} %refs_9_.1), channel_id=1, source_target_pairs={{0,4},{4,0},{8,12},{12,8},{16,20},{20,16},{24,28},{28,24},{1,5},{5... | collective-permute-start | bytes 393224 | tf_op jit(solution)/shard_map/ppermute | solution.py:21
  7.9 6.9 %collective-permute-start.2 = (bf16[512,128]{1,0:T(8,128)(2,1)S(1)}, bf16[512,128]{1,0:T(8,128)(2,1)S(1)}, u32[]{:S(2)}, u32[]{:S(2)}) collective-permute-start(bf16[512,128]{1,0:T(8,128)(2,1)S(1)} %collective-permute-done.1.refs_5_), channel_id=1, source_target_pairs={{0,4},{4,0},{8,12},{12,8},{16,20},{20,16},{24,28},{28,24},{1,5},{5... | collective-permute-start | bytes 393224 | tf_op jit(solution)/shard_map/ppermute | solution.py:21
  11.5 3.3 %collective-permute-start.6 = (bf16[512,128]{1,0:T(8,128)(2,1)S(1)}, bf16[512,128]{1,0:T(8,128)(2,1)S(1)}, u32[]{:S(2)}, u32[]{:S(2)}) collective-permute-start(bf16[512,128]{1,0:T(8,128)(2,1)S(1)} %collective-permute-done.5.refs_9_), channel_id=1, source_target_pairs={{0,4},{4,0},{8,12},{12,8},{16,20},{20,16},{24,28},{28,24},{1,5},{5... | collective-permute-start | bytes 393224 | tf_op jit(solution)/shard_map/ppermute | solution.py:21
  12.9 1.9 %collective-permute-start.4 = (bf16[512,128]{1,0:T(8,128)(2,1)S(1)}, bf16[512,128]{1,0:T(8,128)(2,1)S(1)}, u32[]{:S(2)}, u32[]{:S(2)}) collective-permute-start(bf16[512,128]{1,0:T(8,128)(2,1)S(1)} %collective-permute-done.3.refs_7_), channel_id=1, source_target_pairs={{0,4},{4,0},{8,12},{12,8},{16,20},{20,16},{24,28},{28,24},{1,5},{5... | collective-permute-start | bytes 393224 | tf_op jit(solution)/shard_map/ppermute | solution.py:21
  16.8 7.5 %collective-permute-start.7 = (bf16[456,128]{1,0:T(8,128)(2,1)S(1)}, bf16[456,128]{1,0:T(8,128)(2,1)S(1)}, u32[]{:S(2)}, u32[]{:S(2)}) collective-permute-start(bf16[456,128]{1,0:T(8,128)(2,1)S(1)} %get-tuple-element.27), channel_id=1, source_target_pairs={{0,1},{1,0},{2,3},{3,2},{4,5},{5,4},{6,7},{7,6},{8,9},{9,8},{10,11... | collective-permute-start | bytes 350216 | tf_op jit(solution)/shard_map/ppermute | solution.py:21
  18.5 12.0 %collective-permute-start.8 = (bf16[456,128]{1,0:T(8,128)(2,1)S(1)}, bf16[456,128]{1,0:T(8,128)(2,1)S(1)}, u32[]{:S(2)}, u32[]{:S(2)}) collective-permute-start(bf16[456,128]{1,0:T(8,128)(2,1)S(1)} %get-tuple-element.28), channel_id=1, source_target_pairs={{0,2},{1,3},{2,0},{3,1},{4,6},{5,7},{6,4},{7,5},{8,10},{9,11},{10,... | collective-permute-start | bytes 350216 | tf_op jit(solution)/shard_map/ppermute | solution.py:21
  21.1 9.4 %collective-permute-start.9 = (bf16[456,128]{1,0:T(8,128)(2,1)S(1)}, bf16[456,128]{1,0:T(8,128)(2,1)S(1)}, u32[]{:S(2)}, u32[]{:S(2)}) collective-permute-start(bf16[456,128]{1,0:T(8,128)(2,1)S(1)} %get-tuple-element.29), channel_id=1, source_target_pairs={{0,3},{1,2},{2,1},{3,0},{4,7},{5,6},{6,5},{7,4},{8,11},{9,10},{10,... | collective-permute-start | bytes 350216 | tf_op jit(solution)/shard_map/ppermute | solution.py:21
  30.8 3.2 %collective-permute-start.10 = (bf16[240,128]{1,0:T(8,128)(2,1)S(1)}, bf16[240,128]{1,0:T(8,128)(2,1)S(1)}, u32[]{:S(2)}, u32[]{:S(2)}) collective-permute-start(bf16[240,128]{1,0:T(8,128)(2,1)S(1)} %get-tuple-element.34), channel_id=1, source_target_pairs={{0,4},{4,0},{8,12},{12,8},{16,20},{20,16},{24,28},{28,24},{1,5},{5... | collective-permute-start | bytes 184328 | tf_op jit(solution)/shard_map/ppermute | solution.py:21
  30.8 4.6 %collective-permute-start.11 = (bf16[240,128]{1,0:T(8,128)(2,1)S(1)}, bf16[240,128]{1,0:T(8,128)(2,1)S(1)}, u32[]{:S(2)}, u32[]{:S(2)}) collective-permute-start(bf16[240,128]{1,0:T(8,128)(2,1)S(1)} %get-tuple-element.35), channel_id=1, source_target_pairs={{0,1},{1,0},{2,3},{3,2},{4,8},{5,9},{6,10},{7,11},{8,4},{9,5},{10,... | collective-permute-start | bytes 184328 | tf_op jit(solution)/shard_map/ppermute | solution.py:352

commit v5 on v4

--- a/solution.py
+++ b/solution.py
@@ -85,7 +85,8 @@
     slots = refs[:n_sea]
     near, left, right, own = refs[n_sea : 4 + n_sea]
     outs = refs[4 + n_sea : 3 + n_sea + n_fault]
-    slip, coeffs, acc, wide = refs[3 + n_sea + n_fault :]
+    rims = refs[3 + n_sea + n_fault : 2 + n_sea + 2 * n_fault]
+    slip, coeffs, acc, wide = refs[2 + n_sea + 2 * n_fault :]
     sea = lax.axis_index("sea")
     fault = lax.axis_index("fault")
     members = slip.shape[1]
@@ -122,30 +123,45 @@
     wide[halo : halo + width] = jnp.swapaxes(acc[...].reshape(by, width, members), 0, 1)
     own[...] = wide[pl.ds(fault * bx, wx)].reshape(wx * by, members)
     packed = tucked(pieces(tile[...], bx))
+    reach = bx + halo
     for k in range(1, n_fault):
-        part = wide[pl.ds((fault ^ k) * bx, wx)].reshape(wx * by, members)
-        outs[k - 1][0 : wx * by] = part.astype(jnp.bfloat16)
-        outs[k - 1][wx * by :] = packed
+        target = fault ^ k
+        start = target * bx
+        base = start + jnp.where(target == 0, halo, 0)
+        part = wide[pl.ds(base, reach)].reshape(reach * by, members)
+        outs[k - 1][0 : reach * by] = part.astype(jnp.bfloat16)
+        outs[k - 1][reach * by :] = packed
+        part = wide[pl.ds(start + reach, halo)].reshape(halo * by, members)
+        rims[k - 1][...] = part.astype(jnp.bfloat16)
 
 
 def sum_kernel(dims, *refs):
     n_fault, bx, wx, by = dims
     tile, own = refs[:2]
     parts = refs[2 : 1 + n_fault]
-    total, depth, near_edge, far_edge = refs[1 + n_fault :]
+    rims = refs[1 + n_fault : 2 * n_fault]
+    total, depth, near_edge, far_edge = refs[2 * n_fault :]
     sea = lax.axis_index("sea")
     fault = lax.axis_index("fault")
     halo = (wx - bx) // 2
-    cells = wx * by
-    s = own[...]
-    for part in parts:
-        s = s + part[0:cells].astype(jnp.float32)
+    reach = (bx + halo) * by
+    main = parts[0][0:reach].astype(jnp.float32)
+    for part in parts[1:]:
+        main = main + part[0:reach].astype(jnp.float32)
+    side = rims[0][...].astype(jnp.float32)
+    for rim in rims[1:]:
+        side = side + rim[...].astype(jnp.float32)
+    zero = jnp.zeros_like(side)
+    side = jnp.where(fault == n_fault - 1, zero, side)
+    inner = jnp.concatenate([main, side], axis=0)
+    first = jnp.concatenate([zero, main], axis=0)
+    s = own[...] + jnp.where(fault == 0, first, inner)
     total[...] = s
     mid = tile[...]
     before = jnp.zeros_like(mid)
     after = jnp.zeros_like(mid)
     for k in range(1, n_fault):
-        other = untucked(parts[k - 1][cells:], by, bx)
+        other = untucked(parts[k - 1][reach:], by, bx)
         source = fault ^ k
         before = before + jnp.where(source == fault - 1, other, 0.0)
         after = after + jnp.where(source == fault + 1, other, 0.0)
@@ -303,9 +319,10 @@
     own, *chunks = pl.pallas_call(
         functools.partial(blocks_kernel, dims),
         out_shape=[jax.ShapeDtypeStruct((cells, members), f32)]
-        + [jax.ShapeDtypeStruct((cells + SUB, members), bf16)] * (n_fault - 1),
+        + [jax.ShapeDtypeStruct(((bx + STEPS) * by + SUB, members), bf16)] * (n_fault - 1)
+        + [jax.ShapeDtypeStruct((STEPS * by, members), bf16)] * (n_fault - 1),
         in_specs=[scalar] * 2 + [vector] * (n_sea + 4),
-        out_specs=[vector] * n_fault,
+        out_specs=[vector] * (2 * n_fault - 1),
         scratch_shapes=[
             pltpu.VMEM((n_sea * rows, members), bf16),
             pltpu.VMEM((n_far, rank, members), bf16),
@@ -327,6 +344,18 @@
     got = []
     for k in range(1, n_fault):
         got.append(swap(chunks[k - 1], "fault", k))
+    last = n_fault - 1
+    for k in range(1, n_fault):
+        hops = []
+        for i in range(n_sea):
+            for f in range(n_fault):
+                j, g = i, f ^ k
+                if g in (0, last) and k == last:
+                    j, g = i ^ 1, f
+                elif g in (0, last) and last < 2 * k:
+                    g = last - g
+                hops.append((i * n_fault + f, j * n_fault + g))
+        got.append(lax.ppermute(chunks[last + k - 1], ("sea", "fault"), hops))
 
     edge = jax.ShapeDtypeStruct((wx * SUB + by, members), bf16)
     total, depth, near_edge, far_edge = pl.pallas_call(
@@ -337,7 +366,7 @@
             edge,
             edge,
         ],
-        in_specs=[vector] * (1 + n_fault),
+        in_specs=[vector] * (2 * n_fault),
         out_specs=[vector] * 4,
         compiler_params=pltpu.CompilerParams(vmem_limit_bytes=8 << 20),
         name="sums",

time: 37.4 us -> 37.1 us (level)
  waiting for transfers between devices: 18.2 us -> 12.9 us
  starting transfers between devices: 11.4 us -> 16.5 us
    ppermute x11, waiting for transfers between devices: 16.9 us -> 9.57 us  [swap(): return lax.ppermute(x, axis, [(i, i ^ k) for i in range(count)])]
    ppermute x0 -> x3, starting transfers between devices: none -> 4.18 us  [on_device(): got.append(lax.ppermute(chunks[last + k - 1], ('sea', 'fault'), hops))]
    ppermute x0 -> x3, waiting for transfers between devices: none -> 1.93 us  [on_device(): got.append(lax.ppermute(chunks[last + k - 1], ('sea', 'fault'), hops))]
    ppermute x1, starting transfers between devices: 2.38 us -> 3.27 us  [on_device(): far_edge = lax.ppermute(far_edge, ('sea', 'fault'), ring)]
  transfers between devices with their start and end apart: 12 -> 15, of which waited for: 6 -> 8; matrix products, arithmetic and copies ran while one was open for 0% -> 0% of each run, Pallas kernels for 7% -> 7%
where the time goes in v5:
time: 37.1 us; the launch traced here: 36.9 us
  starting transfers between devices  16.5 us (44%)
  waiting for transfers between devices  12.9 us (35%)
  Pallas kernels  6.86 us (18%)
  between operations  0.7 us (2%)
    ppermute x11, waiting for transfers between devices, swap(): return lax.ppermute(x, axis, [(i, i ^ k) for i in range(count)])  9.57 us
    ppermute x11, starting transfers between devices, swap(): return lax.ppermute(x, axis, [(i, i ^ k) for i in range(count)])  9.04 us
    ppermute x3, starting transfers between devices, on_device(): got.append(lax.ppermute(chunks[last + k - 1], ('sea', 'fault'), hops))  4.18 us
    ppermute x1, starting transfers between devices, on_device(): far_edge = lax.ppermute(far_edge, ('sea', 'fault'), ring)  3.27 us
    pallas_call x1, Pallas kernels, on_device(): pl.pallas_call(functools.partial(blocks_kernel, dims), out_shape=[jax.Sha...  2.04 us
    ppermute x3, waiting for transfers between devices, on_device(): got.append(lax.ppermute(chunks[last + k - 1], ('sea', 'fault'), hops))  1.93 us
    pallas_call x1, Pallas kernels, on_device(): pl.pallas_call(fetch_kernel, out_shape=[jax.ShapeDtypeStruct((SUB, LANES)...  1.87 us
    pallas_call x1, Pallas kernels, on_device(): pl.pallas_call(functools.partial(steps_kernel, (bx, wx, by)), out_shape=j...  1.83 us
  transfers between devices with their start and end apart: 15, of which 8 were waited for; matrix products, arithmetic and copies ran while one was open for 0% of the time, Pallas kernels for 7%

profile of v5, /device:TPU:0, one launch (start us, length us, event | category | flops | bytes accessed | tf_op | source)
XLA Modules:
  0.0 36.9 jit_solution(12504467664258599038)
XLA Ops:
  0.6 3.0 %collective-permute-start.1 = (bf16[512,128]{1,0:T(8,128)(2,1)}, bf16[512,128]{1,0:T(8,128)(2,1)S(1)}, u32[]{:S(2)}, u32[]{:S(2)}) collective-permute-start(bf16[512,128]{1,0:T(8,128)(2,1)} %refs_9_.1), channel_id=1, source_target_pairs={{0,8},{4,12},{8,0},{12,4},{16,24},{20,28},{24,16},{28,20},{1,9},{5... | collective-permute-start | bytes 393224 | tf_op jit(solution)/shard_map/ppermute | solution.py:21
  3.7 1.5 %collective-permute-start.5 = (bf16[512,128]{1,0:T(8,128)(2,1)}, bf16[512,128]{1,0:T(8,128)(2,1)S(1)}, u32[]{:S(2)}, u32[]{:S(2)}) collective-permute-start(bf16[512,128]{1,0:T(8,128)(2,1)} %refs_9_.1), channel_id=1, source_target_pairs={{0,24},{4,28},{8,16},{12,20},{16,8},{20,12},{24,0},{28,4},{1,25},{... | collective-permute-start | bytes 393224 | tf_op jit(solution)/shard_map/ppermute | solution.py:21
  5.2 0.0 collective-permute-start.3
  5.2 0.0 collective-permute-start
  5.2 2.7 %collective-permute-done.1.refs_5_ = bf16[512,128]{1,0:T(8,128)(2,1)S(1)} collective-permute-done((bf16[512,128]{1,0:T(8,128)(2,1)}, bf16[512,128]{1,0:T(8,128)(2,1)S(1)}, u32[]{:S(2)}, u32[]{:S(2)}) %collective-permute-start.1) | collective-permute-done | bytes 131104 | tf_op jit(solution)/shard_map/ppermute | solution.py:21
  7.9 0.0 collective-permute-start.2
  7.9 3.6 %collective-permute-done.5.refs_9_ = bf16[512,128]{1,0:T(8,128)(2,1)S(1)} collective-permute-done((bf16[512,128]{1,0:T(8,128)(2,1)}, bf16[512,128]{1,0:T(8,128)(2,1)S(1)}, u32[]{:S(2)}, u32[]{:S(2)}) %collective-permute-start.5) | collective-permute-done | bytes 131104 | tf_op jit(solution)/shard_map/ppermute | solution.py:21
  11.5 0.0 collective-permute-start.6
  11.5 1.4 %collective-permute-done.3.refs_7_ = bf16[512,128]{1,0:T(8,128)(2,1)S(1)} collective-permute-done((bf16[512,128]{1,0:T(8,128)(2,1)}, bf16[512,128]{1,0:T(8,128)(2,1)S(1)}, u32[]{:S(2)}, u32[]{:S(2)}) %collective-permute-start.3) | collective-permute-done | bytes 131104 | tf_op jit(solution)/shard_map/ppermute | solution.py:21
  12.9 0.0 collective-permute-start.4
  12.9 1.9 %fetch.1 = (s32[8,128]{1,0:T(8,128)S(1)}, f32[8,128]{1,0:T(8,128)S(1)}, f32[16,128]{1,0:T(8,128)S(1)}, bf16[512,128]{1,0:T(8,128)(2,1)S(1)}, bf16[8,256,256]{2,1...) custom-call(s32[1,8]{1,0:T(1,128)} %bitcast.13, s32[1,8]{1,0:T(1,128)} %bitcast.14, ...), custom_call_target="tpu_custom_call" | custom-call | bytes 4718592 | tf_op jit(solution)/shard_map/fetch/pallas_call | solution.py:300
  14.7 0.0 collective-permute-done.refs_4_
  14.7 0.0 collective-permute-done.2.refs_6_
  14.8 0.0 collective-permute-done.6.refs_10_
  14.8 0.0 collective-permute-done.4.refs_8_
  14.8 2.0 %blocks.1 = (f32[448,128]{1,0:T(8,128)S(1)}, bf16[360,128]{1,0:T(8,128)(2,1)S(1)}, bf16[360,128]{1,0:T(8,128)(2,1)S(1)}, bf16[360,128]{1,0:T(8,128)(2,1)S(1)}, b...) custom-call(s32[8,128]{1,0:T(8,128)S(1)} %get-tuple-element.23.refs_0_, ...), custom_call_target="tpu_custom_call" | custom-call | tf_op jit(solution)/shard_map/blocks/pallas_call | solution.py:319
  16.8 1.6 %collective-permute-start.7 = (bf16[360,128]{1,0:T(8,128)(2,1)S(1)}, bf16[360,128]{1,0:T(8,128)(2,1)S(1)}, u32[]{:S(2)}, u32[]{:S(2)}) collective-permute-start(bf16[360,128]{1,0:T(8,128)(2,1)S(1)} %get-tuple-element.30), channel_id=1, source_target_pairs={{0,1},{1,0},{2,3},{3,2},{4,5},{5,4},{6,7},{7,6},{8,9},{9,8},{10,11... | collective-permute-start | bytes 276488 | tf_op jit(solution)/shard_map/ppermute | solution.py:21
  18.5 2.6 %collective-permute-start.8 = (bf16[360,128]{1,0:T(8,128)(2,1)S(1)}, bf16[360,128]{1,0:T(8,128)(2,1)S(1)}, u32[]{:S(2)}, u32[]{:S(2)}) collective-permute-start(bf16[360,128]{1,0:T(8,128)(2,1)S(1)} %get-tuple-element.31), channel_id=1, source_target_pairs={{0,2},{1,3},{2,0},{3,1},{4,6},{5,7},{6,4},{7,5},{8,10},{9,11},{10,... | collective-permute-start | bytes 276488 | tf_op jit(solution)/shard_map/ppermute | solution.py:21
  21.1 0.2 collective-permute-start.9
  21.3 0.7 %collective-permute-start.10 = (bf16[96,128]{1,0:T(8,128)(2,1)S(1)}, bf16[96,128]{1,0:T(8,128)(2,1)S(1)}, u32[]{:S(2)}, u32[]{:S(2)}) collective-permute-start(bf16[96,128]{1,0:T(8,128)(2,1)S(1)} %get-tuple-element.33), channel_id=1, source_target_pairs={{0,1},{1,0},{2,3},{3,2},{4,5},{5,4},{6,7},{7,6},{8,9},{9,8},{10,11... | collective-permute-start | bytes 73736 | tf_op jit(solution)/shard_map/ppermute | solution.py:358
  22.0 3.5 %collective-permute-start.11 = (bf16[96,128]{1,0:T(8,128)(2,1)S(1)}, bf16[96,128]{1,0:T(8,128)(2,1)S(1)}, u32[]{:S(2)}, u32[]{:S(2)}) collective-permute-start(bf16[96,128]{1,0:T(8,128)(2,1)S(1)} %get-tuple-element.34), channel_id=1, source_target_pairs={{0,2},{1,0},{2,3},{3,1},{4,6},{5,4},{6,7},{7,5},{8,10},{9,8},{10,1... | collective-permute-start | bytes 73736 | tf_op jit(solution)/shard_map/ppermute | solution.py:358
  25.5 0.7 %collective-permute-done.10.refs_5_ = bf16[96,128]{1,0:T(8,128)(2,1)S(1)} collective-permute-done((bf16[96,128]{1,0:T(8,128)(2,1)S(1)}, bf16[96,128]{1,0:T(8,128)(2,1)S(1)}, u32[]{:S(2)}, u32[]{:S(2)}) %collective-permute-start.10) | collective-permute-done | bytes 24608 | tf_op jit(solution)/shard_map/ppermute | solution.py:358
  26.2 0.0 collective-permute-start.12
  26.2 0.8 %collective-permute-done.11.refs_6_ = bf16[96,128]{1,0:T(8,128)(2,1)S(1)} collective-permute-done((bf16[96,128]{1,0:T(8,128)(2,1)S(1)}, bf16[96,128]{1,0:T(8,128)(2,1)S(1)}, u32[]{:S(2)}, u32[]{:S(2)}) %collective-permute-start.11) | collective-permute-done | bytes 24608 | tf_op jit(solution)/shard_map/ppermute | solution.py:358
  27.0 0.4 %collective-permute-done.12.refs_7_ = bf16[96,128]{1,0:T(8,128)(2,1)S(1)} collective-permute-done((bf16[96,128]{1,0:T(8,128)(2,1)S(1)}, bf16[96,128]{1,0:T(8,128)(2,1)S(1)}, u32[]{:S(2)}, u32[]{:S(2)}) %collective-permute-start.12) | collective-permute-done | bytes 24608 | tf_op jit(solution)/shard_map/ppermute | solution.py:358
  27.4 0.0 collective-permute-done.7.refs_2_
  27.4 1.9 %collective-permute-done.8.refs_3_ = bf16[360,128]{1,0:T(8,128)(2,1)S(1)} collective-permute-done((bf16[360,128]{1,0:T(8,128)(2,1)S(1)}, bf16[360,128]{1,0:T(8,128)(2,1)S(1)}, u32[]{:S(2)}, u32[]{:S(2)}) %collective-permute-start.8) | collective-permute-done | bytes 92192 | tf_op jit(solution)/shard_map/ppermute | solution.py:21
  29.3 0.0 collective-permute-done.9.refs_4_
  29.3 0.3 sums.1
  29.6 0.0 collective-permute-start.13
  29.6 3.3 %collective-permute-start.14 = (bf16[240,128]{1,0:T(8,128)(2,1)S(1)}, bf16[240,128]{1,0:T(8,128)(2,1)S(1)}, u32[]{:S(2)}, u32[]{:S(2)}) collective-permute-start(bf16[240,128]{1,0:T(8,128)(2,1)S(1)} %get-tuple-element.41), channel_id=1, source_target_pairs={{0,1},{1,0},{2,3},{3,2},{4,8},{5,9},{6,10},{7,11},{8,4},{9,5},{10,... | collective-permute-start | bytes 184328 | tf_op jit(solution)/shard_map/ppermute | solution.py:381
  32.9 0.8 %uplift.1 = (f32[16,16,128]{2,1,0:T(8,128)}, f32[16,16,128]{2,1,0:T(8,128)S(1)}) custom-call(f32[448,128]{1,0:T(8,128)S(1)} %get-tuple-element.36.total, f32[16,128]{1,0:T(8,128)S(1)} %get-tuple-element.37.depth), custom_call_target="tpu_custom_call" | custom-call | bytes 917504 | tf_op jit(solution)/shard_map/uplift/pallas_call | solution.py:384
  33.7 0.0 collective-permute-done.13.near_edge
  33.7 1.4 %collective-permute-done.14.far_edge = bf16[240,128]{1,0:T(8,128)(2,1)S(1)} collective-permute-done((bf16[240,128]{1,0:T(8,128)(2,1)S(1)}, bf16[240,128]{1,0:T(8,128)(2,1)S(1)}, u32[]{:S(2)}, u32[]{:S(2)}) %collective-permute-start.14) | collective-permute-done | bytes 61472 | tf_op jit(solution)/shard_map/ppermute | solution.py:381
  35.1 1.8 %steps.1 = f32[16,16,128]{2,1,0:T(8,128)} custom-call(f32[448,128]{1,0:T(8,128)S(1)} %get-tuple-element.36.total, f32[16,128]{1,0:T(8,128)S(1)} %get-tuple-element.37.depth, f32[16,16,128]{2,1,0:T(8,128)S(1)} %get-tuple-element.39.wet, bf16[240,128]{1,0:T(8,128)(2,1)S(1)} %collective-permute-done.13.near_edge, ...), custom_call_target="tpu_custom_call" | custom-call | tf_op jit(solution)/shard_map/steps/pallas_call | solution.py:394
Async XLA Ops:
  0.6 7.2 %collective-permute-start.1 = (bf16[512,128]{1,0:T(8,128)(2,1)}, bf16[512,128]{1,0:T(8,128)(2,1)S(1)}, u32[]{:S(2)}, u32[]{:S(2)}) collective-permute-start(bf16[512,128]{1,0:T(8,128)(2,1)} %refs_9_.1), channel_id=1, source_target_pairs={{0,8},{4,12},{8,0},{12,4},{16,24},{20,28},{24,16},{28,20},{1,9},{5... | collective-permute-start | bytes 393224 | tf_op jit(solution)/shard_map/ppermute | solution.py:21
  3.7 7.8 %collective-permute-start.5 = (bf16[512,128]{1,0:T(8,128)(2,1)}, bf16[512,128]{1,0:T(8,128)(2,1)S(1)}, u32[]{:S(2)}, u32[]{:S(2)}) collective-permute-start(bf16[512,128]{1,0:T(8,128)(2,1)} %refs_9_.1), channel_id=1, source_target_pairs={{0,24},{4,28},{8,16},{12,20},{16,8},{20,12},{24,0},{28,4},{1,25},{... | collective-permute-start | bytes 393224 | tf_op jit(solution)/shard_map/ppermute | solution.py:21
  5.2 7.7 %collective-permute-start.3 = (bf16[512,128]{1,0:T(8,128)(2,1)}, bf16[512,128]{1,0:T(8,128)(2,1)S(1)}, u32[]{:S(2)}, u32[]{:S(2)}) collective-permute-start(bf16[512,128]{1,0:T(8,128)(2,1)} %refs_9_.1), channel_id=1, source_target_pairs={{0,16},{4,20},{8,24},{12,28},{16,0},{20,4},{24,8},{28,12},{1,17},{... | collective-permute-start | bytes 393224 | tf_op jit(solution)/shard_map/ppermute | solution.py:21
  5.2 9.5 %collective-permute-start = (bf16[512,128]{1,0:T(8,128)(2,1)}, bf16[512,128]{1,0:T(8,128)(2,1)S(1)}, u32[]{:S(2)}, u32[]{:S(2)}) collective-permute-start(bf16[512,128]{1,0:T(8,128)(2,1)} %refs_9_.1), channel_id=1, source_target_pairs={{0,4},{4,0},{8,12},{12,8},{16,20},{20,16},{24,28},{28,24},{1,5},{5... | collective-permute-start | bytes 393224 | tf_op jit(solution)/shard_map/ppermute | solution.py:21
  7.9 6.9 %collective-permute-start.2 = (bf16[512,128]{1,0:T(8,128)(2,1)S(1)}, bf16[512,128]{1,0:T(8,128)(2,1)S(1)}, u32[]{:S(2)}, u32[]{:S(2)}) collective-permute-start(bf16[512,128]{1,0:T(8,128)(2,1)S(1)} %collective-permute-done.1.refs_5_), channel_id=1, source_target_pairs={{0,4},{4,0},{8,12},{12,8},{16,20},{20,16},{24,28},{28,24},{1,5},{5... | collective-permute-start | bytes 393224 | tf_op jit(solution)/shard_map/ppermute | solution.py:21
  11.5 3.3 %collective-permute-start.6 = (bf16[512,128]{1,0:T(8,128)(2,1)S(1)}, bf16[512,128]{1,0:T(8,128)(2,1)S(1)}, u32[]{:S(2)}, u32[]{:S(2)}) collective-permute-start(bf16[512,128]{1,0:T(8,128)(2,1)S(1)} %collective-permute-done.5.refs_9_), channel_id=1, source_target_pairs={{0,4},{4,0},{8,12},{12,8},{16,20},{20,16},{24,28},{28,24},{1,5},{5... | collective-permute-start | bytes 393224 | tf_op jit(solution)/shard_map/ppermute | solution.py:21
  12.9 1.9 %collective-permute-start.4 = (bf16[512,128]{1,0:T(8,128)(2,1)S(1)}, bf16[512,128]{1,0:T(8,128)(2,1)S(1)}, u32[]{:S(2)}, u32[]{:S(2)}) collective-permute-start(bf16[512,128]{1,0:T(8,128)(2,1)S(1)} %collective-permute-done.3.refs_7_), channel_id=1, source_target_pairs={{0,4},{4,0},{8,12},{12,8},{16,20},{20,16},{24,28},{28,24},{1,5},{5... | collective-permute-start | bytes 393224 | tf_op jit(solution)/shard_map/ppermute | solution.py:21
  16.8 10.6 %collective-permute-start.7 = (bf16[360,128]{1,0:T(8,128)(2,1)S(1)}, bf16[360,128]{1,0:T(8,128)(2,1)S(1)}, u32[]{:S(2)}, u32[]{:S(2)}) collective-permute-start(bf16[360,128]{1,0:T(8,128)(2,1)S(1)} %get-tuple-element.30), channel_id=1, source_target_pairs={{0,1},{1,0},{2,3},{3,2},{4,5},{5,4},{6,7},{7,6},{8,9},{9,8},{10,11... | collective-permute-start | bytes 276488 | tf_op jit(solution)/shard_map/ppermute | solution.py:21
  18.5 10.8 %collective-permute-start.8 = (bf16[360,128]{1,0:T(8,128)(2,1)S(1)}, bf16[360,128]{1,0:T(8,128)(2,1)S(1)}, u32[]{:S(2)}, u32[]{:S(2)}) collective-permute-start(bf16[360,128]{1,0:T(8,128)(2,1)S(1)} %get-tuple-element.31), channel_id=1, source_target_pairs={{0,2},{1,3},{2,0},{3,1},{4,6},{5,7},{6,4},{7,5},{8,10},{9,11},{10,... | collective-permute-start | bytes 276488 | tf_op jit(solution)/shard_map/ppermute | solution.py:21
  21.1 8.2 %collective-permute-start.9 = (bf16[360,128]{1,0:T(8,128)(2,1)S(1)}, bf16[360,128]{1,0:T(8,128)(2,1)S(1)}, u32[]{:S(2)}, u32[]{:S(2)}) collective-permute-start(bf16[360,128]{1,0:T(8,128)(2,1)S(1)} %get-tuple-element.32), channel_id=1, source_target_pairs={{0,3},{1,2},{2,1},{3,0},{4,7},{5,6},{6,5},{7,4},{8,11},{9,10},{10,... | collective-permute-start | bytes 276488 | tf_op jit(solution)/shard_map/ppermute | solution.py:21
  21.3 4.9 %collective-permute-start.10 = (bf16[96,128]{1,0:T(8,128)(2,1)S(1)}, bf16[96,128]{1,0:T(8,128)(2,1)S(1)}, u32[]{:S(2)}, u32[]{:S(2)}) collective-permute-start(bf16[96,128]{1,0:T(8,128)(2,1)S(1)} %get-tuple-element.33), channel_id=1, source_target_pairs={{0,1},{1,0},{2,3},{3,2},{4,5},{5,4},{6,7},{7,6},{8,9},{9,8},{10,11... | collective-permute-start | bytes 73736 | tf_op jit(solution)/shard_map/ppermute | solution.py:358
  22.0 5.0 %collective-permute-start.11 = (bf16[96,128]{1,0:T(8,128)(2,1)S(1)}, bf16[96,128]{1,0:T(8,128)(2,1)S(1)}, u32[]{:S(2)}, u32[]{:S(2)}) collective-permute-start(bf16[96,128]{1,0:T(8,128)(2,1)S(1)} %get-tuple-element.34), channel_id=1, source_target_pairs={{0,2},{1,0},{2,3},{3,1},{4,6},{5,4},{6,7},{7,5},{8,10},{9,8},{10,1... | collective-permute-start | bytes 73736 | tf_op jit(solution)/shard_map/ppermute | solution.py:358
  26.2 1.2 %collective-permute-start.12 = (bf16[96,128]{1,0:T(8,128)(2,1)S(1)}, bf16[96,128]{1,0:T(8,128)(2,1)S(1)}, u32[]{:S(2)}, u32[]{:S(2)}) collective-permute-start(bf16[96,128]{1,0:T(8,128)(2,1)S(1)} %get-tuple-element.35), channel_id=1, source_target_pairs={{0,4},{1,2},{2,1},{3,7},{4,0},{5,6},{6,5},{7,3},{8,12},{9,10},{10,... | collective-permute-start | bytes 73736 | tf_op jit(solution)/shard_map/ppermute | solution.py:358
  29.6 4.1 %collective-permute-start.13 = (bf16[240,128]{1,0:T(8,128)(2,1)S(1)}, bf16[240,128]{1,0:T(8,128)(2,1)S(1)}, u32[]{:S(2)}, u32[]{:S(2)}) collective-permute-start(bf16[240,128]{1,0:T(8,128)(2,1)S(1)} %get-tuple-element.40), channel_id=1, source_target_pairs={{0,4},{4,0},{8,12},{12,8},{16,20},{20,16},{24,28},{28,24},{1,5},{5... | collective-permute-start | bytes 184328 | tf_op jit(solution)/shard_map/ppermute | solution.py:21
  29.6 5.5 %collective-permute-start.14 = (bf16[240,128]{1,0:T(8,128)(2,1)S(1)}, bf16[240,128]{1,0:T(8,128)(2,1)S(1)}, u32[]{:S(2)}, u32[]{:S(2)}) collective-permute-start(bf16[240,128]{1,0:T(8,128)(2,1)S(1)} %get-tuple-element.41), channel_id=1, source_target_pairs={{0,1},{1,0},{2,3},{3,2},{4,8},{5,9},{6,10},{7,11},{8,4},{9,5},{10,... | collective-permute-start | bytes 184328 | tf_op jit(solution)/shard_map/ppermute | solution.py:381

commit v6 on v5

--- a/solution.py
+++ b/solution.py
@@ -36,6 +36,10 @@
     d = (t + pltpu.roll(t, lanes - gap, 1)) + pltpu.roll(t, lanes - 2 * gap, 1)
     lane = lax.broadcasted_iota(jnp.int32, t.shape, 1)
     return jnp.where(lane < gap, d, 0.0)
+
+
+def beside(k):
+    return k & (k + 1) == 0
 
 
 def tucked(tile):
@@ -130,7 +134,8 @@
         base = start + jnp.where(target == 0, halo, 0)
         part = wide[pl.ds(base, reach)].reshape(reach * by, members)
         outs[k - 1][0 : reach * by] = part.astype(jnp.bfloat16)
-        outs[k - 1][reach * by :] = packed
+        if beside(k):
+            outs[k - 1][reach * by :] = packed
         part = wide[pl.ds(start + reach, halo)].reshape(halo * by, members)
         rims[k - 1][...] = part.astype(jnp.bfloat16)
 
@@ -161,6 +166,8 @@
     before = jnp.zeros_like(mid)
     after = jnp.zeros_like(mid)
     for k in range(1, n_fault):
+        if not beside(k):
+            continue
         other = untucked(parts[k - 1][reach:], by, bx)
         source = fault ^ k
         before = before + jnp.where(source == fault - 1, other, 0.0)
@@ -319,7 +326,10 @@
     own, *chunks = pl.pallas_call(
         functools.partial(blocks_kernel, dims),
         out_shape=[jax.ShapeDtypeStruct((cells, members), f32)]
-        + [jax.ShapeDtypeStruct(((bx + STEPS) * by + SUB, members), bf16)] * (n_fault - 1)
+        + [
+            jax.ShapeDtypeStruct(((bx + STEPS) * by + SUB * beside(k), members), bf16)
+            for k in range(1, n_fault)
+        ]
         + [jax.ShapeDtypeStruct((STEPS * by, members), bf16)] * (n_fault - 1),
         in_specs=[scalar] * 2 + [vector] * (n_sea + 4),
         out_specs=[vector] * (2 * n_fault - 1),

time: 37.1 us -> 37.3 us (level)
  waiting for transfers between devices: 12.9 us -> 15.4 us
  starting transfers between devices: 16.5 us -> 14.1 us
    ppermute x1, starting transfers between devices: 3.27 us -> 1.75 us  [on_device(): far_edge = lax.ppermute(far_edge, ('sea', 'fault'), ring)]
    ppermute x3, waiting for transfers between devices: 1.93 us -> 3.21 us  [on_device(): got.append(lax.ppermute(chunks[last + k - 1], ('sea', 'fault'), hops))]
    ppermute x11, waiting for transfers between devices: 9.57 us -> 10.5 us  [swap(): return lax.ppermute(x, axis, [(i, i ^ k) for i in range(count)])]
    ppermute x3, starting transfers between devices: 4.18 us -> 3.49 us  [on_device(): got.append(lax.ppermute(chunks[last + k - 1], ('sea', 'fault'), hops))]
where the time goes in v6:
time: 37.3 us; the launch traced here: 37.1 us
  waiting for transfers between devices  15.4 us (41%)
  starting transfers between devices  14.1 us (38%)
  Pallas kernels  6.87 us (18%)
  between operations  0.7 us (2%)
    ppermute x11, waiting for transfers between devices, swap(): return lax.ppermute(x, axis, [(i, i ^ k) for i in range(count)])  10.5 us
    ppermute x11, starting transfers between devices, swap(): return lax.ppermute(x, axis, [(i, i ^ k) for i in range(count)])  8.83 us
    ppermute x3, starting transfers between devices, on_device(): got.append(lax.ppermute(chunks[last + k - 1], ('sea', 'fault'), hops))  3.49 us
    ppermute x3, waiting for transfers between devices, on_device(): got.append(lax.ppermute(chunks[last + k - 1], ('sea', 'fault'), hops))  3.21 us
    pallas_call x1, Pallas kernels, on_device(): pl.pallas_call(functools.partial(blocks_kernel, dims), out_shape=[jax.Sha...  2.04 us
    pallas_call x1, Pallas kernels, on_device(): pl.pallas_call(fetch_kernel, out_shape=[jax.ShapeDtypeStruct((SUB, LANES)...  1.87 us
    pallas_call x1, Pallas kernels, on_device(): pl.pallas_call(functools.partial(steps_kernel, (bx, wx, by)), out_shape=j...  1.83 us
    ppermute x1, starting transfers between devices, on_device(): far_edge = lax.ppermute(far_edge, ('sea', 'fault'), ring)  1.75 us
  transfers between devices with their start and end apart: 15, of which 8 were waited for; matrix products, arithmetic and copies ran while one was open for 0% of the time, Pallas kernels for 7%

profile of v6, /device:TPU:0, one launch (start us, length us, event | category | flops | bytes accessed | tf_op | source)
XLA Modules:
  0.0 37.1 jit_solution(7963976598302813451)
XLA Ops:
  0.6 3.0 %collective-permute-start.1 = (bf16[512,128]{1,0:T(8,128)(2,1)}, bf16[512,128]{1,0:T(8,128)(2,1)S(1)}, u32[]{:S(2)}, u32[]{:S(2)}) collective-permute-start(bf16[512,128]{1,0:T(8,128)(2,1)} %refs_9_.1), channel_id=1, source_target_pairs={{0,8},{4,12},{8,0},{12,4},{16,24},{20,28},{24,16},{28,20},{1,9},{5... | collective-permute-start | bytes 393224 | tf_op jit(solution)/shard_map/ppermute | solution.py:21
  3.7 1.5 %collective-permute-start.5 = (bf16[512,128]{1,0:T(8,128)(2,1)}, bf16[512,128]{1,0:T(8,128)(2,1)S(1)}, u32[]{:S(2)}, u32[]{:S(2)}) collective-permute-start(bf16[512,128]{1,0:T(8,128)(2,1)} %refs_9_.1), channel_id=1, source_target_pairs={{0,24},{4,28},{8,16},{12,20},{16,8},{20,12},{24,0},{28,4},{1,25},{... | collective-permute-start | bytes 393224 | tf_op jit(solution)/shard_map/ppermute | solution.py:21
  5.2 0.0 collective-permute-start.3
  5.2 0.0 collective-permute-start
  5.2 2.7 %collective-permute-done.1.refs_5_ = bf16[512,128]{1,0:T(8,128)(2,1)S(1)} collective-permute-done((bf16[512,128]{1,0:T(8,128)(2,1)}, bf16[512,128]{1,0:T(8,128)(2,1)S(1)}, u32[]{:S(2)}, u32[]{:S(2)}) %collective-permute-start.1) | collective-permute-done | bytes 131104 | tf_op jit(solution)/shard_map/ppermute | solution.py:21
  7.9 0.0 collective-permute-start.2
  7.9 3.6 %collective-permute-done.5.refs_9_ = bf16[512,128]{1,0:T(8,128)(2,1)S(1)} collective-permute-done((bf16[512,128]{1,0:T(8,128)(2,1)}, bf16[512,128]{1,0:T(8,128)(2,1)S(1)}, u32[]{:S(2)}, u32[]{:S(2)}) %collective-permute-start.5) | collective-permute-done | bytes 131104 | tf_op jit(solution)/shard_map/ppermute | solution.py:21
  11.5 0.0 collective-permute-start.6
  11.5 1.4 %collective-permute-done.3.refs_7_ = bf16[512,128]{1,0:T(8,128)(2,1)S(1)} collective-permute-done((bf16[512,128]{1,0:T(8,128)(2,1)}, bf16[512,128]{1,0:T(8,128)(2,1)S(1)}, u32[]{:S(2)}, u32[]{:S(2)}) %collective-permute-start.3) | collective-permute-done | bytes 131104 | tf_op jit(solution)/shard_map/ppermute | solution.py:21
  12.9 0.0 collective-permute-start.4
  12.9 1.9 %fetch.1 = (s32[8,128]{1,0:T(8,128)S(1)}, f32[8,128]{1,0:T(8,128)S(1)}, f32[16,128]{1,0:T(8,128)S(1)}, bf16[512,128]{1,0:T(8,128)(2,1)S(1)}, bf16[8,256,256]{2,1...) custom-call(s32[1,8]{1,0:T(1,128)} %bitcast.13, s32[1,8]{1,0:T(1,128)} %bitcast.14, ...), custom_call_target="tpu_custom_call" | custom-call | bytes 4718592 | tf_op jit(solution)/shard_map/fetch/pallas_call | solution.py:307
  14.7 0.0 collective-permute-done.refs_4_
  14.7 0.0 collective-permute-done.2.refs_6_
  14.8 0.0 collective-permute-done.6.refs_10_
  14.8 0.0 collective-permute-done.4.refs_8_
  14.8 2.0 %blocks.1 = (f32[448,128]{1,0:T(8,128)S(1)}, bf16[360,128]{1,0:T(8,128)(2,1)S(1)}, bf16[352,128]{1,0:T(8,128)(2,1)S(1)}, bf16[360,128]{1,0:T(8,128)(2,1)S(1)}, b...) custom-call(s32[8,128]{1,0:T(8,128)S(1)} %get-tuple-element.23.refs_0_, ...), custom_call_target="tpu_custom_call" | custom-call | tf_op jit(solution)/shard_map/blocks/pallas_call | solution.py:326
  16.8 1.6 %collective-permute-start.7 = (bf16[360,128]{1,0:T(8,128)(2,1)S(1)}, bf16[360,128]{1,0:T(8,128)(2,1)S(1)}, u32[]{:S(2)}, u32[]{:S(2)}) collective-permute-start(bf16[360,128]{1,0:T(8,128)(2,1)S(1)} %get-tuple-element.30), channel_id=1, source_target_pairs={{0,1},{1,0},{2,3},{3,2},{4,5},{5,4},{6,7},{7,6},{8,9},{9,8},{10,11... | collective-permute-start | bytes 276488 | tf_op jit(solution)/shard_map/ppermute | solution.py:21
  18.5 2.5 %collective-permute-start.9 = (bf16[360,128]{1,0:T(8,128)(2,1)S(1)}, bf16[360,128]{1,0:T(8,128)(2,1)S(1)}, u32[]{:S(2)}, u32[]{:S(2)}) collective-permute-start(bf16[360,128]{1,0:T(8,128)(2,1)S(1)} %get-tuple-element.32), channel_id=1, source_target_pairs={{0,3},{1,2},{2,1},{3,0},{4,7},{5,6},{6,5},{7,4},{8,11},{9,10},{10,... | collective-permute-start | bytes 276488 | tf_op jit(solution)/shard_map/ppermute | solution.py:21
  20.9 0.1 collective-permute-start.8
  21.1 1.8 %collective-permute-start.10 = (bf16[96,128]{1,0:T(8,128)(2,1)S(1)}, bf16[96,128]{1,0:T(8,128)(2,1)S(1)}, u32[]{:S(2)}, u32[]{:S(2)}) collective-permute-start(bf16[96,128]{1,0:T(8,128)(2,1)S(1)} %get-tuple-element.33), channel_id=1, source_target_pairs={{0,1},{1,0},{2,3},{3,2},{4,5},{5,4},{6,7},{7,6},{8,9},{9,8},{10,11... | collective-permute-start | bytes 73736 | tf_op jit(solution)/shard_map/ppermute | solution.py:368
  22.9 1.7 %collective-permute-start.11 = (bf16[96,128]{1,0:T(8,128)(2,1)S(1)}, bf16[96,128]{1,0:T(8,128)(2,1)S(1)}, u32[]{:S(2)}, u32[]{:S(2)}) collective-permute-start(bf16[96,128]{1,0:T(8,128)(2,1)S(1)} %get-tuple-element.34), channel_id=1, source_target_pairs={{0,2},{1,0},{2,3},{3,1},{4,6},{5,4},{6,7},{7,5},{8,10},{9,8},{10,1... | collective-permute-start | bytes 73736 | tf_op jit(solution)/shard_map/ppermute | solution.py:368
  24.6 2.0 %collective-permute-done.10.refs_5_ = bf16[96,128]{1,0:T(8,128)(2,1)S(1)} collective-permute-done((bf16[96,128]{1,0:T(8,128)(2,1)S(1)}, bf16[96,128]{1,0:T(8,128)(2,1)S(1)}, u32[]{:S(2)}, u32[]{:S(2)}) %collective-permute-start.10) | collective-permute-done | bytes 24608 | tf_op jit(solution)/shard_map/ppermute | solution.py:368
  26.6 0.0 collective-permute-start.12
  26.6 0.3 collective-permute-done.11.refs_6_
  26.9 0.9 %collective-permute-done.12.refs_7_ = bf16[96,128]{1,0:T(8,128)(2,1)S(1)} collective-permute-done((bf16[96,128]{1,0:T(8,128)(2,1)S(1)}, bf16[96,128]{1,0:T(8,128)(2,1)S(1)}, u32[]{:S(2)}, u32[]{:S(2)}) %collective-permute-start.12) | collective-permute-done | bytes 24608 | tf_op jit(solution)/shard_map/ppermute | solution.py:368
  27.8 2.9 %collective-permute-done.8.refs_3_ = bf16[352,128]{1,0:T(8,128)(2,1)S(1)} collective-permute-done((bf16[352,128]{1,0:T(8,128)(2,1)S(1)}, bf16[352,128]{1,0:T(8,128)(2,1)S(1)}, u32[]{:S(2)}, u32[]{:S(2)}) %collective-permute-start.8) | collective-permute-done | bytes 90144 | tf_op jit(solution)/shard_map/ppermute | solution.py:21
  30.6 0.0 collective-permute-done.7.refs_2_
  30.6 0.0 collective-permute-done.9.refs_4_
  30.7 0.3 sums.1
  31.0 0.0 collective-permute-start.13
  31.0 1.8 %collective-permute-start.14 = (bf16[240,128]{1,0:T(8,128)(2,1)S(1)}, bf16[240,128]{1,0:T(8,128)(2,1)S(1)}, u32[]{:S(2)}, u32[]{:S(2)}) collective-permute-start(bf16[240,128]{1,0:T(8,128)(2,1)S(1)} %get-tuple-element.41), channel_id=1, source_target_pairs={{0,1},{1,0},{2,3},{3,2},{4,8},{5,9},{6,10},{7,11},{8,4},{9,5},{10,... | collective-permute-start | bytes 184328 | tf_op jit(solution)/shard_map/ppermute | solution.py:391
  32.7 0.8 %uplift.1 = (f32[16,16,128]{2,1,0:T(8,128)}, f32[16,16,128]{2,1,0:T(8,128)S(1)}) custom-call(f32[448,128]{1,0:T(8,128)S(1)} %get-tuple-element.36.total, f32[16,128]{1,0:T(8,128)S(1)} %get-tuple-element.37.depth), custom_call_target="tpu_custom_call" | custom-call | bytes 917504 | tf_op jit(solution)/shard_map/uplift/pallas_call | solution.py:394
  33.5 0.0 collective-permute-done.13.near_edge
  33.5 1.7 %collective-permute-done.14.far_edge = bf16[240,128]{1,0:T(8,128)(2,1)S(1)} collective-permute-done((bf16[240,128]{1,0:T(8,128)(2,1)S(1)}, bf16[240,128]{1,0:T(8,128)(2,1)S(1)}, u32[]{:S(2)}, u32[]{:S(2)}) %collective-permute-start.14) | collective-permute-done | bytes 61472 | tf_op jit(solution)/shard_map/ppermute | solution.py:391
  35.3 1.8 %steps.1 = f32[16,16,128]{2,1,0:T(8,128)} custom-call(f32[448,128]{1,0:T(8,128)S(1)} %get-tuple-element.36.total, f32[16,128]{1,0:T(8,128)S(1)} %get-tuple-element.37.depth, f32[16,16,128]{2,1,0:T(8,128)S(1)} %get-tuple-element.39.wet, bf16[240,128]{1,0:T(8,128)(2,1)S(1)} %collective-permute-done.13.near_edge, ...), custom_call_target="tpu_custom_call" | custom-call | tf_op jit(solution)/shard_map/steps/pallas_call | solution.py:404
Async XLA Ops:
  0.6 7.2 %collective-permute-start.1 = (bf16[512,128]{1,0:T(8,128)(2,1)}, bf16[512,128]{1,0:T(8,128)(2,1)S(1)}, u32[]{:S(2)}, u32[]{:S(2)}) collective-permute-start(bf16[512,128]{1,0:T(8,128)(2,1)} %refs_9_.1), channel_id=1, source_target_pairs={{0,8},{4,12},{8,0},{12,4},{16,24},{20,28},{24,16},{28,20},{1,9},{5... | collective-permute-start | bytes 393224 | tf_op jit(solution)/shard_map/ppermute | solution.py:21
  3.7 7.8 %collective-permute-start.5 = (bf16[512,128]{1,0:T(8,128)(2,1)}, bf16[512,128]{1,0:T(8,128)(2,1)S(1)}, u32[]{:S(2)}, u32[]{:S(2)}) collective-permute-start(bf16[512,128]{1,0:T(8,128)(2,1)} %refs_9_.1), channel_id=1, source_target_pairs={{0,24},{4,28},{8,16},{12,20},{16,8},{20,12},{24,0},{28,4},{1,25},{... | collective-permute-start | bytes 393224 | tf_op jit(solution)/shard_map/ppermute | solution.py:21
  5.2 7.7 %collective-permute-start.3 = (bf16[512,128]{1,0:T(8,128)(2,1)}, bf16[512,128]{1,0:T(8,128)(2,1)S(1)}, u32[]{:S(2)}, u32[]{:S(2)}) collective-permute-start(bf16[512,128]{1,0:T(8,128)(2,1)} %refs_9_.1), channel_id=1, source_target_pairs={{0,16},{4,20},{8,24},{12,28},{16,0},{20,4},{24,8},{28,12},{1,17},{... | collective-permute-start | bytes 393224 | tf_op jit(solution)/shard_map/ppermute | solution.py:21
  5.2 9.5 %collective-permute-start = (bf16[512,128]{1,0:T(8,128)(2,1)}, bf16[512,128]{1,0:T(8,128)(2,1)S(1)}, u32[]{:S(2)}, u32[]{:S(2)}) collective-permute-start(bf16[512,128]{1,0:T(8,128)(2,1)} %refs_9_.1), channel_id=1, source_target_pairs={{0,4},{4,0},{8,12},{12,8},{16,20},{20,16},{24,28},{28,24},{1,5},{5... | collective-permute-start | bytes 393224 | tf_op jit(solution)/shard_map/ppermute | solution.py:21
  7.9 6.9 %collective-permute-start.2 = (bf16[512,128]{1,0:T(8,128)(2,1)S(1)}, bf16[512,128]{1,0:T(8,128)(2,1)S(1)}, u32[]{:S(2)}, u32[]{:S(2)}) collective-permute-start(bf16[512,128]{1,0:T(8,128)(2,1)S(1)} %collective-permute-done.1.refs_5_), channel_id=1, source_target_pairs={{0,4},{4,0},{8,12},{12,8},{16,20},{20,16},{24,28},{28,24},{1,5},{5... | collective-permute-start | bytes 393224 | tf_op jit(solution)/shard_map/ppermute | solution.py:21
  11.5 3.3 %collective-permute-start.6 = (bf16[512,128]{1,0:T(8,128)(2,1)S(1)}, bf16[512,128]{1,0:T(8,128)(2,1)S(1)}, u32[]{:S(2)}, u32[]{:S(2)}) collective-permute-start(bf16[512,128]{1,0:T(8,128)(2,1)S(1)} %collective-permute-done.5.refs_9_), channel_id=1, source_target_pairs={{0,4},{4,0},{8,12},{12,8},{16,20},{20,16},{24,28},{28,24},{1,5},{5... | collective-permute-start | bytes 393224 | tf_op jit(solution)/shard_map/ppermute | solution.py:21
  12.9 1.9 %collective-permute-start.4 = (bf16[512,128]{1,0:T(8,128)(2,1)S(1)}, bf16[512,128]{1,0:T(8,128)(2,1)S(1)}, u32[]{:S(2)}, u32[]{:S(2)}) collective-permute-start(bf16[512,128]{1,0:T(8,128)(2,1)S(1)} %collective-permute-done.3.refs_7_), channel_id=1, source_target_pairs={{0,4},{4,0},{8,12},{12,8},{16,20},{20,16},{24,28},{28,24},{1,5},{5... | collective-permute-start | bytes 393224 | tf_op jit(solution)/shard_map/ppermute | solution.py:21
  16.8 13.8 %collective-permute-start.7 = (bf16[360,128]{1,0:T(8,128)(2,1)S(1)}, bf16[360,128]{1,0:T(8,128)(2,1)S(1)}, u32[]{:S(2)}, u32[]{:S(2)}) collective-permute-start(bf16[360,128]{1,0:T(8,128)(2,1)S(1)} %get-tuple-element.30), channel_id=1, source_target_pairs={{0,1},{1,0},{2,3},{3,2},{4,5},{5,4},{6,7},{7,6},{8,9},{9,8},{10,11... | collective-permute-start | bytes 276488 | tf_op jit(solution)/shard_map/ppermute | solution.py:21
  18.5 12.2 %collective-permute-start.9 = (bf16[360,128]{1,0:T(8,128)(2,1)S(1)}, bf16[360,128]{1,0:T(8,128)(2,1)S(1)}, u32[]{:S(2)}, u32[]{:S(2)}) collective-permute-start(bf16[360,128]{1,0:T(8,128)(2,1)S(1)} %get-tuple-element.32), channel_id=1, source_target_pairs={{0,3},{1,2},{2,1},{3,0},{4,7},{5,6},{6,5},{7,4},{8,11},{9,10},{10,... | collective-permute-start | bytes 276488 | tf_op jit(solution)/shard_map/ppermute | solution.py:21
  20.9 9.7 %collective-permute-start.8 = (bf16[352,128]{1,0:T(8,128)(2,1)S(1)}, bf16[352,128]{1,0:T(8,128)(2,1)S(1)}, u32[]{:S(2)}, u32[]{:S(2)}) collective-permute-start(bf16[352,128]{1,0:T(8,128)(2,1)S(1)} %get-tuple-element.31), channel_id=1, source_target_pairs={{0,2},{1,3},{2,0},{3,1},{4,6},{5,7},{6,4},{7,5},{8,10},{9,11},{10,... | collective-permute-start | bytes 270344 | tf_op jit(solution)/shard_map/ppermute | solution.py:21
  21.1 5.5 %collective-permute-start.10 = (bf16[96,128]{1,0:T(8,128)(2,1)S(1)}, bf16[96,128]{1,0:T(8,128)(2,1)S(1)}, u32[]{:S(2)}, u32[]{:S(2)}) collective-permute-start(bf16[96,128]{1,0:T(8,128)(2,1)S(1)} %get-tuple-element.33), channel_id=1, source_target_pairs={{0,1},{1,0},{2,3},{3,2},{4,5},{5,4},{6,7},{7,6},{8,9},{9,8},{10,11... | collective-permute-start | bytes 73736 | tf_op jit(solution)/shard_map/ppermute | solution.py:368
  22.9 4.0 %collective-permute-start.11 = (bf16[96,128]{1,0:T(8,128)(2,1)S(1)}, bf16[96,128]{1,0:T(8,128)(2,1)S(1)}, u32[]{:S(2)}, u32[]{:S(2)}) collective-permute-start(bf16[96,128]{1,0:T(8,128)(2,1)S(1)} %get-tuple-element.34), channel_id=1, source_target_pairs={{0,2},{1,0},{2,3},{3,1},{4,6},{5,4},{6,7},{7,5},{8,10},{9,8},{10,1... | collective-permute-start | bytes 73736 | tf_op jit(solution)/shard_map/ppermute | solution.py:368
  26.6 1.2 %collective-permute-start.12 = (bf16[96,128]{1,0:T(8,128)(2,1)S(1)}, bf16[96,128]{1,0:T(8,128)(2,1)S(1)}, u32[]{:S(2)}, u32[]{:S(2)}) collective-permute-start(bf16[96,128]{1,0:T(8,128)(2,1)S(1)} %get-tuple-element.35), channel_id=1, source_target_pairs={{0,4},{1,2},{2,1},{3,7},{4,0},{5,6},{6,5},{7,3},{8,12},{9,10},{10,... | collective-permute-start | bytes 73736 | tf_op jit(solution)/shard_map/ppermute | solution.py:368
  31.0 2.6 %collective-permute-start.13 = (bf16[240,128]{1,0:T(8,128)(2,1)S(1)}, bf16[240,128]{1,0:T(8,128)(2,1)S(1)}, u32[]{:S(2)}, u32[]{:S(2)}) collective-permute-start(bf16[240,128]{1,0:T(8,128)(2,1)S(1)} %get-tuple-element.40), channel_id=1, source_target_pairs={{0,4},{4,0},{8,12},{12,8},{16,20},{20,16},{24,28},{28,24},{1,5},{5... | collective-permute-start | bytes 184328 | tf_op jit(solution)/shard_map/ppermute | solution.py:21
  31.0 4.3 %collective-permute-start.14 = (bf16[240,128]{1,0:T(8,128)(2,1)S(1)}, bf16[240,128]{1,0:T(8,128)(2,1)S(1)}, u32[]{:S(2)}, u32[]{:S(2)}) collective-permute-start(bf16[240,128]{1,0:T(8,128)(2,1)S(1)} %get-tuple-element.41), channel_id=1, source_target_pairs={{0,1},{1,0},{2,3},{3,2},{4,8},{5,9},{6,10},{7,11},{8,4},{9,5},{10,... | collective-permute-start | bytes 184328 | tf_op jit(solution)/shard_map/ppermute | solution.py:391

commit v7 on v6

--- a/solution.py
+++ b/solution.py
@@ -218,13 +218,17 @@
     post_d = jnp.where(sea == lax.axis_size("sea") - 1, 0.0, post_d)
     d = jnp.concatenate([prev_d, depth[...], post_d], axis=0)
     scale = gravity_step * height_step
-    rows[0] = scale * jnp.minimum(d, pltpu.roll(d, lanes - 1, 1))
-    rows[1] = scale * jnp.minimum(d, pltpu.roll(d, span - 1, 0))
-    folded = [[rows[k, pl.ds(v, SUB, stride=folds), :] for v in range(folds)] for k in range(2)]
-
-    def spread(part, x):
-        return [jnp.broadcast_to(f[:, x : x + 1], (SUB, lanes)) for f in part]
-
+    rows[...] = scale * d
+    folded = [rows[pl.ds(v, SUB, stride=folds), :] for v in range(folds)]
+
+    cell = [
+        [jnp.broadcast_to(f[:, x : x + 1], (SUB, lanes)) for f in folded] for x in range(wx)
+    ]
+    de = [[jnp.minimum(a, b) for a, b in zip(cell[x], cell[x + 1])] for x in range(wx - 1)]
+    dn = [
+        [jnp.minimum(a, b) for a, b in zip(c, c[1:] + [pltpu.roll(c[0], SUB - 1, 0)])]
+        for c in cell
+    ]
     h = []
     for x in range(wx):
         base = x * span
@@ -232,8 +236,6 @@
         column[base + SUB : base + SUB + by] = total[x * by : (x + 1) * by]
         column[base + SUB + by : base + span] = post[x * SUB : (x + 1) * SUB]
         h.append([column[pl.ds(base + v, SUB, stride=folds), :] for v in range(folds)])
-    de = [spread(folded[0], x) for x in range(wx)]
-    dn = [spread(folded[1], x) for x in range(wx)]
     e = [None] * wx
     n = [None] * wx
     for step in range(STEPS):
@@ -406,7 +408,7 @@
         out_shape=jax.ShapeDtypeStruct((by, bx, members), f32),
         in_specs=[vector] * 5,
         out_specs=vector,
-        scratch_shapes=[pltpu.VMEM((wx * span, members), f32), pltpu.VMEM((2, span, LANES), f32)],
+        scratch_shapes=[pltpu.VMEM((wx * span, members), f32), pltpu.VMEM((span, LANES), f32)],
         compiler_params=pltpu.CompilerParams(vmem_limit_bytes=8 << 20),
         name="steps",
     )(total, depth, wet, near_edge, far_edge)

time: 37.3 us -> 37.1 us (level)
  no operation moved by 1% of the time
where the time goes in v7:
time: 37.1 us; the launch traced here: 36.9 us
  waiting for transfers between devices  15.4 us (42%)
  starting transfers between devices  14.1 us (38%)
  Pallas kernels  6.72 us (18%)
  between operations  0.7 us (2%)
    ppermute x11, waiting for transfers between devices, swap(): return lax.ppermute(x, axis, [(i, i ^ k) for i in range(count)])  10.5 us
    ppermute x11, starting transfers between devices, swap(): return lax.ppermute(x, axis, [(i, i ^ k) for i in range(count)])  8.83 us
    ppermute x3, starting transfers between devices, on_device(): got.append(lax.ppermute(chunks[last + k - 1], ('sea', 'fault'), hops))  3.49 us
    ppermute x3, waiting for transfers between devices, on_device(): got.append(lax.ppermute(chunks[last + k - 1], ('sea', 'fault'), hops))  3.21 us
    pallas_call x1, Pallas kernels, on_device(): pl.pallas_call(functools.partial(blocks_kernel, dims), out_shape=[jax.Sha...  2.04 us
    pallas_call x1, Pallas kernels, on_device(): pl.pallas_call(fetch_kernel, out_shape=[jax.ShapeDtypeStruct((SUB, LANES)...  1.87 us
    ppermute x1, starting transfers between devices, on_device(): far_edge = lax.ppermute(far_edge, ('sea', 'fault'), ring)  1.75 us
    ppermute x1, waiting for transfers between devices, on_device(): far_edge = lax.ppermute(far_edge, ('sea', 'fault'), ring)  1.71 us
  transfers between devices with their start and end apart: 15, of which 8 were waited for; matrix products, arithmetic and copies ran while one was open for 0% of the time, Pallas kernels for 7%

profile of v7, /device:TPU:0, one launch (start us, length us, event | category | flops | bytes accessed | tf_op | source)
XLA Modules:
  0.0 36.9 jit_solution(16538727031072619259)
XLA Ops:
  0.6 3.0 %collective-permute-start.1 = (bf16[512,128]{1,0:T(8,128)(2,1)}, bf16[512,128]{1,0:T(8,128)(2,1)S(1)}, u32[]{:S(2)}, u32[]{:S(2)}) collective-permute-start(bf16[512,128]{1,0:T(8,128)(2,1)} %refs_9_.1), channel_id=1, source_target_pairs={{0,8},{4,12},{8,0},{12,4},{16,24},{20,28},{24,16},{28,20},{1,9},{5... | collective-permute-start | bytes 393224 | tf_op jit(solution)/shard_map/ppermute | solution.py:21
  3.7 1.5 %collective-permute-start.5 = (bf16[512,128]{1,0:T(8,128)(2,1)}, bf16[512,128]{1,0:T(8,128)(2,1)S(1)}, u32[]{:S(2)}, u32[]{:S(2)}) collective-permute-start(bf16[512,128]{1,0:T(8,128)(2,1)} %refs_9_.1), channel_id=1, source_target_pairs={{0,24},{4,28},{8,16},{12,20},{16,8},{20,12},{24,0},{28,4},{1,25},{... | collective-permute-start | bytes 393224 | tf_op jit(solution)/shard_map/ppermute | solution.py:21
  5.2 0.0 collective-permute-start.3
  5.2 0.0 collective-permute-start
  5.2 2.7 %collective-permute-done.1.refs_5_ = bf16[512,128]{1,0:T(8,128)(2,1)S(1)} collective-permute-done((bf16[512,128]{1,0:T(8,128)(2,1)}, bf16[512,128]{1,0:T(8,128)(2,1)S(1)}, u32[]{:S(2)}, u32[]{:S(2)}) %collective-permute-start.1) | collective-permute-done | bytes 131104 | tf_op jit(solution)/shard_map/ppermute | solution.py:21
  7.9 0.0 collective-permute-start.2
  7.9 3.6 %collective-permute-done.5.refs_9_ = bf16[512,128]{1,0:T(8,128)(2,1)S(1)} collective-permute-done((bf16[512,128]{1,0:T(8,128)(2,1)}, bf16[512,128]{1,0:T(8,128)(2,1)S(1)}, u32[]{:S(2)}, u32[]{:S(2)}) %collective-permute-start.5) | collective-permute-done | bytes 131104 | tf_op jit(solution)/shard_map/ppermute | solution.py:21
  11.5 0.0 collective-permute-start.6
  11.5 1.4 %collective-permute-done.3.refs_7_ = bf16[512,128]{1,0:T(8,128)(2,1)S(1)} collective-permute-done((bf16[512,128]{1,0:T(8,128)(2,1)}, bf16[512,128]{1,0:T(8,128)(2,1)S(1)}, u32[]{:S(2)}, u32[]{:S(2)}) %collective-permute-start.3) | collective-permute-done | bytes 131104 | tf_op jit(solution)/shard_map/ppermute | solution.py:21
  12.9 0.0 collective-permute-start.4
  12.9 1.9 %fetch.1 = (s32[8,128]{1,0:T(8,128)S(1)}, f32[8,128]{1,0:T(8,128)S(1)}, f32[16,128]{1,0:T(8,128)S(1)}, bf16[512,128]{1,0:T(8,128)(2,1)S(1)}, bf16[8,256,256]{2,1...) custom-call(s32[1,8]{1,0:T(1,128)} %bitcast.13, s32[1,8]{1,0:T(1,128)} %bitcast.14, ...), custom_call_target="tpu_custom_call" | custom-call | bytes 4718592 | tf_op jit(solution)/shard_map/fetch/pallas_call | solution.py:309
  14.7 0.0 collective-permute-done.refs_4_
  14.7 0.0 collective-permute-done.2.refs_6_
  14.8 0.0 collective-permute-done.6.refs_10_
  14.8 0.0 collective-permute-done.4.refs_8_
  14.8 2.0 %blocks.1 = (f32[448,128]{1,0:T(8,128)S(1)}, bf16[360,128]{1,0:T(8,128)(2,1)S(1)}, bf16[352,128]{1,0:T(8,128)(2,1)S(1)}, bf16[360,128]{1,0:T(8,128)(2,1)S(1)}, b...) custom-call(s32[8,128]{1,0:T(8,128)S(1)} %get-tuple-element.23.refs_0_, ...), custom_call_target="tpu_custom_call" | custom-call | tf_op jit(solution)/shard_map/blocks/pallas_call | solution.py:328
  16.8 1.6 %collective-permute-start.7 = (bf16[360,128]{1,0:T(8,128)(2,1)S(1)}, bf16[360,128]{1,0:T(8,128)(2,1)S(1)}, u32[]{:S(2)}, u32[]{:S(2)}) collective-permute-start(bf16[360,128]{1,0:T(8,128)(2,1)S(1)} %get-tuple-element.30), channel_id=1, source_target_pairs={{0,1},{1,0},{2,3},{3,2},{4,5},{5,4},{6,7},{7,6},{8,9},{9,8},{10,11... | collective-permute-start | bytes 276488 | tf_op jit(solution)/shard_map/ppermute | solution.py:21
  18.5 2.5 %collective-permute-start.9 = (bf16[360,128]{1,0:T(8,128)(2,1)S(1)}, bf16[360,128]{1,0:T(8,128)(2,1)S(1)}, u32[]{:S(2)}, u32[]{:S(2)}) collective-permute-start(bf16[360,128]{1,0:T(8,128)(2,1)S(1)} %get-tuple-element.32), channel_id=1, source_target_pairs={{0,3},{1,2},{2,1},{3,0},{4,7},{5,6},{6,5},{7,4},{8,11},{9,10},{10,... | collective-permute-start | bytes 276488 | tf_op jit(solution)/shard_map/ppermute | solution.py:21
  20.9 0.1 collective-permute-start.8
  21.1 1.8 %collective-permute-start.10 = (bf16[96,128]{1,0:T(8,128)(2,1)S(1)}, bf16[96,128]{1,0:T(8,128)(2,1)S(1)}, u32[]{:S(2)}, u32[]{:S(2)}) collective-permute-start(bf16[96,128]{1,0:T(8,128)(2,1)S(1)} %get-tuple-element.33), channel_id=1, source_target_pairs={{0,1},{1,0},{2,3},{3,2},{4,5},{5,4},{6,7},{7,6},{8,9},{9,8},{10,11... | collective-permute-start | bytes 73736 | tf_op jit(solution)/shard_map/ppermute | solution.py:370
  22.9 1.7 %collective-permute-start.11 = (bf16[96,128]{1,0:T(8,128)(2,1)S(1)}, bf16[96,128]{1,0:T(8,128)(2,1)S(1)}, u32[]{:S(2)}, u32[]{:S(2)}) collective-permute-start(bf16[96,128]{1,0:T(8,128)(2,1)S(1)} %get-tuple-element.34), channel_id=1, source_target_pairs={{0,2},{1,0},{2,3},{3,1},{4,6},{5,4},{6,7},{7,5},{8,10},{9,8},{10,1... | collective-permute-start | bytes 73736 | tf_op jit(solution)/shard_map/ppermute | solution.py:370
  24.6 2.0 %collective-permute-done.10.refs_5_ = bf16[96,128]{1,0:T(8,128)(2,1)S(1)} collective-permute-done((bf16[96,128]{1,0:T(8,128)(2,1)S(1)}, bf16[96,128]{1,0:T(8,128)(2,1)S(1)}, u32[]{:S(2)}, u32[]{:S(2)}) %collective-permute-start.10) | collective-permute-done | bytes 24608 | tf_op jit(solution)/shard_map/ppermute | solution.py:370
  26.6 0.0 collective-permute-start.12
  26.6 0.3 collective-permute-done.11.refs_6_
  26.9 0.9 %collective-permute-done.12.refs_7_ = bf16[96,128]{1,0:T(8,128)(2,1)S(1)} collective-permute-done((bf16[96,128]{1,0:T(8,128)(2,1)S(1)}, bf16[96,128]{1,0:T(8,128)(2,1)S(1)}, u32[]{:S(2)}, u32[]{:S(2)}) %collective-permute-start.12) | collective-permute-done | bytes 24608 | tf_op jit(solution)/shard_map/ppermute | solution.py:370
  27.8 2.9 %collective-permute-done.8.refs_3_ = bf16[352,128]{1,0:T(8,128)(2,1)S(1)} collective-permute-done((bf16[352,128]{1,0:T(8,128)(2,1)S(1)}, bf16[352,128]{1,0:T(8,128)(2,1)S(1)}, u32[]{:S(2)}, u32[]{:S(2)}) %collective-permute-start.8) | collective-permute-done | bytes 90144 | tf_op jit(solution)/shard_map/ppermute | solution.py:21
  30.6 0.0 collective-permute-done.7.refs_2_
  30.6 0.0 collective-permute-done.9.refs_4_
  30.7 0.3 sums.1
  31.0 0.0 collective-permute-start.13
  31.0 1.8 %collective-permute-start.14 = (bf16[240,128]{1,0:T(8,128)(2,1)S(1)}, bf16[240,128]{1,0:T(8,128)(2,1)S(1)}, u32[]{:S(2)}, u32[]{:S(2)}) collective-permute-start(bf16[240,128]{1,0:T(8,128)(2,1)S(1)} %get-tuple-element.41), channel_id=1, source_target_pairs={{0,1},{1,0},{2,3},{3,2},{4,8},{5,9},{6,10},{7,11},{8,4},{9,5},{10,... | collective-permute-start | bytes 184328 | tf_op jit(solution)/shard_map/ppermute | solution.py:393
  32.7 0.8 %uplift.1 = (f32[16,16,128]{2,1,0:T(8,128)}, f32[16,16,128]{2,1,0:T(8,128)S(1)}) custom-call(f32[448,128]{1,0:T(8,128)S(1)} %get-tuple-element.36.total, f32[16,128]{1,0:T(8,128)S(1)} %get-tuple-element.37.depth), custom_call_target="tpu_custom_call" | custom-call | bytes 917504 | tf_op jit(solution)/shard_map/uplift/pallas_call | solution.py:396
  33.5 0.0 collective-permute-done.13.near_edge
  33.5 1.7 %collective-permute-done.14.far_edge = bf16[240,128]{1,0:T(8,128)(2,1)S(1)} collective-permute-done((bf16[240,128]{1,0:T(8,128)(2,1)S(1)}, bf16[240,128]{1,0:T(8,128)(2,1)S(1)}, u32[]{:S(2)}, u32[]{:S(2)}) %collective-permute-start.14) | collective-permute-done | bytes 61472 | tf_op jit(solution)/shard_map/ppermute | solution.py:393
  35.3 1.7 %steps.1 = f32[16,16,128]{2,1,0:T(8,128)} custom-call(f32[448,128]{1,0:T(8,128)S(1)} %get-tuple-element.36.total, f32[16,128]{1,0:T(8,128)S(1)} %get-tuple-element.37.depth, f32[16,16,128]{2,1,0:T(8,128)S(1)} %get-tuple-element.39.wet, bf16[240,128]{1,0:T(8,128)(2,1)S(1)} %collective-permute-done.13.near_edge, ...), custom_call_target="tpu_custom_call" | custom-call | tf_op jit(solution)/shard_map/steps/pallas_call | solution.py:406
Async XLA Ops:
  0.6 7.2 %collective-permute-start.1 = (bf16[512,128]{1,0:T(8,128)(2,1)}, bf16[512,128]{1,0:T(8,128)(2,1)S(1)}, u32[]{:S(2)}, u32[]{:S(2)}) collective-permute-start(bf16[512,128]{1,0:T(8,128)(2,1)} %refs_9_.1), channel_id=1, source_target_pairs={{0,8},{4,12},{8,0},{12,4},{16,24},{20,28},{24,16},{28,20},{1,9},{5... | collective-permute-start | bytes 393224 | tf_op jit(solution)/shard_map/ppermute | solution.py:21
  3.7 7.8 %collective-permute-start.5 = (bf16[512,128]{1,0:T(8,128)(2,1)}, bf16[512,128]{1,0:T(8,128)(2,1)S(1)}, u32[]{:S(2)}, u32[]{:S(2)}) collective-permute-start(bf16[512,128]{1,0:T(8,128)(2,1)} %refs_9_.1), channel_id=1, source_target_pairs={{0,24},{4,28},{8,16},{12,20},{16,8},{20,12},{24,0},{28,4},{1,25},{... | collective-permute-start | bytes 393224 | tf_op jit(solution)/shard_map/ppermute | solution.py:21
  5.2 7.7 %collective-permute-start.3 = (bf16[512,128]{1,0:T(8,128)(2,1)}, bf16[512,128]{1,0:T(8,128)(2,1)S(1)}, u32[]{:S(2)}, u32[]{:S(2)}) collective-permute-start(bf16[512,128]{1,0:T(8,128)(2,1)} %refs_9_.1), channel_id=1, source_target_pairs={{0,16},{4,20},{8,24},{12,28},{16,0},{20,4},{24,8},{28,12},{1,17},{... | collective-permute-start | bytes 393224 | tf_op jit(solution)/shard_map/ppermute | solution.py:21
  5.2 9.5 %collective-permute-start = (bf16[512,128]{1,0:T(8,128)(2,1)}, bf16[512,128]{1,0:T(8,128)(2,1)S(1)}, u32[]{:S(2)}, u32[]{:S(2)}) collective-permute-start(bf16[512,128]{1,0:T(8,128)(2,1)} %refs_9_.1), channel_id=1, source_target_pairs={{0,4},{4,0},{8,12},{12,8},{16,20},{20,16},{24,28},{28,24},{1,5},{5... | collective-permute-start | bytes 393224 | tf_op jit(solution)/shard_map/ppermute | solution.py:21
  7.9 6.9 %collective-permute-start.2 = (bf16[512,128]{1,0:T(8,128)(2,1)S(1)}, bf16[512,128]{1,0:T(8,128)(2,1)S(1)}, u32[]{:S(2)}, u32[]{:S(2)}) collective-permute-start(bf16[512,128]{1,0:T(8,128)(2,1)S(1)} %collective-permute-done.1.refs_5_), channel_id=1, source_target_pairs={{0,4},{4,0},{8,12},{12,8},{16,20},{20,16},{24,28},{28,24},{1,5},{5... | collective-permute-start | bytes 393224 | tf_op jit(solution)/shard_map/ppermute | solution.py:21
  11.5 3.3 %collective-permute-start.6 = (bf16[512,128]{1,0:T(8,128)(2,1)S(1)}, bf16[512,128]{1,0:T(8,128)(2,1)S(1)}, u32[]{:S(2)}, u32[]{:S(2)}) collective-permute-start(bf16[512,128]{1,0:T(8,128)(2,1)S(1)} %collective-permute-done.5.refs_9_), channel_id=1, source_target_pairs={{0,4},{4,0},{8,12},{12,8},{16,20},{20,16},{24,28},{28,24},{1,5},{5... | collective-permute-start | bytes 393224 | tf_op jit(solution)/shard_map/ppermute | solution.py:21
  12.9 1.9 %collective-permute-start.4 = (bf16[512,128]{1,0:T(8,128)(2,1)S(1)}, bf16[512,128]{1,0:T(8,128)(2,1)S(1)}, u32[]{:S(2)}, u32[]{:S(2)}) collective-permute-start(bf16[512,128]{1,0:T(8,128)(2,1)S(1)} %collective-permute-done.3.refs_7_), channel_id=1, source_target_pairs={{0,4},{4,0},{8,12},{12,8},{16,20},{20,16},{24,28},{28,24},{1,5},{5... | collective-permute-start | bytes 393224 | tf_op jit(solution)/shard_map/ppermute | solution.py:21
  16.8 13.8 %collective-permute-start.7 = (bf16[360,128]{1,0:T(8,128)(2,1)S(1)}, bf16[360,128]{1,0:T(8,128)(2,1)S(1)}, u32[]{:S(2)}, u32[]{:S(2)}) collective-permute-start(bf16[360,128]{1,0:T(8,128)(2,1)S(1)} %get-tuple-element.30), channel_id=1, source_target_pairs={{0,1},{1,0},{2,3},{3,2},{4,5},{5,4},{6,7},{7,6},{8,9},{9,8},{10,11... | collective-permute-start | bytes 276488 | tf_op jit(solution)/shard_map/ppermute | solution.py:21
  18.5 12.2 %collective-permute-start.9 = (bf16[360,128]{1,0:T(8,128)(2,1)S(1)}, bf16[360,128]{1,0:T(8,128)(2,1)S(1)}, u32[]{:S(2)}, u32[]{:S(2)}) collective-permute-start(bf16[360,128]{1,0:T(8,128)(2,1)S(1)} %get-tuple-element.32), channel_id=1, source_target_pairs={{0,3},{1,2},{2,1},{3,0},{4,7},{5,6},{6,5},{7,4},{8,11},{9,10},{10,... | collective-permute-start | bytes 276488 | tf_op jit(solution)/shard_map/ppermute | solution.py:21
  20.9 9.7 %collective-permute-start.8 = (bf16[352,128]{1,0:T(8,128)(2,1)S(1)}, bf16[352,128]{1,0:T(8,128)(2,1)S(1)}, u32[]{:S(2)}, u32[]{:S(2)}) collective-permute-start(bf16[352,128]{1,0:T(8,128)(2,1)S(1)} %get-tuple-element.31), channel_id=1, source_target_pairs={{0,2},{1,3},{2,0},{3,1},{4,6},{5,7},{6,4},{7,5},{8,10},{9,11},{10,... | collective-permute-start | bytes 270344 | tf_op jit(solution)/shard_map/ppermute | solution.py:21
  21.1 5.5 %collective-permute-start.10 = (bf16[96,128]{1,0:T(8,128)(2,1)S(1)}, bf16[96,128]{1,0:T(8,128)(2,1)S(1)}, u32[]{:S(2)}, u32[]{:S(2)}) collective-permute-start(bf16[96,128]{1,0:T(8,128)(2,1)S(1)} %get-tuple-element.33), channel_id=1, source_target_pairs={{0,1},{1,0},{2,3},{3,2},{4,5},{5,4},{6,7},{7,6},{8,9},{9,8},{10,11... | collective-permute-start | bytes 73736 | tf_op jit(solution)/shard_map/ppermute | solution.py:370
  22.9 4.0 %collective-permute-start.11 = (bf16[96,128]{1,0:T(8,128)(2,1)S(1)}, bf16[96,128]{1,0:T(8,128)(2,1)S(1)}, u32[]{:S(2)}, u32[]{:S(2)}) collective-permute-start(bf16[96,128]{1,0:T(8,128)(2,1)S(1)} %get-tuple-element.34), channel_id=1, source_target_pairs={{0,2},{1,0},{2,3},{3,1},{4,6},{5,4},{6,7},{7,5},{8,10},{9,8},{10,1... | collective-permute-start | bytes 73736 | tf_op jit(solution)/shard_map/ppermute | solution.py:370
  26.6 1.2 %collective-permute-start.12 = (bf16[96,128]{1,0:T(8,128)(2,1)S(1)}, bf16[96,128]{1,0:T(8,128)(2,1)S(1)}, u32[]{:S(2)}, u32[]{:S(2)}) collective-permute-start(bf16[96,128]{1,0:T(8,128)(2,1)S(1)} %get-tuple-element.35), channel_id=1, source_target_pairs={{0,4},{1,2},{2,1},{3,7},{4,0},{5,6},{6,5},{7,3},{8,12},{9,10},{10,... | collective-permute-start | bytes 73736 | tf_op jit(solution)/shard_map/ppermute | solution.py:370
  31.0 2.6 %collective-permute-start.13 = (bf16[240,128]{1,0:T(8,128)(2,1)S(1)}, bf16[240,128]{1,0:T(8,128)(2,1)S(1)}, u32[]{:S(2)}, u32[]{:S(2)}) collective-permute-start(bf16[240,128]{1,0:T(8,128)(2,1)S(1)} %get-tuple-element.40), channel_id=1, source_target_pairs={{0,4},{4,0},{8,12},{12,8},{16,20},{20,16},{24,28},{28,24},{1,5},{5... | collective-permute-start | bytes 184328 | tf_op jit(solution)/shard_map/ppermute | solution.py:21
  31.0 4.3 %collective-permute-start.14 = (bf16[240,128]{1,0:T(8,128)(2,1)S(1)}, bf16[240,128]{1,0:T(8,128)(2,1)S(1)}, u32[]{:S(2)}, u32[]{:S(2)}) collective-permute-start(bf16[240,128]{1,0:T(8,128)(2,1)S(1)} %get-tuple-element.41), channel_id=1, source_target_pairs={{0,1},{1,0},{2,3},{3,2},{4,8},{5,9},{6,10},{7,11},{8,4},{9,5},{10,... | collective-permute-start | bytes 184328 | tf_op jit(solution)/shard_map/ppermute | solution.py:393
